TPU v7x, 32 devices: a whole 2x2x4 slice. The times are simulated.
32 devices in a mesh: wide: 8 (over z, core), narrow: 4 (over y, x).
Axes of the slice: x: 2, y: 2, z: 4, core: 2. Of those that a mesh axis runs over, the one named last changes fastest.
Arguments:
- homolog_embedding: float32 [32, 1024, 256], P('wide', 'narrow'), may hold values from -6 to 6
- pair_state: float32 [1024, 1024, 128], P('wide', 'narrow'), may hold values from -6 to 6
- probe_projector: float32 [256, 256], replicated, may hold values from -0.375 to 0.375
- lookup_projector: float32 [256, 256], replicated, may hold values from -0.375 to 0.375
- content_projector: float32 [256, 256], replicated, may hold values from -0.375 to 0.375
- sigmoid_projector: float32 [256, 256], replicated, may hold values from -0.375 to 0.375
- sigmoid_offset: float32 [256], replicated, may hold values from -4 to 4
- pair_bias_weight: float32 [128, 8], replicated, may hold values from -4 to 4
- mixing_projector: float32 [256, 256], replicated, may hold values from -0.375 to 0.375
- mixing_offset: float32 [256], replicated, may hold values from -3 to 3
- first_factor_projector: float32 [256, 32], replicated, may hold values from -0.375 to 0.375
- second_factor_projector: float32 [256, 32], replicated, may hold values from -0.375 to 0.375
- outer_product_weight: float32 [1024, 128], replicated, may hold values from -0.5 to 0.5
- outer_product_bias: float32 [128], replicated, may hold values from -3 to 3
- up_weight: float32 [128, 512], replicated, may hold values from -0.5 to 0.5
- expand_bias: float32 [512], replicated, may hold values from -3 to 3
- down_weight: float32 [512, 128], replicated, may hold values from -0.25 to 0.25
Outputs:
- alignment_state_next: float32 [32, 1024, 256], P('wide', 'narrow')
- pair_state_next: float32 [1024, 1024, 128], P('wide', 'narrow')
All inputs are finite; a program needn't handle non-finite values.
Results may differ from a plain program's by a relative error of at most 0.0003.
Values sent between devices are 32-bit elements; how exact they have to be, the bound alone decides.
No kernel may reach another device: no remote copies, remote signals or barrier semaphores. Data moves between devices by JAX's collectives and lax.ppermute only.
A program may use at most 192 MiB of HBM per device.

v0:
```python
import math

import jax
import jax.numpy as jnp
from jax import lax
from jax.sharding import PartitionSpec as P

finest_precision = lax.Precision.HIGHEST


def layer_normalize(tensor):
    row_mean = jnp.mean(tensor, axis=-1, keepdims=True)
    centered = tensor - row_mean
    variance = jnp.mean(centered * centered, axis=-1, keepdims=True)
    return centered * lax.rsqrt(variance + 1e-05)


def matrix_multiply(first_arr, second_arr):
    return jnp.dot(
        first_arr, second_arr, precision=finest_precision, preferred_element_type=jnp.float32
    )


def per_device(
    homolog_embedding,
    pair_state,
    probe_projector,
    lookup_projector,
    content_projector,
    sigmoid_projector,
    sigmoid_offset,
    pair_bias_weight,
    mixing_projector,
    mixing_offset,
    first_factor_projector,
    second_factor_projector,
    outer_product_weight,
    outer_product_bias,
    up_weight,
    expand_bias,
    down_weight,
):
    head_count = pair_bias_weight.shape[1]
    channel_count = homolog_embedding.shape[2]
    head_width = channel_count // head_count
    alignment_normed = layer_normalize(homolog_embedding)
    query_vectors = matrix_multiply(alignment_normed, probe_projector) / math.sqrt(head_width)
    key_rows = matrix_multiply(alignment_normed, lookup_projector)
    value_rows = matrix_multiply(alignment_normed, content_projector)
    gate_logits = matrix_multiply(alignment_normed, sigmoid_projector) + sigmoid_offset
    bias_tile = jnp.einsum(
        "ijc,ch->hij", layer_normalize(pair_state), pair_bias_weight, precision=finest_precision
    )
    own_heads = lax.all_to_all(bias_tile, "narrow", split_axis=0, concat_axis=2, tiled=True)
    pair_bias = lax.all_gather(own_heads, "wide", axis=1, tiled=True)
    operands = (
        lax.all_to_all(query_vectors, "narrow", split_axis=2, concat_axis=1, tiled=True),
        lax.all_to_all(key_rows, "narrow", split_axis=2, concat_axis=1, tiled=True),
        lax.all_to_all(value_rows, "narrow", split_axis=2, concat_axis=1, tiled=True),
        lax.all_to_all(gate_logits, "narrow", split_axis=2, concat_axis=1, tiled=True),
    )
    seq_len = operands[0].shape[1]
    local_width = operands[0].shape[2]
    local_heads = pair_bias.shape[0]
    local_size = local_width // local_heads
    row_span = min(512, seq_len)
    span_count = seq_len // row_span

    def per_item(item_parts):
        query_item = item_parts[0].reshape(seq_len, local_heads, local_size)
        key_item = item_parts[1].reshape(seq_len, local_heads, local_size)
        value_item = item_parts[2].reshape(seq_len, local_heads, local_size)

        def per_block(block_index):
            query_rows = lax.dynamic_slice_in_dim(query_item, block_index * row_span, row_span, 0)
            bias_rows = lax.dynamic_slice_in_dim(pair_bias, block_index * row_span, row_span, 1)
            scores = (
                jnp.einsum("qhd,khd->hqk", query_rows, key_item, precision=finest_precision)
                + bias_rows
            )
            row_max = jnp.max(scores, axis=-1, keepdims=True)
            exponent = jnp.exp(scores - row_max)
            softmax_probabilities = exponent / jnp.sum(exponent, axis=-1, keepdims=True)
            returned_tensor = jnp.einsum(
                "hqk,khd->qhd", softmax_probabilities, value_item, precision=finest_precision
            )
            return returned_tensor.reshape(row_span, local_width)

        blocks = lax.map(per_block, jnp.arange(span_count, dtype=jnp.int32))
        return blocks.reshape(seq_len, local_width)

    outcome = lax.map(per_item, (operands[0], operands[1], operands[2]))
    outcome = outcome * jax.nn.sigmoid(operands[3])
    merged_heads = lax.all_to_all(outcome, "narrow", split_axis=1, concat_axis=2, tiled=True)
    alignment_state_next = (
        homolog_embedding + matrix_multiply(merged_heads, mixing_projector) + mixing_offset
    )
    outer_product_normed = layer_normalize(alignment_state_next)
    left_proj = jnp.einsum(
        "srm,mc->scr", outer_product_normed, first_factor_projector, precision=finest_precision
    )
    right_proj = jnp.einsum(
        "srm,mc->scr", outer_product_normed, second_factor_projector, precision=finest_precision
    )
    left_rows = lax.all_gather(left_proj, "narrow", axis=2, tiled=True)
    left_all = lax.all_to_all(left_rows, "wide", split_axis=2, concat_axis=0, tiled=True)
    seq_count = left_all.shape[0]
    tile_rows = left_all.shape[2]
    tile_cols = right_proj.shape[2]
    outer_width = left_all.shape[1] * right_proj.shape[1]
    right_all = lax.all_gather(right_proj, "wide", axis=0, tiled=True)
    block_rows = math.gcd(16, tile_rows)

    def outer_block(block_index):
        left_part = lax.dynamic_slice_in_dim(left_all, block_index * block_rows, block_rows, 2)
        product = (
            jnp.einsum("sci,sdj->ijcd", left_part, right_all, precision=finest_precision)
            / seq_count
        )
        flat = product.reshape(block_rows * tile_cols, outer_width)
        return matrix_multiply(flat, outer_product_weight).reshape(block_rows, tile_cols, -1)

    update = lax.map(outer_block, jnp.arange(tile_rows // block_rows, dtype=jnp.int32))
    update = update.reshape(tile_rows, tile_cols, -1)
    pair_mid = pair_state + update + outer_product_bias
    hidden = jax.nn.relu(matrix_multiply(layer_normalize(pair_mid), up_weight) + expand_bias)
    pair_state_next = pair_mid + matrix_multiply(hidden, down_weight)
    return (alignment_state_next, pair_state_next)


def solution(mesh):
    placed = (
        P("wide", "narrow", None),
        P("wide", "narrow", None),
        P(),
        P(),
        P(),
        P(),
        P(),
        P(),
        P(),
        P(),
        P(),
        P(),
        P(),
        P(),
        P(),
        P(),
        P(),
    )
    return jax.shard_map(
        per_device,
        mesh=mesh,
        in_specs=placed,
        out_specs=(P("wide", "narrow", None), P("wide", "narrow", None)),
        check_vma=False,
    )
```

profile of v0, /device:TPU:0, one launch (start us, length us, event | category | flops | bytes accessed | tf_op | source)
XLA Modules:
  0.0 893.6 jit_solution(2013924085573206081)
XLA Ops:
  26.8 27.4 %fusion.36 = f32[8,128,256]{2,0,1:T(8,128)S(1)} fusion(f32[128,256,128]{2,1,0:T(8,128)S(1)} %copy-done.1, f32[128,256]{1,0:T(8,128)S(1)} %add_rsqrt_fusion.1, f32[128,256]{1,0:T(8,128)S(1)} %broadcast_multiply_fusion.1, f32[128,8]{0,1:T(8,128)S(1)} %copy-done.11), kind=kOutput, calls=%fused_computation.49 | convolution fusion | flops 411041792 | bytes 18092032 | tf_op jit(solution)/shard_map/ijc,ch->hij/dot_general | solution.py:51
  54.6 19.1 %all_to_all.117 = f32[8,128,256]{2,1,0:T(8,128)S(1)} all-to-all(f32[8,128,256]{2,1,0:T(8,128)S(1)} %copy.112), channel_id=1, replica_groups=mesh['wide'=8,'narrow'=4] {'narrow'}, dimensions={0} | all-to-all | bytes 2097152 | tf_op jit(solution)/shard_map/all_to_all | solution.py:54
  156.8 111.2 %while.31 = (s32[]{:T(128)}, f32[4,1024,64]{1,2,0:T(8,128)}, f32[4,1024,64]{1,2,0:T(8,128)S(1)}, f32[4,1024,64]{1,2,0:T(8,128)}, f32[4,1024,64]{1,2,0:T(8,128)},...) while((s32[]{:T(128)}, f32[4,1024,64]{1,2,0:T(8,128)}, ...), condition=%wide.region_9.10_spmd, body=%wide.region_4.9_spmd.sunk | while | flops 811595776 | bytes 20993444 | solution.py:92
  157.9 25.5 %while.33 = (s32[]{:T(128)}, f32[2,512,64]{1,2,0:T(8,128)S(1)}, s32[2]{0:T(128)S(1)}, f32[1024,2,32]{0,2,1:T(8,128)S(1)}, f32[1024,2,32]{0,2,1:T(8,128)S(1)}, /*...) while((s32[]{:T(128)}, f32[2,512,64]{1,2,0:T(8,128)S(1)}, ...), condition=%wide.region_8.8_spmd, body=%wide.region_5.7_spmd.sunk | while | flops 811595776 | bytes 17847476 | solution.py:89
  185.7 25.5 %while.33 = (s32[]{:T(128)}, f32[2,512,64]{1,2,0:T(8,128)S(1)}, s32[2]{0:T(128)S(1)}, f32[1024,2,32]{0,2,1:T(8,128)S(1)}, f32[1024,2,32]{0,2,1:T(8,128)S(1)}, /*...) while((s32[]{:T(128)}, f32[2,512,64]{1,2,0:T(8,128)S(1)}, ...), condition=%wide.region_8.8_spmd, body=%wide.region_5.7_spmd.sunk | while | flops 811595776 | bytes 17847476 | solution.py:89
  213.5 25.5 %while.33 = (s32[]{:T(128)}, f32[2,512,64]{1,2,0:T(8,128)S(1)}, s32[2]{0:T(128)S(1)}, f32[1024,2,32]{0,2,1:T(8,128)S(1)}, f32[1024,2,32]{0,2,1:T(8,128)S(1)}, /*...) while((s32[]{:T(128)}, f32[2,512,64]{1,2,0:T(8,128)S(1)}, ...), condition=%wide.region_8.8_spmd, body=%wide.region_5.7_spmd.sunk | while | flops 811595776 | bytes 17847476 | solution.py:89
  241.3 25.5 %while.33 = (s32[]{:T(128)}, f32[2,512,64]{1,2,0:T(8,128)S(1)}, s32[2]{0:T(128)S(1)}, f32[1024,2,32]{0,2,1:T(8,128)S(1)}, f32[1024,2,32]{0,2,1:T(8,128)S(1)}, /*...) while((s32[]{:T(128)}, f32[2,512,64]{1,2,0:T(8,128)S(1)}, ...), condition=%wide.region_8.8_spmd, body=%wide.region_5.7_spmd.sunk | while | flops 811595776 | bytes 17847476 | solution.py:89
  350.4 393.9 %while.32 = (s32[]{:T(128)}, f32[8,16,256,128]{3,2,1,0:T(8,128)}, s32[8]{0:T(128)S(1)}, f32[32,32,128]{0,2,1:T(8,128)}, f32[32,32,256]{2,0,1:T(8,128)S(1)}, /*in...) while((s32[]{:T(128)}, f32[8,16,256,128]{3,2,1,0:T(8,128)}, ...), condition=%wide.region_13.14_spmd, body=%wide.region_12.13_spmd.sunk | while | flops 8057257984 | bytes 37486768 | solution.py:123
  351.7 14.4 %convolution_multiply_fusion.3 = f32[32,16,32,256]{3,1,2,0:T(8,128)S(1)} fusion(f32[32,32,256]{2,0,1:T(8,128)S(1)} %get-tuple-element.424, f32[32,32,128]{0,2,1:T(8,128)} %get-tuple-element.423, s32[]{:T(128)S(6)} %select_n.9), kind=kOutput, calls=%fused_computation.16.clone.1 | convolution fusion | flops 1614807040 | bytes 18087940 | tf_op jit(solution)/shard_map/while/body/eval_jaxpr/sci,sdj->ijcd/dot_general | solution.py:117
  366.1 32.8 %bitcast_dynamic-update-slice_fusion.4 = f32[8,16,256,128]{3,2,1,0:T(8,128)} fusion(f32[8,16,256,128]{3,2,1,0:T(8,128)} %get-tuple-element.411, s32[]{:T(128)S(6)} %copy.191, f32[16,256,1024]{1,0,2:T(8,128)S(1)} %bitcast.139, f32[1024,128]{1,0:T(8,128)S(1)} %get-tuple-element.425), kind=kOutput, calls=%fused_computation.17.clone.1 | convolution fusion | flops 6442450944 | bytes 19398660 | tf_op jit(solution)/shard_map/while/body/eval_jaxpr/dot_general | solution.py:19
  400.1 14.4 %convolution_multiply_fusion.3 = f32[32,16,32,256]{3,1,2,0:T(8,128)S(1)} fusion(f32[32,32,256]{2,0,1:T(8,128)S(1)} %get-tuple-element.424, f32[32,32,128]{0,2,1:T(8,128)} %get-tuple-element.423, s32[]{:T(128)S(6)} %select_n.9), kind=kOutput, calls=%fused_computation.16.clone.1 | convolution fusion | flops 1614807040 | bytes 18087940 | tf_op jit(solution)/shard_map/while/body/eval_jaxpr/sci,sdj->ijcd/dot_general | solution.py:117
  414.5 32.8 %bitcast_dynamic-update-slice_fusion.4 = f32[8,16,256,128]{3,2,1,0:T(8,128)} fusion(f32[8,16,256,128]{3,2,1,0:T(8,128)} %get-tuple-element.411, s32[]{:T(128)S(6)} %copy.191, f32[16,256,1024]{1,0,2:T(8,128)S(1)} %bitcast.139, f32[1024,128]{1,0:T(8,128)S(1)} %get-tuple-element.425), kind=kOutput, calls=%fused_computation.17.clone.1 | convolution fusion | flops 6442450944 | bytes 19398660 | tf_op jit(solution)/shard_map/while/body/eval_jaxpr/dot_general | solution.py:19
  448.4 14.4 %convolution_multiply_fusion.3 = f32[32,16,32,256]{3,1,2,0:T(8,128)S(1)} fusion(f32[32,32,256]{2,0,1:T(8,128)S(1)} %get-tuple-element.424, f32[32,32,128]{0,2,1:T(8,128)} %get-tuple-element.423, s32[]{:T(128)S(6)} %select_n.9), kind=kOutput, calls=%fused_computation.16.clone.1 | convolution fusion | flops 1614807040 | bytes 18087940 | tf_op jit(solution)/shard_map/while/body/eval_jaxpr/sci,sdj->ijcd/dot_general | solution.py:117
  462.8 32.8 %bitcast_dynamic-update-slice_fusion.4 = f32[8,16,256,128]{3,2,1,0:T(8,128)} fusion(f32[8,16,256,128]{3,2,1,0:T(8,128)} %get-tuple-element.411, s32[]{:T(128)S(6)} %copy.191, f32[16,256,1024]{1,0,2:T(8,128)S(1)} %bitcast.139, f32[1024,128]{1,0:T(8,128)S(1)} %get-tuple-element.425), kind=kOutput, calls=%fused_computation.17.clone.1 | convolution fusion | flops 6442450944 | bytes 19398660 | tf_op jit(solution)/shard_map/while/body/eval_jaxpr/dot_general | solution.py:19
  511.2 32.8 %bitcast_dynamic-update-slice_fusion.4 = f32[8,16,256,128]{3,2,1,0:T(8,128)} fusion(f32[8,16,256,128]{3,2,1,0:T(8,128)} %get-tuple-element.411, s32[]{:T(128)S(6)} %copy.191, f32[16,256,1024]{1,0,2:T(8,128)S(1)} %bitcast.139, f32[1024,128]{1,0:T(8,128)S(1)} %get-tuple-element.425), kind=kOutput, calls=%fused_computation.17.clone.1 | convolution fusion | flops 6442450944 | bytes 19398660 | tf_op jit(solution)/shard_map/while/body/eval_jaxpr/dot_general | solution.py:19
  559.5 32.8 %bitcast_dynamic-update-slice_fusion.4 = f32[8,16,256,128]{3,2,1,0:T(8,128)} fusion(f32[8,16,256,128]{3,2,1,0:T(8,128)} %get-tuple-element.411, s32[]{:T(128)S(6)} %copy.191, f32[16,256,1024]{1,0,2:T(8,128)S(1)} %bitcast.139, f32[1024,128]{1,0:T(8,128)S(1)} %get-tuple-element.425), kind=kOutput, calls=%fused_computation.17.clone.1 | convolution fusion | flops 6442450944 | bytes 19398660 | tf_op jit(solution)/shard_map/while/body/eval_jaxpr/dot_general | solution.py:19
  593.5 14.4 %convolution_multiply_fusion.3 = f32[32,16,32,256]{3,1,2,0:T(8,128)S(1)} fusion(f32[32,32,256]{2,0,1:T(8,128)S(1)} %get-tuple-element.424, f32[32,32,128]{0,2,1:T(8,128)} %get-tuple-element.423, s32[]{:T(128)S(6)} %select_n.9), kind=kOutput, calls=%fused_computation.16.clone.1 | convolution fusion | flops 1614807040 | bytes 18087940 | tf_op jit(solution)/shard_map/while/body/eval_jaxpr/sci,sdj->ijcd/dot_general | solution.py:117
  607.9 32.8 %bitcast_dynamic-update-slice_fusion.4 = f32[8,16,256,128]{3,2,1,0:T(8,128)} fusion(f32[8,16,256,128]{3,2,1,0:T(8,128)} %get-tuple-element.411, s32[]{:T(128)S(6)} %copy.191, f32[16,256,1024]{1,0,2:T(8,128)S(1)} %bitcast.139, f32[1024,128]{1,0:T(8,128)S(1)} %get-tuple-element.425), kind=kOutput, calls=%fused_computation.17.clone.1 | convolution fusion | flops 6442450944 | bytes 19398660 | tf_op jit(solution)/shard_map/while/body/eval_jaxpr/dot_general | solution.py:19
  641.9 14.4 %convolution_multiply_fusion.3 = f32[32,16,32,256]{3,1,2,0:T(8,128)S(1)} fusion(f32[32,32,256]{2,0,1:T(8,128)S(1)} %get-tuple-element.424, f32[32,32,128]{0,2,1:T(8,128)} %get-tuple-element.423, s32[]{:T(128)S(6)} %select_n.9), kind=kOutput, calls=%fused_computation.16.clone.1 | convolution fusion | flops 1614807040 | bytes 18087940 | tf_op jit(solution)/shard_map/while/body/eval_jaxpr/sci,sdj->ijcd/dot_general | solution.py:117
  656.3 32.8 %bitcast_dynamic-update-slice_fusion.4 = f32[8,16,256,128]{3,2,1,0:T(8,128)} fusion(f32[8,16,256,128]{3,2,1,0:T(8,128)} %get-tuple-element.411, s32[]{:T(128)S(6)} %copy.191, f32[16,256,1024]{1,0,2:T(8,128)S(1)} %bitcast.139, f32[1024,128]{1,0:T(8,128)S(1)} %get-tuple-element.425), kind=kOutput, calls=%fused_computation.17.clone.1 | convolution fusion | flops 6442450944 | bytes 19398660 | tf_op jit(solution)/shard_map/while/body/eval_jaxpr/dot_general | solution.py:19
  690.2 14.4 %convolution_multiply_fusion.3 = f32[32,16,32,256]{3,1,2,0:T(8,128)S(1)} fusion(f32[32,32,256]{2,0,1:T(8,128)S(1)} %get-tuple-element.424, f32[32,32,128]{0,2,1:T(8,128)} %get-tuple-element.423, s32[]{:T(128)S(6)} %select_n.9), kind=kOutput, calls=%fused_computation.16.clone.1 | convolution fusion | flops 1614807040 | bytes 18087940 | tf_op jit(solution)/shard_map/while/body/eval_jaxpr/sci,sdj->ijcd/dot_general | solution.py:117
  704.6 32.8 %bitcast_dynamic-update-slice_fusion.4 = f32[8,16,256,128]{3,2,1,0:T(8,128)} fusion(f32[8,16,256,128]{3,2,1,0:T(8,128)} %get-tuple-element.411, s32[]{:T(128)S(6)} %copy.191, f32[16,256,1024]{1,0,2:T(8,128)S(1)} %bitcast.139, f32[1024,128]{1,0:T(8,128)S(1)} %get-tuple-element.425), kind=kOutput, calls=%fused_computation.17.clone.1 | convolution fusion | flops 6442450944 | bytes 19398660 | tf_op jit(solution)/shard_map/while/body/eval_jaxpr/dot_general | solution.py:19
  770.0 57.5 %fusion.21 = f32[128,256,512]{2,1,0:T(8,128)} fusion(f32[128,256,128]{2,1,0:T(8,128)S(1)} %bitcast_add_fusion, f32[128,256]{1,0:T(8,128)S(1)} %add_rsqrt_fusion, f32[128,256]{1,0:T(8,128)S(1)} %broadcast_multiply_fusion, f32[128]{0:T(128)S(1)} %copy-done.9, f32[128,512]{1,0:T(8,128)S(1)} %copy-done), kind=kOutput, calls=%fused_computation.29 | convolution fusion | flops 25782386688 | bytes 84410880 | tf_op jit(solution)/shard_map/dot_general | solution.py:19
  827.5 59.1 %add_add_fusion = f32[128,256,128]{2,1,0:T(8,128)} fusion(f32[128,256,128]{2,1,0:T(8,128)S(1)} %bitcast_add_fusion, f32[128,256,512]{2,1,0:T(8,128)} %fusion.21, f32[512]{0:T(512)S(1)} %copy-done.10, f32[128]{0:T(128)S(1)} %copy-done.9, f32[512,128]{1,0:T(8,128)S(1)} %copy-done.5), kind=kOutput, calls=%fused_computation.38 | convolution fusion | flops 25811746816 | bytes 100928000 | tf_op jit(solution)/shard_map/dot_general | solution.py:19
  (181 shorter events, 349.5 us)
Async XLA Ops:
  7.2 762.8 %copy-start = (f32[128,512]{1,0:T(8,128)S(1)}, f32[128,512]{1,0:T(8,128)}, u32[]{:S(2)}) copy-start(f32[128,512]{1,0:T(8,128)} %param.37) | copy-start | bytes 786436
  7.2 19.6 %copy-start.11 = (f32[128,8]{0,1:T(8,128)S(1)}, f32[128,8]{0,1:T(8,128)}, u32[]{:S(2)}) copy-start(f32[128,8]{0,1:T(8,128)} %param.30) | copy-start | bytes 12292
  7.2 149.6 %all-gather.3.cloned.1.call-start = ((), (), s32[]{:S(2)}) async-start(), calls=%async_computation.7 | async-start | bytes 9437184 | tf_op jit(solution)/shard_map/all_gather | solution.py:55
  15.5 11.3 %copy-start.1 = (f32[128,256,128]{2,1,0:T(8,128)S(1)}, f32[128,256,128]{2,1,0:T(8,128)}, u32[]{:S(2)}) copy-start(f32[128,256,128]{2,1,0:T(8,128)} %param.24) | copy-start | bytes 50331652
  26.8 48.1 %copy-start.2 = (f32[4,256,256]{2,1,0:T(8,128)S(1)}, f32[4,256,256]{2,1,0:T(8,128)}, u32[]{:S(2)}) copy-start(f32[4,256,256]{2,1,0:T(8,128)} %param.23) | copy-start | bytes 3145732
  26.8 48.7 %copy-start.6 = (f32[256,256]{1,0:T(8,128)S(1)}, f32[256,256]{1,0:T(8,128)}, u32[]{:S(2)}) copy-start(f32[256,256]{1,0:T(8,128)} %param.28) | copy-start | bytes 786436
  26.8 48.7 %copy-start.13 = (f32[256]{0:T(256)S(1)}, f32[256]{0:T(256)}, u32[]{:S(2)}) copy-start(f32[256]{0:T(256)} %param.29) | copy-start | bytes 3076
  77.8 15.9 %all-to-all-start.4 = ((f32[4,256,256]{1,0,2:T(4,128)}), f32[4,256,256]{1,0,2:T(4,128)S(1)}, u32[]{:S(2)}, u32[]{:S(2)}) async-start(f32[4,256,256]{1,0,2:T(4,128)} %copy.114), calls=%async_computation.4 | async-start | bytes 2097152 | tf_op jit(solution)/shard_map/all_to_all | solution.py:60
  93.8 16.7 %all-to-all-start.2 = ((f32[4,256,256]{1,0,2:T(4,128)}), f32[4,256,256]{1,0,2:T(4,128)S(1)}, u32[]{:S(2)}, u32[]{:S(2)}) async-start(f32[4,256,256]{1,0,2:T(4,128)} %copy.109), calls=%async_computation.2 | async-start | bytes 2097152 | tf_op jit(solution)/shard_map/all_to_all | solution.py:59
  110.5 17.6 %all-to-all-start.1 = ((f32[4,256,256]{1,0,2:T(4,128)}), f32[4,256,256]{1,0,2:T(4,128)}, u32[]{:S(2)}, u32[]{:S(2)}) async-start(f32[4,256,256]{1,0,2:T(4,128)} %copy.106), calls=%async_computation.1 | async-start | bytes 2097152 | tf_op jit(solution)/shard_map/all_to_all | solution.py:58
  128.1 17.1 %all-to-all-start = ((f32[4,256,256]{1,0,2:T(4,128)}), f32[4,256,256]{1,0,2:T(4,128)S(1)}, u32[]{:S(2)}, u32[]{:S(2)}) async-start(f32[4,256,256]{1,0,2:T(4,128)} %copy.103), calls=%async_computation | async-start | bytes 2097152 | tf_op jit(solution)/shard_map/all_to_all | solution.py:57
  156.8 122.6 %copy-start.3 = (f32[4,256,256]{2,1,0:T(8,128)S(1)}, f32[4,256,256]{2,1,0:T(8,128)}, u32[]{:S(2)}) copy-start(f32[4,256,256]{2,1,0:T(8,128)} %param.23) | copy-start | bytes 3145732
  268.0 34.8 %copy-start.12 = (f32[256]{0:T(256)S(1)}, f32[256]{0:T(256)}, u32[]{:S(2)}) copy-start(f32[256]{0:T(256)} %param.32) | copy-start | bytes 3076
  268.0 37.7 %copy-start.7 = (f32[256,32]{0,1:T(8,128)S(1)}, f32[256,32]{0,1:T(8,128)}, u32[]{:S(2)}) copy-start(f32[256,32]{0,1:T(8,128)} %param.34) | copy-start | bytes 98308
  268.0 39.2 %copy-start.8 = (f32[256,32]{0,1:T(8,128)S(1)}, f32[256,32]{0,1:T(8,128)}, u32[]{:S(2)}) copy-start(f32[256,32]{0,1:T(8,128)} %param.33) | copy-start | bytes 98308
  275.5 17.8 %all-to-all-start.5 = ((f32[4,1,65536]{2,1,0:T(1,128)}), f32[4,1,65536]{2,1,0:T(1,128)S(1)}, u32[]{:S(2)}, u32[]{:S(2)}) async-start(f32[4,1,65536]{2,1,0:T(1,128)} %reshape.117), calls=%async_computation.5 | async-start | bytes 2097152 | tf_op jit(solution)/shard_map/all_to_all | solution.py:94
  279.1 69.4 %all-gather.5.cloned.1.call-start = ((), (), s32[]{:S(2)}) async-start(), calls=%async_computation.8 | async-start | bytes 1179648 | tf_op jit(solution)/shard_map/all_gather | solution.py:111
  298.5 51.9 %copy-start.4 = (f32[1024,128]{1,0:T(8,128)S(1)}, f32[1024,128]{1,0:T(8,128)}, u32[]{:S(2)}) copy-start(f32[1024,128]{1,0:T(8,128)} %param.35) | copy-start | bytes 1572868
  323.7 19.1 %all-to-all-start.6 = ((f32[8,1,16384]{2,1,0:T(1,128)}), f32[8,1,16384]{2,1,0:T(1,128)S(1)}, u32[]{:S(2)}, u32[]{:S(2)}) async-start(f32[8,1,16384]{2,1,0:T(1,128)} %reshape.119), calls=%async_computation.6 | async-start | bytes 1048576 | tf_op jit(solution)/shard_map/all_to_all | solution.py:106
  744.3 11.4 %copy-start.9 = (f32[128]{0:T(128)S(1)}, f32[128]{0:T(128)}, u32[]{:S(2)}) copy-start(f32[128]{0:T(128)} %param.36) | copy-start | bytes 1540
  769.9 57.5 %copy-start.5 = (f32[512,128]{1,0:T(8,128)S(1)}, f32[512,128]{1,0:T(8,128)}, u32[]{:S(2)}) copy-start(f32[512,128]{1,0:T(8,128)} %param.39) | copy-start | bytes 786436
  769.9 57.5 %copy-start.10 = (f32[512]{0:T(512)S(1)}, f32[512]{0:T(512)}, u32[]{:S(2)}) copy-start(f32[512]{0:T(512)} %param.38) | copy-start | bytes 6148
Sparse Core Ops, SparseCore 0:
  75.0 81.7 all-gather.2
  307.3 19.8 all-gather.4
where the time goes:
time: 902 us; the launch traced here: 894 us
  matrix products  618 us (69%)
  waiting for transfers between devices  70 us (8%)
  other arithmetic  64.1 us (7%)
  local copies, waits for them, and re-layouts  56.5 us (6%)
  blocking collectives  29.6 us (3%)
  starting transfers between devices  23.1 us (3%)
  loops' own time  17.1 us (2%)
  between operations  14.7 us (2%)
    dot_general x15, matrix products, matrix_multiply(): jnp.dot(first_arr, second_arr, precision=finest_precision, preferred_elem...  391 us
    dot_general x8, matrix products, outer_block(): jnp.einsum('sci,sdj->ijcd', left_part, right_all, precision=finest_precis...  115 us
    dot_general x8, matrix products, per_block(): jnp.einsum('qhd,khd->hqk', query_rows, key_item, precision=finest_precision)  45.8 us
    dot_general x8, matrix products, per_block(): jnp.einsum('hqk,khd->qhd', softmax_probabilities, value_item, precision=f...  36.8 us
    dot_general x1, matrix products, per_device(): jnp.einsum('ijc,ch->hij', layer_normalize(pair_state), pair_bias_weight,...  27.4 us
    reduce_sum x4, other arithmetic, layer_normalize(): variance = jnp.mean(centered * centered, axis=-1, keepdims=True)  21.3 us
    all_to_all x1, blocking collectives, per_device(): lax.all_to_all(bias_tile, 'narrow', split_axis=0, concat_axis=2, tiled=True)  19.1 us
  transfers between devices with their start and end apart: 8, of which 7 were waited for; matrix products, arithmetic and copies ran while one was open for 4% of the time, Pallas kernels for 0%

commit v1 on v0

v1 whole, which is shorter than its diff:
```python
import functools
import math

import jax
import jax.numpy as jnp
from jax import lax
from jax.experimental import pallas as pl
from jax.experimental.pallas import tpu as pltpu
from jax.sharding import PartitionSpec as P

F32, BF16 = jnp.float32, jnp.bfloat16
PARAMS = pltpu.CompilerParams(vmem_limit_bytes=60 * 2**20)


def split(x):
    hi = x.astype(BF16)
    lo = (x - hi.astype(F32)).astype(BF16)
    return hi, lo


def mm(a, b):
    return jnp.dot(a, b, preferred_element_type=F32)


def mm_nt(a, b):
    return lax.dot_general(a, b, (((1,), (1,)), ((), ())), preferred_element_type=F32)


def norm_rows(x):
    mean = jnp.mean(x, axis=-1, keepdims=True)
    c = x - mean
    var = jnp.mean(c * c, axis=-1, keepdims=True)
    return c * lax.rsqrt(var + 1e-05)


def whole(a):
    return pl.BlockSpec(a.shape, lambda *_: (0,) * a.ndim, pipeline_mode=pl.Buffered(1))


def bias_kernel(pair_ref, w_ref, out_ref):
    rows, cols, cz = pair_ref.shape
    heads = w_ref.shape[1]
    wh, wl = split(w_ref[...].T)
    lhs = jnp.concatenate(
        [jnp.concatenate([wh, wh], axis=1), jnp.concatenate([wl, wl], axis=1)], axis=0
    )
    for i in range(rows):
        yh, yl = split(norm_rows(pair_ref[i]))
        r = mm_nt(lhs, jnp.concatenate([yh, yl], axis=1))
        out_ref[:, i, :] = r[:heads] + r[heads:]


def bias_tile(pair, w, step=8):
    rows, cols, cz = pair.shape
    heads = w.shape[1]
    return pl.pallas_call(
        bias_kernel,
        out_shape=jax.ShapeDtypeStruct((heads, rows, cols), F32),
        grid=(rows // step,),
        in_specs=[pl.BlockSpec((step, cols, cz), lambda i: (i, 0, 0)), whole(w)],
        out_specs=pl.BlockSpec((heads, step, cols), lambda i: (0, i, 0)),
        compiler_params=PARAMS,
        name="bias_tile",
    )(pair, w)


def project_kernel(parts, scale, x_ref, wq_ref, wk_ref, wv_ref, wg_ref, bg_ref, qkv_ref, gate_ref, w_hi, w_lo):
    ch = x_ref.shape[-1]
    own = ch // parts

    @pl.when(pl.program_id(0) == 0)
    def _():
        for t, (ref, f) in enumerate(((wq_ref, scale), (wk_ref, 1.0), (wv_ref, 1.0), (wg_ref, 1.0))):
            hi, lo = split(ref[...].T * f)
            w_hi[t * ch:(t + 1) * ch, :] = hi
            w_lo[t * ch:(t + 1) * ch, :] = lo

    yh, yl = split(norm_rows(x_ref[0]))
    r = mm_nt(w_hi[...], yh) + mm_nt(w_hi[...], yl) + mm_nt(w_lo[...], yh)
    for t in range(3):
        for n in range(parts):
            lo = t * ch + n * own
            qkv_ref[n, t, 0] = r[lo:lo + own]
    gate_ref[0] = jax.nn.sigmoid(r[3 * ch:] + bg_ref[...])


def project(x, wq, wk, wv, wg, bg, parts, head_width):
    seqs, span, ch = x.shape
    own = ch // parts
    bg = bg.reshape(ch, 1)
    return pl.pallas_call(
        functools.partial(project_kernel, parts, 1.0 / math.sqrt(head_width)),
        out_shape=(
            jax.ShapeDtypeStruct((parts, 3, seqs, own, span), F32),
            jax.ShapeDtypeStruct((seqs, ch, span), F32),
        ),
        grid=(seqs,),
        in_specs=[pl.BlockSpec((1, span, ch), lambda s: (s, 0, 0))] + [whole(a) for a in (wq, wk, wv, wg, bg)],
        out_specs=(
            pl.BlockSpec((parts, 3, 1, own, span), lambda s: (0, 0, s, 0, 0)),
            pl.BlockSpec((1, ch, span), lambda s: (s, 0, 0)),
        ),
        scratch_shapes=[pltpu.VMEM((4 * ch, ch), BF16), pltpu.VMEM((4 * ch, ch), BF16)],
        compiler_params=PARAMS,
        name="project",
    )(x, wq, wk, wv, wg, bg)


def attention_kernel(hw, q_ref, k_ref, v_ref, bias_ref, out_ref, ks, vs):
    parts = k_ref.shape[0]
    span = k_ref.shape[-1]
    s = pl.program_id(1)

    @pl.when(pl.program_id(0) == 0)
    def _():
        for n in range(parts):
            at = slice(n * span, (n + 1) * span)
            hi, lo = split(k_ref[n, 0, 0])
            ks[s, 0:hw, at] = hi
            ks[s, hw:2 * hw, at] = lo
            ks[s, 2 * hw:3 * hw, at] = hi
            v = v_ref[n, 0, 0]
            vh = v.astype(BF16).astype(F32)
            st = jnp.concatenate([vh, v - vh, jnp.ones((hw, span), F32), jnp.zeros((hw, span), F32)], axis=0)
            vs[s, at, :] = st.T.astype(BF16)

    q = q_ref[0, 0, 0]
    qh = q.astype(BF16).astype(F32)
    qst = jnp.concatenate([qh, qh, q - qh, jnp.zeros_like(q)], axis=0).T[:, :3 * hw].astype(BF16)
    bias = jnp.concatenate(
        [
            jnp.concatenate([bias_ref[w, n] for n in range(parts)], axis=1)
            for w in range(bias_ref.shape[0])
        ],
        axis=0,
    )
    scores = mm(qst, ks[s]) + bias
    top = jnp.max(scores, axis=1, keepdims=True)
    ph, plo = split(jnp.exp(scores - top))
    t = (mm(ph, vs[s]) + mm(plo, vs[s])).T
    out_ref[0, 0] = (t[0:hw] + t[hw:2 * hw]) / t[2 * hw:2 * hw + 1]


def attention(qkv, bias, head, hw):
    parts, _, seqs, own, span = qkv.shape
    wide, _, rows, _ = bias.shape
    per = span // rows
    return pl.pallas_call(
        functools.partial(attention_kernel, hw),
        out_shape=jax.ShapeDtypeStruct((parts, seqs, hw, span), F32),
        grid=(parts, seqs),
        in_specs=[
            pl.BlockSpec((1, 1, 1, hw, span), lambda b, s: (b, 0, s, head, 0)),
            pl.BlockSpec((parts, 1, 1, hw, span), lambda b, s: (0, 1, s, head, 0)),
            pl.BlockSpec((parts, 1, 1, hw, span), lambda b, s: (0, 2, s, head, 0)),
            pl.BlockSpec((per, parts, rows, span), lambda b, s: (b, 0, 0, 0)),
        ],
        out_specs=pl.BlockSpec((1, 1, hw, span), lambda b, s: (b, s, 0, 0)),
        scratch_shapes=[
            pltpu.VMEM((seqs, 3 * hw, parts * span), BF16),
            pltpu.VMEM((seqs, parts * span, 4 * hw), BF16),
        ],
        compiler_params=PARAMS,
        name="attention",
    )(qkv, qkv, qkv, bias)


def merge_kernel(*refs):
    heads = len(refs) - 12
    att = refs[:heads]
    gate_ref, x_ref, wm_ref, bm_ref, f1_ref, f2_ref, next_ref, left_ref, right_ref, m_hi, m_lo, f_st = refs[heads:]
    parts, _, hw, span = att[0].shape
    ch = x_ref.shape[-1]
    hid = f1_ref.shape[1]
    blocks, _, _, rows = left_ref.shape

    @pl.when(pl.program_id(0) == 0)
    def _():
        hi, lo = split(wm_ref[...])
        m_hi[...] = hi
        m_lo[...] = lo
        hi, lo = split(jnp.concatenate([f1_ref[...], f2_ref[...]], axis=1).T)
        f_st[0:2 * hid, :] = hi
        f_st[2 * hid:4 * hid, :] = lo

    a = jnp.concatenate([att[h][n, 0] for n in range(parts) for h in range(heads)], axis=0)
    ah, al = split((a * gate_ref[0]).T)
    y = x_ref[0] + (mm(ah, m_hi[...]) + mm(al, m_hi[...]) + mm(ah, m_lo[...])) + bm_ref[...]
    next_ref[0] = y
    zh, zl = split(norm_rows(y))
    p = mm_nt(f_st[...], zh)
    p = p[:2 * hid] + p[2 * hid:] + mm_nt(f_st[0:2 * hid, :], zl)
    for b in range(blocks):
        left_ref[b, 0] = p[:hid, b * rows:(b + 1) * rows]
    right_ref[0] = p[hid:]


def merge(att, gate, x, wm, bm, f1, f2, rows):
    seqs, span, ch = x.shape
    parts, _, hw, _ = att[0].shape
    hid = f1.shape[1]
    bm = bm.reshape(1, ch)
    blocks = span // rows
    return pl.pallas_call(
        merge_kernel,
        out_shape=(
            jax.ShapeDtypeStruct(x.shape, F32),
            jax.ShapeDtypeStruct((blocks, seqs, hid, rows), F32),
            jax.ShapeDtypeStruct((seqs, hid, span), F32),
        ),
        grid=(seqs,),
        in_specs=[pl.BlockSpec((parts, 1, hw, span), lambda s: (0, s, 0, 0)) for _ in att]
        + [
            pl.BlockSpec((1, ch, span), lambda s: (s, 0, 0)),
            pl.BlockSpec((1, span, ch), lambda s: (s, 0, 0)),
        ]
        + [whole(a) for a in (wm, bm, f1, f2)],
        out_specs=(
            pl.BlockSpec((1, span, ch), lambda s: (s, 0, 0)),
            pl.BlockSpec((blocks, 1, hid, rows), lambda s: (0, s, 0, 0)),
            pl.BlockSpec((1, hid, span), lambda s: (s, 0, 0)),
        ),
        scratch_shapes=[
            pltpu.VMEM((ch, ch), BF16),
            pltpu.VMEM((ch, ch), BF16),
            pltpu.VMEM((4 * hid, ch), BF16),
        ],
        compiler_params=PARAMS,
        name="merge",
    )(*att, gate, x, wm, bm, f1, f2)


def pair_kernel(
    step_rows, seqs, left_ref, right_ref, w_ref, pair_ref, ob_ref, up_ref, eb_ref, dn_ref,
    out_ref, r_hi, r_lo, w_st, up_st, dn_st,
):
    cz = pair_ref.shape[2]
    c_n = w_ref.shape[0]
    d_n = w_ref.shape[1] // cz

    @pl.when(pl.program_id(0) == 0)
    def _():
        hi, lo = split(right_ref[...])
        r_hi[...] = hi
        r_lo[...] = lo
        hi, lo = split(w_ref[...])
        w_st[0:c_n, :] = hi
        w_st[c_n:2 * c_n, :] = lo
        w_st[2 * c_n:3 * c_n, :] = hi
        hi, lo = split(up_ref[...])
        up_st[0:cz, :] = hi
        up_st[cz:2 * cz, :] = hi
        up_st[2 * cz:3 * cz, :] = lo
        hi, lo = split(dn_ref[...])
        dn_st[:, 0:cz] = hi
        dn_st[:, cz:2 * cz] = lo

    def body(p, carry):
        lrow = left_ref[pl.ds(pl.multiple_of(p * 2 * seqs, 2 * seqs), 2 * seqs), :]
        lhi = lrow.astype(BF16).astype(F32)
        u = mm(jnp.concatenate([lhi, lhi, lrow - lhi], axis=1).astype(BF16), w_st[...])
        his, los = [], []
        for q in range(2):
            sub = u[q * seqs:(q + 1) * seqs, :]
            hi, lo = split(jnp.concatenate([sub[:, d * cz:(d + 1) * cz] for d in range(d_n)], axis=0))
            his.append(hi)
            los.append(lo)
        cross = mm(r_lo[...], jnp.concatenate(his, axis=1))
        mids = []
        for q in range(2):
            a = mm(r_hi[...], jnp.concatenate([his[q], los[q]], axis=1))
            o = a[:, :cz] + a[:, cz:] + cross[:, q * cz:(q + 1) * cz]
            mids.append(pair_ref[2 * p + q] + o / seqs + ob_ref[...])
        for q in range(2):
            yh, yl = split(norm_rows(mids[q]))
            h = mm(jnp.concatenate([yh, yl, yh], axis=1), up_st[...])
            hh, hl = split(jnp.maximum(h + eb_ref[...], 0.0))
            a = mm(hh, dn_st[...])
            out_ref[2 * p + q] = mids[q] + (a[:, :cz] + a[:, cz:] + mm(hl, dn_st[:, 0:cz]))
        return carry

    lax.fori_loop(0, step_rows // 2, body, 0, unroll=2)


def pair_update(left_rows, right_cols, w2, pair, ob, up, eb, dn, step_rows=8):
    rows, cols, cz = pair.shape
    seqs = left_rows.shape[0] // rows
    c_n = w2.shape[0]
    ob = ob.reshape(1, -1)
    eb = eb.reshape(1, -1)
    return pl.pallas_call(
        functools.partial(pair_kernel, step_rows, seqs),
        out_shape=jax.ShapeDtypeStruct(pair.shape, F32),
        grid=(rows // step_rows,),
        in_specs=[
            pl.BlockSpec((step_rows * seqs, left_rows.shape[1]), lambda i: (i, 0)),
            whole(right_cols), whole(w2),
            pl.BlockSpec((step_rows, cols, cz), lambda i: (i, 0, 0)),
            whole(ob), whole(up), whole(eb), whole(dn),
        ],
        out_specs=pl.BlockSpec((step_rows, cols, cz), lambda i: (i, 0, 0)),
        scratch_shapes=[
            pltpu.VMEM(right_cols.shape, BF16),
            pltpu.VMEM(right_cols.shape, BF16),
            pltpu.VMEM((3 * c_n, w2.shape[1]), BF16),
            pltpu.VMEM((3 * cz, up.shape[1]), BF16),
            pltpu.VMEM((up.shape[1], 2 * cz), BF16),
        ],
        compiler_params=PARAMS,
        name="pair_update",
    )(left_rows, right_cols, w2, pair, ob, up, eb, dn)


def per_device(
    parts,
    homolog_embedding,
    pair_state,
    probe_projector,
    lookup_projector,
    content_projector,
    sigmoid_projector,
    sigmoid_offset,
    pair_bias_weight,
    mixing_projector,
    mixing_offset,
    first_factor_projector,
    second_factor_projector,
    outer_product_weight,
    outer_product_bias,
    up_weight,
    expand_bias,
    down_weight,
):
    seqs, span, ch = homolog_embedding.shape
    rows, cols, cz = pair_state.shape
    heads = pair_bias_weight.shape[1]
    hw = ch // heads
    own_heads = heads // parts
    hid = first_factor_projector.shape[1]

    bias = bias_tile(pair_state, pair_bias_weight).reshape(parts, own_heads, rows, cols)
    bias = lax.all_to_all(bias, "narrow", 0, 0, tiled=True)
    gathered = [
        lax.all_gather(bias[:, h], "wide", axis=0, tiled=False) for h in range(own_heads)
    ]
    qkv, gate = project(
        homolog_embedding, probe_projector, lookup_projector, content_projector, sigmoid_projector,
        sigmoid_offset, parts, hw,
    )
    qkv = lax.all_to_all(qkv, "narrow", 0, 0, tiled=True)
    att = [
        lax.all_to_all(attention(qkv, gathered[h], h, hw), "narrow", 0, 0, tiled=True)
        for h in range(own_heads)
    ]
    alignment_state_next, left, right = merge(
        att, gate, homolog_embedding, mixing_projector, mixing_offset,
        first_factor_projector, second_factor_projector, rows,
    )
    left = lax.all_gather(left, "narrow", axis=0, tiled=True)
    left = lax.all_to_all(left, "wide", 0, 0, tiled=True)
    right = lax.all_gather(right, "wide", axis=0, tiled=True)
    left = left.reshape(-1, hid, rows)
    all_seqs = left.shape[0]
    left_rows = jnp.transpose(left, (2, 0, 1)).reshape(rows * all_seqs, hid)
    right_cols = jnp.transpose(right, (2, 1, 0)).reshape(cols, hid * all_seqs)
    pair_state_next = pair_update(
        left_rows, right_cols, outer_product_weight.reshape(hid, hid * cz), pair_state,
        outer_product_bias, up_weight, expand_bias, down_weight,
    )
    return (alignment_state_next, pair_state_next)


def solution(mesh):
    placed = (P("wide", "narrow", None), P("wide", "narrow", None)) + (P(),) * 15
    return jax.shard_map(
        functools.partial(per_device, mesh.shape["narrow"]),
        mesh=mesh,
        in_specs=placed,
        out_specs=(P("wide", "narrow", None), P("wide", "narrow", None)),
        check_vma=False,
    )
```

time: 902 us -> 332 us (0.37)
  matrix products: 618 us -> 0 us
  Pallas kernels: 0 us -> 175 us
  other arithmetic: 64.1 us -> 0 us
  local copies, waits for them, and re-layouts: 56.5 us -> 12.4 us
  blocking collectives: 29.6 us -> 70.9 us
  waiting for transfers between devices: 70 us -> 46.3 us
  loops' own time: 17.1 us -> 0 us
  starting transfers between devices: 23.1 us -> 10.9 us
    dot_general x42 -> x0, matrix products: 618 us -> none  [the longest x15 391 us: matrix_multiply(): jnp.dot(first_arr, second_arr, precision=finest_precision, preferred_elem...]
    pallas_call x0 -> x6, Pallas kernels: none -> 175 us  [the longest x1 106 us: pair_update(): pl.pallas_call(functools.partial(pair_kernel, step_rows, seqs), out_shape...]
    reduce_sum x15 -> x0, other arithmetic: 43.2 us -> none  [the longest x4 21.3 us: layer_normalize(): variance = jnp.mean(centered * centered, axis=-1, keepdims=True)]
    all_to_all x1 -> x2, blocking collectives: 19.1 us -> 60.3 us  [the longest x1 40.8 us: per_device(): qkv = lax.all_to_all(qkv, 'narrow', 0, 0, tiled=True)]
    all_to_all x6 -> x3, waiting for transfers between devices: 58.8 us -> 22.2 us  [the longest x1 15.2 us: per_device(): left = lax.all_to_all(left, 'wide', 0, 0, tiled=True)]
    another operation x6 -> x0, loops' own time: 17.1 us -> none  [the longest x1 11.5 us: per_device(): lax.map(outer_block, jnp.arange(tile_rows // block_rows, dtype=jnp.int32))]
    dynamic_slice x24 -> x0, local copies, waits for them, and re-layouts: 14.1 us -> none  [the longest x8 5.2 us: per_item(): blocks = lax.map(per_block, jnp.arange(span_count, dtype=jnp.int32))]
    all_gather x2 -> x3, waiting for transfers between devices: 11.1 us -> 23.3 us  [the longest x2 23.3 us: per_device(): lax.all_gather(bias[:, h], 'wide', axis=0, tiled=False)]
  transfers between devices with their start and end apart: 8 -> 6, of which waited for: 7 -> 3; matrix products, arithmetic and copies ran while one was open for 4% -> 2% of each run, Pallas kernels for 0% -> 13%
where the time goes in v1:
time: 332 us; the launch traced here: 330 us
  Pallas kernels  175 us (53%)
  blocking collectives  70.9 us (21%)
  waiting for transfers between devices  46.3 us (14%)
  between operations  13.8 us (4%)
  local copies, waits for them, and re-layouts  12.4 us (4%)
  starting transfers between devices  10.9 us (3%)
    pallas_call x1, Pallas kernels, pair_update(): pl.pallas_call(functools.partial(pair_kernel, step_rows, seqs), out_shape...  106 us
    all_to_all x1, blocking collectives, per_device(): qkv = lax.all_to_all(qkv, 'narrow', 0, 0, tiled=True)  40.8 us
    pallas_call x2, Pallas kernels, attention(): pl.pallas_call(functools.partial(attention_kernel, hw), out_shape=jax.Sha...  38.1 us
    all_gather x2, waiting for transfers between devices, per_device(): lax.all_gather(bias[:, h], 'wide', axis=0, tiled=False)  23.3 us
    pallas_call x1, Pallas kernels, bias_tile(): pl.pallas_call(bias_kernel, out_shape=jax.ShapeDtypeStruct((heads, rows,...  19.6 us
    all_to_all x1, blocking collectives, per_device(): bias = lax.all_to_all(bias, 'narrow', 0, 0, tiled=True)  19.5 us
    all_to_all x1, waiting for transfers between devices, per_device(): left = lax.all_to_all(left, 'wide', 0, 0, tiled=True)  15.2 us
    all_gather x1, blocking collectives, per_device(): left = lax.all_gather(left, 'narrow', axis=0, tiled=True)  10.6 us
  transfers between devices with their start and end apart: 6, of which 3 were waited for; matrix products, arithmetic and copies ran while one was open for 2% of the time, Pallas kernels for 13%

profile of v1, /device:TPU:0, one launch (start us, length us, event | category | flops | bytes accessed | tf_op | source)
XLA Modules:
  0.0 329.7 jit_solution(12866894421726091419)
XLA Ops:
  7.2 1.4 copy.34.w_ref
  8.6 19.6 %bias_tile.1 = f32[8,128,256]{2,1,0:T(8,128)} custom-call(f32[128,256,128]{2,1,0:T(8,128)} %pair_ref.3, f32[128,8]{1,0:T(8,128)} %copy.34.w_ref), custom_call_target="tpu_custom_call" | custom-call | tf_op jit(solution)/shard_map/bias_tile/pallas_call | solution.py:56
  28.2 19.5 %all_to_all.25 = f32[4,2,128,256]{3,2,1,0:T(8,128)S(1)} all-to-all(f32[4,2,128,256]{3,2,1,0:T(8,128)} %bitcast.17), channel_id=1, replica_groups=mesh['wide'=8,'narrow'=4] {'narrow'}, dimensions={0} | all-to-all | bytes 2097152 | tf_op jit(solution)/shard_map/all_to_all | solution.py:342
  47.7 1.1 fusion
  49.6 0.8 copy.33.bg_ref
  50.3 6.4 %project.1 = (f32[4,3,4,64,256]{4,3,2,1,0:T(8,128)}, f32[4,256,256]{2,1,0:T(8,128)}) custom-call(f32[4,256,256]{2,1,0:T(8,128)} %refs_3_.1, f32[256,256]{1,0:T(8,128)} %wq_ref.1, f32[256,256]{1,0:T(8,128)} %wk_ref.1, f32[256,256]{1,0:T(8,128)} %wv_ref.1, f32[256,256]{1,0:T(8,128)} %wg_ref.1, f32[256,1]{1,0:T(8,128)} %copy.33.bg_ref), custom_call_target="tpu_custom_call" | custom-call | tf_op jit(solution)/shard_map/project/pallas_call | solution.py:91
  56.7 40.8 %all_to_all.26.q_ref.k_ref.v_ref = f32[4,3,4,64,256]{4,3,2,1,0:T(8,128)} all-to-all(f32[4,3,4,64,256]{4,3,2,1,0:T(8,128)} %get-tuple-element.7), channel_id=1, replica_groups=mesh['wide'=8,'narrow'=4] {'narrow'}, dimensions={0} | all-to-all | bytes 6291456 | tf_op jit(solution)/shard_map/all_to_all | solution.py:350
  97.5 19.1 %attention.2 = f32[4,4,32,256]{3,2,1,0:T(8,128)} custom-call(f32[4,3,4,64,256]{4,3,2,1,0:T(8,128)} %all_to_all.26.q_ref.k_ref.v_ref, f32[4,3,4,64,256]{4,3,2,1,0:T(8,128)} %all_to_all.26.q_ref.k_ref.v_ref, f32[4,3,4,64,256]{4,3,2,1,0:T(8,128)} %all_to_all.26.q_ref.k_ref.v_ref, f32[8,4,128,256]{3,2,1,0:T(8,128)} %bitcast.15), custom_call_target="tpu_custom_call" | custom-call | tf_op jit(solution)/shard_map/attention/pallas_call | solution.py:148
  116.7 3.5 %all-to-all-start.2 = ((f32[4,4,32,256]{3,2,1,0:T(8,128)}), f32[4,4,32,256]{3,2,1,0:T(8,128)S(1)}, u32[]{:S(2)}, u32[]{:S(2)}) async-start(f32[4,4,32,256]{3,2,1,0:T(8,128)} %attention.2), calls=%async_computation.2 | async-start | bytes 1048576 | tf_op jit(solution)/shard_map/all_to_all | solution.py:352
  120.2 23.3 %all-gather.10.cloned.1.call-done = f32[32,1,128,256]{3,2,1,0:T(8,128)} async-done(((f32[4,1,128,256]{3,2,1,0:T(8,128)}), f32[32,1,128,256]{3,2,1,0:T(8,128)}) %all-gather.10.cloned.1.call-update) | async-done | bytes 4194320 | tf_op jit(solution)/shard_map/all_gather | solution.py:344
  143.5 19.0 %attention.3 = f32[4,4,32,256]{3,2,1,0:T(8,128)} custom-call(f32[4,3,4,64,256]{4,3,2,1,0:T(8,128)} %all_to_all.26.q_ref.k_ref.v_ref, f32[4,3,4,64,256]{4,3,2,1,0:T(8,128)} %all_to_all.26.q_ref.k_ref.v_ref, f32[4,3,4,64,256]{4,3,2,1,0:T(8,128)} %all_to_all.26.q_ref.k_ref.v_ref, f32[8,4,128,256]{3,2,1,0:T(8,128)} %bitcast.16), custom_call_target="tpu_custom_call" | custom-call | tf_op jit(solution)/shard_map/attention/pallas_call | solution.py:148
  162.5 3.8 %all-to-all-start.3 = ((f32[4,4,32,256]{3,2,1,0:T(8,128)}), f32[4,4,32,256]{3,2,1,0:T(8,128)S(1)}, u32[]{:S(2)}, u32[]{:S(2)}) async-start(f32[4,4,32,256]{3,2,1,0:T(8,128)} %attention.3), calls=%async_computation.3 | async-start | bytes 1048576 | tf_op jit(solution)/shard_map/all_to_all | solution.py:352
  167.0 0.7 copy.36.refs_7_
  167.8 7.0 %all-to-all-done.3.refs_1_ = f32[4,4,32,256]{3,2,1,0:T(8,128)S(1)} async-done(((f32[4,4,32,256]{3,2,1,0:T(8,128)}), f32[4,4,32,256]{3,2,1,0:T(8,128)S(1)}, u32[]{:S(2)}, u32[]{:S(2)}) %all-to-all-start.3) | async-done | bytes 524320 | tf_op jit(solution)/shard_map/all_to_all | solution.py:352
  174.8 0.8 copy-done.1
  175.6 5.6 %merge.1 = (f32[4,256,256]{2,1,0:T(8,128)}, f32[2,4,32,128]{3,2,1,0:T(8,128)}, f32[4,32,256]{2,1,0:T(8,128)}) custom-call(f32[4,4,32,256]{3,2,1,0:T(8,128)} %copy-done, f32[4,4,32,256]{3,2,1,0:T(8,128)} %copy-done.1, f32[4,256,256]{2,1,0:T(8,128)} %get-tuple-element.8.refs_2_, f32[4,256,256]{2,1,0:T(8,128)} %refs_3_.1, f32[256,256]{1,0:T(8,128)} %refs_4_.1, ...), custom_call_target="tpu_custom_call" | custom-call | tf_op jit(solution)/shard_map/merge/pallas_call | solution.py:204
  181.2 10.6 %all_gather.14 = f32[8,4,32,128]{3,2,1,0:T(8,128)} all-gather(f32[2,4,32,128]{3,2,1,0:T(8,128)} %get-tuple-element.10), channel_id=1, replica_groups=mesh['wide'=8,'narrow'=4] {'narrow'}, dimensions={0}, use_global_device_ids=true | all-gather | bytes 655360 | tf_op jit(solution)/shard_map/all_gather | solution.py:359
  191.8 3.5 %all-to-all-start.4 = ((f32[8,4,32,128]{3,2,1,0:T(8,128)}), f32[8,4,32,128]{3,2,1,0:T(8,128)S(1)}, u32[]{:S(2)}, u32[]{:S(2)}) async-start(f32[8,4,32,128]{3,2,1,0:T(8,128)} %all_gather.14), calls=%async_computation.4 | async-start | bytes 1048576 | tf_op jit(solution)/shard_map/all_to_all | solution.py:360
  195.3 0.9 reshape.37.w_ref
  196.2 15.2 %all-to-all-done.4 = f32[8,4,32,128]{3,2,1,0:T(8,128)S(1)} async-done(((f32[8,4,32,128]{3,2,1,0:T(8,128)}), f32[8,4,32,128]{3,2,1,0:T(8,128)S(1)}, u32[]{:S(2)}, u32[]{:S(2)}) %all-to-all-start.4) | async-done | bytes 524320 | tf_op jit(solution)/shard_map/all_to_all | solution.py:360
  211.4 2.8 copy.37
  214.2 1.8 copy.38
  216.1 1.3 copy.39.right_ref
  217.4 105.8 %pair_update.1 = f32[128,256,128]{2,1,0:T(8,128)} custom-call(f32[4096,32]{1,0:T(8,128)} %bitcast.14, f32[256,1024]{1,0:T(8,128)} %copy.39.right_ref, f32[32,4096]{1,0:T(8,128)} %reshape.37.w_ref, f32[128,256,128]{2,1,0:T(8,128)} %pair_ref.3, f32[1,128]{1,0:T(1,128)} %bitcast.23, f32[128,512]{1,0:T(8,128)} %up_ref.1, f32[1,512]{1,0:T(1,128)} %bitcast.20, ...), custom_call_target="tpu_custom_call" | custom-call | tf_op jit(solution)/shard_map/pair_update/pallas_call | solution.py:291
  (21 shorter events, 1.6 us)
Async XLA Ops:
  7.2 90.4 %all-gather.8.cloned.1.call-start = ((), (), s32[]{:S(2)}) async-start(), calls=%async_computation.6 | async-start | bytes 4718592 | tf_op jit(solution)/shard_map/all_gather | solution.py:344
  28.2 21.3 %copy-start.5 = (f32[256]{0:T(256)S(1)}, f32[256]{0:T(256)}, u32[]{:S(2)}) copy-start(f32[256]{0:T(256)} %param.23) | copy-start | bytes 3076
  48.8 94.7 %all-gather.10.cloned.1.call-start = ((), (), s32[]{:S(2)}) async-start(), calls=%async_computation.7 | async-start | bytes 4718592 | tf_op jit(solution)/shard_map/all_gather | solution.py:344
  116.7 45.8 %all-to-all-start.2 = ((f32[4,4,32,256]{3,2,1,0:T(8,128)}), f32[4,4,32,256]{3,2,1,0:T(8,128)S(1)}, u32[]{:S(2)}, u32[]{:S(2)}) async-start(f32[4,4,32,256]{3,2,1,0:T(8,128)} %attention.2), calls=%async_computation.2 | async-start | bytes 1048576 | tf_op jit(solution)/shard_map/all_to_all | solution.py:352
  143.5 22.8 %copy-start.3 = (f32[256,32]{0,1:T(8,128)S(1)}, f32[256,32]{0,1:T(8,128)}, u32[]{:S(2)}) copy-start(f32[256,32]{0,1:T(8,128)} %param.27) | copy-start | bytes 98308
  143.5 23.6 %copy-start.4 = (f32[256,32]{0,1:T(8,128)S(1)}, f32[256,32]{0,1:T(8,128)}, u32[]{:S(2)}) copy-start(f32[256,32]{0,1:T(8,128)} %param.28) | copy-start | bytes 98308
  162.5 32.9 %copy-start.2 = (f32[1024,128]{1,0:T(8,128)S(1)}, f32[1024,128]{1,0:T(8,128)}, u32[]{:S(2)}) copy-start(f32[1024,128]{1,0:T(8,128)} %param.29) | copy-start | bytes 1572868
  162.5 12.3 %copy-start = (f32[4,4,32,256]{3,2,1,0:T(8,128)}, f32[4,4,32,256]{3,2,1,0:T(8,128)S(1)}, u32[]{:S(2)}) copy-start(f32[4,4,32,256]{3,2,1,0:T(8,128)S(1)} %all-to-all-done.2.refs_0_) | copy-start | bytes 1572868
  162.5 12.3 %all-to-all-start.3 = ((f32[4,4,32,256]{3,2,1,0:T(8,128)}), f32[4,4,32,256]{3,2,1,0:T(8,128)S(1)}, u32[]{:S(2)}, u32[]{:S(2)}) async-start(f32[4,4,32,256]{3,2,1,0:T(8,128)} %attention.3), calls=%async_computation.3 | async-start | bytes 1048576 | tf_op jit(solution)/shard_map/all_to_all | solution.py:352
  166.3 48.0 %all-gather.6.cloned.1.call-start = ((), (), s32[]{:S(2)}) async-start(), calls=%async_computation.5 | async-start | bytes 1179648 | tf_op jit(solution)/shard_map/all_gather | solution.py:361
  174.8 0.8 copy-start.1
  191.8 19.6 %all-to-all-start.4 = ((f32[8,4,32,128]{3,2,1,0:T(8,128)}), f32[8,4,32,128]{3,2,1,0:T(8,128)S(1)}, u32[]{:S(2)}, u32[]{:S(2)}) async-start(f32[8,4,32,128]{3,2,1,0:T(8,128)} %all_gather.14), calls=%async_computation.4 | async-start | bytes 1048576 | tf_op jit(solution)/shard_map/all_to_all | solution.py:360
Sparse Core Ops, SparseCore 0:
  48.9 46.6 all-gather.7
  97.8 45.6 all-gather.9
  181.3 21.3 all-gather.5

commit v2 on v1

--- a/solution.py
+++ b/solution.py
@@ -231,10 +231,10 @@
 
 
 def pair_kernel(
-    step_rows, seqs, left_ref, right_ref, w_ref, pair_ref, ob_ref, up_ref, eb_ref, dn_ref,
+    step_rows, group, seqs, left_ref, right_ref, w_ref, pair_ref, ob_ref, up_ref, eb_ref, dn_ref,
     out_ref, r_hi, r_lo, w_st, up_st, dn_st,
 ):
-    cz = pair_ref.shape[2]
+    _, cols, cz = pair_ref.shape
     c_n = w_ref.shape[0]
     d_n = w_ref.shape[1] // cz
 
@@ -256,40 +256,44 @@
         dn_st[:, cz:2 * cz] = lo
 
     def body(p, carry):
-        lrow = left_ref[pl.ds(pl.multiple_of(p * 2 * seqs, 2 * seqs), 2 * seqs), :]
+        lrow = left_ref[pl.ds(pl.multiple_of(p * group * seqs, group * seqs), group * seqs), :]
         lhi = lrow.astype(BF16).astype(F32)
         u = mm(jnp.concatenate([lhi, lhi, lrow - lhi], axis=1).astype(BF16), w_st[...])
         his, los = [], []
-        for q in range(2):
+        for q in range(group):
             sub = u[q * seqs:(q + 1) * seqs, :]
             hi, lo = split(jnp.concatenate([sub[:, d * cz:(d + 1) * cz] for d in range(d_n)], axis=0))
             his.append(hi)
             los.append(lo)
-        cross = mm(r_lo[...], jnp.concatenate(his, axis=1))
         mids = []
-        for q in range(2):
-            a = mm(r_hi[...], jnp.concatenate([his[q], los[q]], axis=1))
-            o = a[:, :cz] + a[:, cz:] + cross[:, q * cz:(q + 1) * cz]
-            mids.append(pair_ref[2 * p + q] + o / seqs + ob_ref[...])
-        for q in range(2):
-            yh, yl = split(norm_rows(mids[q]))
+        for q in range(0, group, 2):
+            cross = mm(r_lo[...], jnp.concatenate(his[q:q + 2], axis=1))
+            for i in range(2):
+                a = mm(r_hi[...], jnp.concatenate([his[q + i], los[q + i]], axis=1))
+                o = a[:, :cz] + a[:, cz:] + cross[:, i * cz:(i + 1) * cz]
+                mids.append(pair_ref[group * p + q + i] + o / seqs + ob_ref[...])
+        for q in range(0, group, 2):
+            mid = jnp.concatenate(mids[q:q + 2], axis=0)
+            yh, yl = split(norm_rows(mid))
             h = mm(jnp.concatenate([yh, yl, yh], axis=1), up_st[...])
             hh, hl = split(jnp.maximum(h + eb_ref[...], 0.0))
             a = mm(hh, dn_st[...])
-            out_ref[2 * p + q] = mids[q] + (a[:, :cz] + a[:, cz:] + mm(hl, dn_st[:, 0:cz]))
+            o = mid + (a[:, :cz] + a[:, cz:] + mm(hl, dn_st[:, 0:cz]))
+            for i in range(2):
+                out_ref[group * p + q + i] = o[i * cols:(i + 1) * cols]
         return carry
 
-    lax.fori_loop(0, step_rows // 2, body, 0, unroll=2)
-
-
-def pair_update(left_rows, right_cols, w2, pair, ob, up, eb, dn, step_rows=8):
+    lax.fori_loop(0, step_rows // group, body, 0)
+
+
+def pair_update(left_rows, right_cols, w2, pair, ob, up, eb, dn, step_rows=8, group=4):
     rows, cols, cz = pair.shape
     seqs = left_rows.shape[0] // rows
     c_n = w2.shape[0]
     ob = ob.reshape(1, -1)
     eb = eb.reshape(1, -1)
     return pl.pallas_call(
-        functools.partial(pair_kernel, step_rows, seqs),
+        functools.partial(pair_kernel, step_rows, group, seqs),
         out_shape=jax.ShapeDtypeStruct(pair.shape, F32),
         grid=(rows // step_rows,),
         in_specs=[
@@ -311,7 +315,7 @@
     )(left_rows, right_cols, w2, pair, ob, up, eb, dn)
 
 
-def per_device(
+def spread_heads(
     parts,
     homolog_embedding,
     pair_state,
@@ -370,10 +374,422 @@
     return (alignment_state_next, pair_state_next)
 
 
+AXES = ("wide", "narrow")
+PLANES, CORES = 4, 2
+PARTNER = {1: 2, 2: 1}
+OUTWARD = {1: 0, 2: 3}
+ORDER = ((0, 1, 2, 3), (1, 0, 2, 3), (2, 3, 1, 0), (3, 2, 1, 0))
+
+
+def send(x, parts, route):
+    pairs = []
+    for z in range(PLANES):
+        for c in range(CORES):
+            for n in range(parts):
+                to = route(z, c, n)
+                if to is not None:
+                    pairs.append(((z * CORES + c) * parts + n, (to[0] * CORES + to[1]) * parts + to[2]))
+    return lax.ppermute(x, AXES, pairs)
+
+
+def exchange(blocks, parts):
+    out = [blocks[0]]
+    for k in range(1, len(blocks)):
+        dn, dc = divmod(k, CORES)
+        out.append(send(blocks[k], parts, lambda z, c, n: (z, c ^ dc, n ^ dn)))
+    return out
+
+
+def line_gather(x, parts):
+    middle = lambda table: lambda z, c, n: (table[z], c, n) if z in table else None
+    near = send(x, parts, lambda z, c, n: (z ^ 1, c, n))
+    across = send(x, parts, middle(PARTNER))
+    out2 = send(across, parts, middle(OUTWARD))
+    far = send(near, parts, middle(PARTNER))
+    out3 = send(far, parts, middle(OUTWARD))
+    return near, (across, out2), (far, out3)
+
+
+def head_bias_kernel(group, pair_ref, w_ref, *refs):
+    out_refs, w_st = refs[:-1], refs[-1]
+    rows, cols, cz = pair_ref.shape
+    heads = len(out_refs)
+    lanes = heads * group
+
+    @pl.when(pl.program_id(0) == 0)
+    def _():
+        w = w_ref[...]
+        hi = w.astype(BF16).astype(F32)
+        row_of = lax.broadcasted_iota(jnp.int32, w.shape, 1) % group
+        for i in range(group):
+            h = jnp.where(row_of == i, hi, 0.0).astype(BF16)
+            l = jnp.where(row_of == i, w - hi, 0.0).astype(BF16)
+            for t in range(2):
+                w_st[i, t * cz:(t + 1) * cz, 0:lanes] = h
+                w_st[i, t * cz:(t + 1) * cz, lanes:2 * lanes] = l
+
+    for g in range(0, rows, group):
+        ys = []
+        for i in range(group):
+            yh, yl = split(norm_rows(pair_ref[g + i]))
+            ys += [yh, yl]
+        r = mm(jnp.concatenate(ys, axis=1), w_st[...].reshape(group * 2 * cz, 2 * lanes))
+        t = (r[:, :lanes] + r[:, lanes:]).T
+        for k in range(heads):
+            out_refs[k][g:g + group, :] = t[k * group:(k + 1) * group]
+
+
+def head_bias(pair, w, heads, step=32):
+    rows, cols, cz = pair.shape
+    group = w.shape[1] // heads
+    return pl.pallas_call(
+        functools.partial(head_bias_kernel, group),
+        out_shape=(jax.ShapeDtypeStruct((rows, cols), F32),) * heads,
+        grid=(rows // step,),
+        in_specs=[pl.BlockSpec((step, cols, cz), lambda i: (i, 0, 0)), whole(w)],
+        out_specs=(pl.BlockSpec((step, cols), lambda i: (i, 0)),) * heads,
+        scratch_shapes=[pltpu.VMEM((group, 2 * cz, 2 * heads * group), BF16)],
+        compiler_params=PARAMS,
+        name="head_bias",
+    )(pair, w)
+
+
+def head_project_kernel(heads, scale, me_ref, x_ref, wq_ref, wk_ref, wv_ref, wg_ref, bg_ref, *refs):
+    qkv_refs, (gate_ref, w_t, b_p, w_hi, w_lo) = refs[:heads], refs[heads:]
+    ch = x_ref.shape[-1]
+    hw = ch // heads
+
+    @pl.when(pl.program_id(0) == 0)
+    def _():
+        me = me_ref[0]
+        for t, (ref, f) in enumerate(((wq_ref, scale), (wk_ref, 1.0), (wv_ref, 1.0), (wg_ref, 1.0))):
+            w_t[...] = ref[...].T * f
+            for k in range(heads):
+                src = pl.ds(pl.multiple_of((me ^ k) * hw, hw), hw)
+                hi, lo = split(w_t[src, :])
+                at = slice(t * ch + k * hw, t * ch + (k + 1) * hw)
+                w_hi[at, :] = hi
+                w_lo[at, :] = lo
+                if t == 3:
+                    b_p[k * hw:(k + 1) * hw, :] = bg_ref[src, :]
+
+    yh, yl = split(norm_rows(x_ref[0]))
+    r = mm_nt(w_hi[...], yh) + mm_nt(w_hi[...], yl) + mm_nt(w_lo[...], yh)
+    for t in range(3):
+        for k in range(heads):
+            lo = t * ch + k * hw
+            qkv_refs[k][t, 0] = r[lo:lo + hw]
+    gate_ref[0] = jax.nn.sigmoid(r[3 * ch:] + b_p[...])
+
+
+def head_project(me, x, wq, wk, wv, wg, bg, heads):
+    seqs, span, ch = x.shape
+    hw = ch // heads
+    bg = bg.reshape(ch, 1)
+    return pl.pallas_call(
+        functools.partial(head_project_kernel, heads, 1.0 / math.sqrt(hw)),
+        out_shape=(jax.ShapeDtypeStruct((3, seqs, hw, span), F32),) * heads
+        + (jax.ShapeDtypeStruct((seqs, ch, span), F32),),
+        grid_spec=pltpu.PrefetchScalarGridSpec(
+            num_scalar_prefetch=1,
+            grid=(seqs,),
+            in_specs=[pl.BlockSpec((1, span, ch), lambda s, _: (s, 0, 0))]
+            + [whole(a) for a in (wq, wk, wv, wg, bg)],
+            out_specs=(pl.BlockSpec((3, 1, hw, span), lambda s, _: (0, s, 0, 0)),) * heads
+            + (pl.BlockSpec((1, ch, span), lambda s, _: (s, 0, 0)),),
+            scratch_shapes=[
+                pltpu.VMEM((ch, ch), F32),
+                pltpu.VMEM((ch, 1), F32),
+                pltpu.VMEM((4 * ch, ch), BF16),
+                pltpu.VMEM((4 * ch, ch), BF16),
+            ],
+        ),
+        compiler_params=PARAMS,
+        name="head_project",
+    )(me, x, wq, wk, wv, wg, bg)
+
+
+def stage_kernel(n_ref, *refs):
+    pieces, (q_ref, k_ref, v_ref) = refs[:-3], refs[-3:]
+    _, _, hw, span = pieces[0].shape
+    for p, ref in enumerate(pieces):
+        part, core = divmod(p, CORES)
+        at = slice(part * span, (part + 1) * span)
+        q = ref[0, 0]
+        qh = q.astype(BF16).astype(F32)
+        q_ref[core, 0, n_ref[0] ^ part] = (
+            jnp.concatenate([qh, qh, q - qh, jnp.zeros_like(q)], axis=0).T.astype(BF16)
+        )
+        hi, lo = split(ref[1, 0])
+        k_ref[core, 0, 0:hw, at] = hi
+        k_ref[core, 0, hw:2 * hw, at] = lo
+        k_ref[core, 0, 2 * hw:3 * hw, at] = hi
+        k_ref[core, 0, 3 * hw:4 * hw, at] = jnp.zeros_like(hi)
+        v = ref[2, 0]
+        vh = v.astype(BF16).astype(F32)
+        st = jnp.concatenate([vh, v - vh, jnp.ones((hw, span), F32), jnp.zeros((hw, span), F32)], axis=0)
+        v_ref[core, 0, at, :] = st.T.astype(BF16)
+
+
+def stage(n, pieces, parts):
+    _, seqs, hw, span = pieces[0].shape
+    return pl.pallas_call(
+        stage_kernel,
+        out_shape=(
+            jax.ShapeDtypeStruct((CORES, seqs, parts, span, 4 * hw), BF16),
+            jax.ShapeDtypeStruct((CORES, seqs, 4 * hw, parts * span), BF16),
+            jax.ShapeDtypeStruct((CORES, seqs, parts * span, 4 * hw), BF16),
+        ),
+        grid_spec=pltpu.PrefetchScalarGridSpec(
+            num_scalar_prefetch=1,
+            grid=(seqs,),
+            in_specs=[pl.BlockSpec((3, 1, hw, span), lambda s, _: (0, s, 0, 0)) for _ in pieces],
+            out_specs=(
+                pl.BlockSpec((CORES, 1, parts, span, 4 * hw), lambda s, _: (0, s, 0, 0, 0)),
+                pl.BlockSpec((CORES, 1, 4 * hw, parts * span), lambda s, _: (0, s, 0, 0)),
+                pl.BlockSpec((CORES, 1, parts * span, 4 * hw), lambda s, _: (0, s, 0, 0)),
+            ),
+        ),
+        compiler_params=PARAMS,
+        name="stage",
+    )(n, *pieces)
+
+
+def head_attention_kernel(hw, at_ref, q_ref, k_ref, v_ref, *refs):
+    bias_refs, out_ref = refs[:-2], refs[-1]
+    _, parts, rows, _ = bias_refs[0].shape
+    cores, seqs = q_ref.shape[:2]
+    bias = jnp.concatenate(
+        [
+            jnp.concatenate([sum(b[h ^ at_ref[2], n] for b in bias_refs) for n in range(parts)], axis=1)
+            for h in range(CORES)
+        ],
+        axis=0,
+    )
+    for g in range(cores):
+        for s in range(seqs):
+            scores = mm(q_ref[g, s, 0], k_ref[g, s]) + bias
+            top = jnp.max(scores, axis=1, keepdims=True)
+            ph, plo = split(jnp.exp(scores - top))
+            t = (mm(ph, v_ref[g, s]) + mm(plo, v_ref[g, s])).T
+            out_ref[0, g, s] = (t[0:hw] + t[hw:2 * hw]) / t[2 * hw:2 * hw + 1]
+
+
+def head_attention(at, q, k, v, tiles, prev, hw, step=2):
+    cores, seqs, parts, span, _ = q.shape
+    return pl.pallas_call(
+        functools.partial(head_attention_kernel, hw),
+        out_shape=jax.ShapeDtypeStruct(prev.shape, F32),
+        grid_spec=pltpu.PrefetchScalarGridSpec(
+            num_scalar_prefetch=1,
+            grid=(seqs // step,),
+            in_specs=[
+                pl.BlockSpec((cores, step, 1, span, 4 * hw), lambda s, at: (0, s, at[0], 0, 0)),
+                pl.BlockSpec((cores, step, 4 * hw, parts * span), lambda s, at: (0, s, 0, 0)),
+                pl.BlockSpec((cores, step, parts * span, 4 * hw), lambda s, at: (0, s, 0, 0)),
+            ]
+            + [whole(b) for b in tiles]
+            + [pl.BlockSpec(memory_space=pl.ANY)],
+            out_specs=pl.BlockSpec((1, cores, step, hw, span), lambda s, at: (at[1], 0, s, 0, 0)),
+        ),
+        input_output_aliases={4 + len(tiles): 0},
+        compiler_params=PARAMS,
+        name="head_attention",
+    )(at, q, k, v, *tiles, prev)
+
+
+def head_merge_kernel(heads, me_ref, *refs):
+    pieces = refs[:heads]
+    gate_ref, x_ref, wm_ref, bm_ref, f1_ref, f2_ref = refs[heads:heads + 6]
+    next_ref, left_refs, right_ref = refs[heads + 6], refs[heads + 7:heads + 9], refs[heads + 9]
+    m_hi, m_lo, f_st = refs[heads + 10:]
+    _, hw, span = pieces[0].shape
+    hid = f1_ref.shape[1]
+    rows = span // CORES
+
+    @pl.when(pl.program_id(0) == 0)
+    def _():
+        for k in range(heads):
+            hi, lo = split(wm_ref[pl.ds(pl.multiple_of((me_ref[0] ^ k) * hw, hw), hw), :])
+            m_hi[k * hw:(k + 1) * hw, :] = hi
+            m_lo[k * hw:(k + 1) * hw, :] = lo
+        hi, lo = split(jnp.concatenate([f1_ref[...], f2_ref[...]], axis=1).T)
+        f_st[0:2 * hid, :] = hi
+        f_st[2 * hid:4 * hid, :] = lo
+
+    a = jnp.concatenate([p[0] for p in pieces], axis=0)
+    ah, al = split((a * gate_ref[0]).T)
+    y = x_ref[0] + (mm(ah, m_hi[...]) + mm(al, m_hi[...]) + mm(ah, m_lo[...])) + bm_ref[...]
+    next_ref[0] = y
+    zh, zl = split(norm_rows(y))
+    p = mm_nt(f_st[...], zh)
+    p = p[:2 * hid] + p[2 * hid:] + mm_nt(f_st[0:2 * hid, :], zl)
+    swap = me_ref[1] == 1
+    left_refs[0][0] = jnp.where(swap, p[:hid, rows:], p[:hid, :rows])
+    left_refs[1][0] = jnp.where(swap, p[:hid, :rows], p[:hid, rows:])
+    right_ref[0] = p[hid:]
+
+
+def head_merge(me, pieces, gate, x, wm, bm, f1, f2):
+    seqs, span, ch = x.shape
+    heads = len(pieces)
+    hw = ch // heads
+    hid = f1.shape[1]
+    rows = span // CORES
+    bm = bm.reshape(1, ch)
+    return pl.pallas_call(
+        functools.partial(head_merge_kernel, heads),
+        out_shape=(jax.ShapeDtypeStruct(x.shape, F32),)
+        + (jax.ShapeDtypeStruct((seqs, hid, rows), F32),) * CORES
+        + (jax.ShapeDtypeStruct((seqs, hid, span), F32),),
+        grid_spec=pltpu.PrefetchScalarGridSpec(
+            num_scalar_prefetch=1,
+            grid=(seqs,),
+            in_specs=[pl.BlockSpec((1, hw, span), lambda s, _: (s, 0, 0)) for _ in pieces]
+            + [
+                pl.BlockSpec((1, ch, span), lambda s, _: (s, 0, 0)),
+                pl.BlockSpec((1, span, ch), lambda s, _: (s, 0, 0)),
+            ]
+            + [whole(a) for a in (wm, bm, f1, f2)],
+            out_specs=(pl.BlockSpec((1, span, ch), lambda s, _: (s, 0, 0)),)
+            + (pl.BlockSpec((1, hid, rows), lambda s, _: (s, 0, 0)),) * CORES
+            + (pl.BlockSpec((1, hid, span), lambda s, _: (s, 0, 0)),),
+            scratch_shapes=[
+                pltpu.VMEM((ch, ch), BF16),
+                pltpu.VMEM((ch, ch), BF16),
+                pltpu.VMEM((4 * hid, ch), BF16),
+            ],
+        ),
+        compiler_params=PARAMS,
+        name="head_merge",
+    )(me, *pieces, gate, x, wm, bm, f1, f2)
+
+
+def pack_kernel(slots_ref, *refs):
+    left_refs, (own_ref, sib_ref, lr_ref, rc_ref, right) = refs[:-5], refs[-5:]
+    cores, seqs, hid, rows = left_refs[0].shape
+    slots = len(left_refs) * cores
+    for i in range(own_ref.shape[0]):
+        at = slots_ref[i] * cores
+        for t, ref in enumerate((own_ref, sib_ref)):
+            right[pl.ds((at + t) * seqs, seqs)] = ref[i]
+    rt = jnp.concatenate([right[:, d, :] for d in range(hid)], axis=0)
+    rc_ref[...] = rt.T
+    for p, ref in enumerate(left_refs):
+        for t in range(cores):
+            for s in range(seqs):
+                at = (p * cores + t) * seqs + s
+                lr_ref[pl.ds(at, rows, stride=slots * seqs), :] = ref[t, s].T
+
+
+def pack(slots, lefts, own, sib):
+    cores, seqs, hid, rows = lefts[0].shape
+    planes, _, _, cols = own.shape
+    total = planes * cores * seqs
+    return pl.pallas_call(
+        pack_kernel,
+        out_shape=(
+            jax.ShapeDtypeStruct((rows * total, hid), F32),
+            jax.ShapeDtypeStruct((cols, hid * total), F32),
+        ),
+        in_specs=[pl.BlockSpec(memory_space=pltpu.SMEM)]
+        + [pl.BlockSpec(memory_space=pltpu.VMEM)] * (len(lefts) + 2),
+        out_specs=(pl.BlockSpec(memory_space=pltpu.VMEM),) * 2,
+        scratch_shapes=[pltpu.VMEM((total, hid, cols), F32)],
+        compiler_params=PARAMS,
+        name="pack",
+    )(slots, *lefts, own, sib)
+
+
+def after(x, *deps):
+    return lax.optimization_barrier((x, deps))[0]
+
+
+def per_head(
+    parts,
+    homolog_embedding,
+    pair_state,
+    probe_projector,
+    lookup_projector,
+    content_projector,
+    sigmoid_projector,
+    sigmoid_offset,
+    pair_bias_weight,
+    mixing_projector,
+    mixing_offset,
+    first_factor_projector,
+    second_factor_projector,
+    outer_product_weight,
+    outer_product_bias,
+    up_weight,
+    expand_bias,
+    down_weight,
+):
+    seqs, span, ch = homolog_embedding.shape
+    rows, cols, cz = pair_state.shape
+    heads = pair_bias_weight.shape[1]
+    hw = ch // heads
+    hid = first_factor_projector.shape[1]
+    wide = lax.axis_index("wide")
+    n = lax.axis_index("narrow")
+    z, c = wide // CORES, wide % CORES
+    me = n * CORES + c
+    order = jnp.asarray(ORDER, jnp.int32)[z]
+
+    group = 16
+    lane = jnp.arange(heads * group, dtype=jnp.int32) // group
+    own_first = jnp.take(pair_bias_weight, lane ^ me, axis=1)
+    tiles = head_bias(pair_state, own_first, heads)
+    *qkv, gate = head_project(
+        me[None], after(homolog_embedding, tiles[0]), probe_projector, lookup_projector, content_projector,
+        sigmoid_projector, sigmoid_offset, heads,
+    )
+    tiles = after(exchange(tiles, parts), gate)
+    bias = jnp.stack(
+        [jnp.stack([tiles[p * CORES + r] for p in range(parts)]) for r in range(CORES)]
+    )
+    near, second, third = line_gather(bias, parts)
+    qkv = exchange(after(qkv, bias), parts)
+    q, k, v = stage(n[None], after(qkv, near, second[0]), parts)
+    att = jnp.zeros((parts, CORES, seqs, hw, span), F32)
+    bias = after(bias, second[1], third[0])
+    for i, tile in enumerate(((bias,), (near,), second, third)):
+        at = jnp.stack([order[i], order[i] ^ n, c])
+        att = head_attention(at, q, k, v, tile, att, hw)
+    pieces = exchange([att[p, r] for p in range(parts) for r in range(CORES)], parts)
+    alignment_state_next, left_a, left_b, right = head_merge(
+        jnp.stack([me, c]), pieces, gate, homolog_embedding, mixing_projector, mixing_offset,
+        first_factor_projector, second_factor_projector,
+    )
+    turn = lambda z0, c0, n0: (n0, c0, z0)
+    left_a, left_b = send(left_a, parts, turn), send(left_b, parts, turn)
+    sibling = lambda z0, c0, n0: (z0, c0 ^ 1, n0)
+    left = jnp.stack([left_a, send(left_b, parts, sibling)])
+    near, second, third = line_gather(right, parts)
+    lefts = [left] + [
+        send(left, parts, lambda z0, c0, n0, d=d: (z0, c0, n0 ^ d)) for d in range(1, parts)
+    ]
+    own = jnp.stack([right, near, sum(second), sum(third)])
+    left_rows, right_cols = pack(order ^ n, lefts, own, send(own, parts, sibling))
+    pair_state_next = pair_update(
+        left_rows, right_cols, outer_product_weight.reshape(hid, hid * cz), pair_state,
+        outer_product_bias, up_weight, expand_bias, down_weight,
+    )
+    return (alignment_state_next, pair_state_next)
+
+
+def step(mesh, *args):
+    wide, parts = mesh.shape["wide"], mesh.shape["narrow"]
+    heads = args[7].shape[1]
+    if wide == PLANES * CORES and parts == PLANES and heads == CORES * parts:
+        return per_head(parts, *args)
+    return spread_heads(parts, *args)
+
+
 def solution(mesh):
     placed = (P("wide", "narrow", None), P("wide", "narrow", None)) + (P(),) * 15
     return jax.shard_map(
-        functools.partial(per_device, mesh.shape["narrow"]),
+        functools.partial(step, mesh),
         mesh=mesh,
         in_specs=placed,
         out_specs=(P("wide", "narrow", None), P("wide", "narrow", None)),

time: 332 us -> 335 us (level)
  blocking collectives: 70.9 us -> 0 us
  starting transfers between devices: 10.9 us -> 76.9 us
  waiting for transfers between devices: 46.3 us -> 72 us
  Pallas kernels: 175 us -> 163 us
  between operations: 13.8 us -> 3.66 us
  other arithmetic: 0 us -> 8.34 us
    ppermute x0 -> x38, starting transfers between devices: none -> 76.9 us  [send(): return lax.ppermute(x, AXES, pairs)]
    ppermute x0 -> x38, waiting for transfers between devices: none -> 72 us  [send(): return lax.ppermute(x, AXES, pairs)]
    all_to_all x2 -> x0, blocking collectives: 60.3 us -> none  [the longest x1 40.8 us: per_device(): qkv = lax.all_to_all(qkv, 'narrow', 0, 0, tiled=True)]
    all_gather x3 -> x0, waiting for transfers between devices: 23.3 us -> none  [the longest x2 23.3 us: per_device(): lax.all_gather(bias[:, h], 'wide', axis=0, tiled=False)]
    all_to_all x3 -> x0, waiting for transfers between devices: 22.2 us -> none  [the longest x1 15.2 us: per_device(): left = lax.all_to_all(left, 'wide', 0, 0, tiled=True)]
    pallas_call x6 -> x10, Pallas kernels: 175 us -> 163 us  [the longest x1 82.7 us: pair_update(): pl.pallas_call(functools.partial(pair_kernel, step_rows, group, seqs), ou...]
    all_to_all x3 -> x0, starting transfers between devices: 10.8 us -> none  [the longest x2 7.3 us: per_device(): lax.all_to_all(attention(qkv, gathered[h], h, hw), 'narrow', 0, 0, tiled=...]
    all_gather x1 -> x0, blocking collectives: 10.6 us -> none  [per_device(): left = lax.all_gather(left, 'narrow', axis=0, tiled=True)]
  transfers between devices with their start and end apart: 6 -> 38, of which waited for: 3 -> 18; matrix products, arithmetic and copies ran while one was open for 2% -> 3% of each run, Pallas kernels for 13% -> 12%
where the time goes in v2:
time: 335 us; the launch traced here: 334 us
  Pallas kernels  163 us (49%)
  starting transfers between devices  76.9 us (23%)
  waiting for transfers between devices  72 us (21%)
  local copies, waits for them, and re-layouts  10.1 us (3%)
  other arithmetic  8.34 us (2%)
  between operations  3.66 us (1%)
    pallas_call x1, Pallas kernels, pair_update(): pl.pallas_call(functools.partial(pair_kernel, step_rows, group, seqs), ou...  82.7 us
    ppermute x38, starting transfers between devices, send(): return lax.ppermute(x, AXES, pairs)  76.9 us
    ppermute x38, waiting for transfers between devices, send(): return lax.ppermute(x, AXES, pairs)  72 us
    pallas_call x4, Pallas kernels, head_attention(): pl.pallas_call(functools.partial(head_attention_kernel, hw), out_shape=ja...  36.7 us
    pallas_call x1, Pallas kernels, head_bias(): pl.pallas_call(functools.partial(head_bias_kernel, group), out_shape=(jax...  19.5 us
  transfers between devices with their start and end apart: 38, of which 18 were waited for; matrix products, arithmetic and copies ran while one was open for 3% of the time, Pallas kernels for 12%

profile of v2, /device:TPU:0, one launch (start us, length us, event | category | flops | bytes accessed | tf_op | source)
XLA Modules:
  0.0 333.6 jit_solution(17623750177990592721)
XLA Ops:
  2.7 19.5 %head_bias.1 = (f32[128,256]{1,0:T(8,128)}, f32[128,256]{1,0:T(8,128)}, f32[128,256]{1,0:T(8,128)}, f32[128,256]{1,0:T(8,128)}, f32[128,256]{1,0:T(8,128)}, /*in...) custom-call(f32[128,256,128]{2,1,0:T(8,128)} %pair_ref.3, f32[128,128]{1,0:T(8,128)} %select_bitcast_fusion.w_ref), custom_call_target="tpu_custom_call" | custom-call | tf_op jit(solution)/shard_map/head_bias/pallas_call | solution.py:445
  22.8 2.6 collective-permute-start.1
  27.2 2.6 collective-permute-start.5
  32.3 6.5 %head_project.1 = (f32[3,4,32,256]{3,2,1,0:T(8,128)}, f32[3,4,32,256]{3,2,1,0:T(8,128)}, f32[3,4,32,256]{3,2,1,0:T(8,128)}, f32[3,4,32,256]{3,2,1,0:T(8,128)}, f...) custom-call(s32[1]{0:T(128)} %bitcast.me_ref, ...), custom_call_target="tpu_custom_call" | custom-call | tf_op jit(solution)/shard_map/head_project/pallas_call | solution.py:489
  43.0 22.4 %collective-permute-done.14.refs_0_ = f32[2,4,128,256]{3,2,1,0:T(8,128)S(1)} collective-permute-done((f32[2,4,128,256]{3,2,1,0:T(8,128)S(1)}, f32[2,4,128,256]{3,2,1,0:T(8,128)S(1)}, u32[]{:S(2)}, u32[]{:S(2)}) %collective-permute-start.14) | collective-permute-done | bytes 1048608 | tf_op jit(solution)/shard_map/ppermute | solution.py:392
  73.3 8.0 %collective-permute-done.8.refs_2_ = f32[3,4,32,256]{3,2,1,0:T(8,128)} collective-permute-done((f32[3,4,32,256]{3,2,1,0:T(8,128)}, f32[3,4,32,256]{3,2,1,0:T(8,128)}, u32[]{:S(2)}, u32[]{:S(2)}) %collective-permute-start.8) | collective-permute-done | bytes 393248 | tf_op jit(solution)/shard_map/ppermute | solution.py:392
  81.3 7.2 %collective-permute-done.9.refs_3_ = f32[3,4,32,256]{3,2,1,0:T(8,128)} collective-permute-done((f32[3,4,32,256]{3,2,1,0:T(8,128)}, f32[3,4,32,256]{3,2,1,0:T(8,128)}, u32[]{:S(2)}, u32[]{:S(2)}) %collective-permute-start.9) | collective-permute-done | bytes 393248 | tf_op jit(solution)/shard_map/ppermute | solution.py:392
  88.6 2.4 collective-permute-start.12
  99.5 2.3 collective-permute-done.12.refs_6_
  101.8 7.9 %collective-permute-done.13.refs_7_ = f32[3,4,32,256]{3,2,1,0:T(8,128)} collective-permute-done((f32[3,4,32,256]{3,2,1,0:T(8,128)}, f32[3,4,32,256]{3,2,1,0:T(8,128)}, u32[]{:S(2)}, u32[]{:S(2)}) %collective-permute-start.13) | collective-permute-done | bytes 393248 | tf_op jit(solution)/shard_map/ppermute | solution.py:392
  109.6 6.0 %stage.1 = (bf16[2,4,4,256,128]{4,3,2,1,0:T(8,128)(2,1)}, bf16[2,4,128,1024]{3,2,1,0:T(8,128)(2,1)}, bf16[2,4,1024,128]{3,2,1,0:T(8,128)(2,1)}) custom-call(s32[1]{0:T(128)} %bitcast.5.n_ref, f32[3,4,32,256]{3,2,1,0:T(8,128)} %get-tuple-element.88.refs_0_, f32[3,4,32,256]{3,2,1,0:T(8,128)} %copy-done.9, f32[3,4,32,256]{3,2,1,0:T(8,128)} %collective-permute-done.8.refs_2_, ...), custom_call_target="tpu_custom_call" | custom-call | tf_op jit(solution)/shard_map/stage/pallas_call | solution.py:536
  116.7 9.0 %head_attention.4.refs_1_ = f32[4,2,4,32,256]{4,3,2,1,0:T(8,128)} custom-call(s32[3]{0:T(128)} %add_add_fusion.3.at_ref, bf16[2,4,4,256,128]{4,3,2,1,0:T(8,128)(2,1)} %get-tuple-element.96.q_ref, bf16[2,4,128,1024]{3,2,1,0:T(8,128)(2,1)} %get-tuple-element.97.k_ref, ...), custom_call_target="tpu_custom_call", output_to_operand_aliasing={{}: (5, {})} | custom-call | tf_op jit(solution)/shard_map/head_attention/pallas_call | solution.py:580
  125.7 9.0 %head_attention.5.refs_2_ = f32[4,2,4,32,256]{4,3,2,1,0:T(8,128)} custom-call(s32[3]{0:T(128)} %add_add_fusion.2.at_ref, bf16[2,4,4,256,128]{4,3,2,1,0:T(8,128)(2,1)} %get-tuple-element.96.q_ref, bf16[2,4,128,1024]{3,2,1,0:T(8,128)(2,1)} %get-tuple-element.97.k_ref, ...), custom_call_target="tpu_custom_call", output_to_operand_aliasing={{}: (5, {})} | custom-call | tf_op jit(solution)/shard_map/head_attention/pallas_call | solution.py:580
  134.7 9.4 %head_attention.6.refs_2_ = f32[4,2,4,32,256]{4,3,2,1,0:T(8,128)} custom-call(s32[3]{0:T(128)} %get-tuple-element.121.at_ref, bf16[2,4,4,256,128]{4,3,2,1,0:T(8,128)(2,1)} %get-tuple-element.96.q_ref, bf16[2,4,128,1024]{3,2,1,0:T(8,128)(2,1)} %get-tuple-element.97.k_ref, ...), custom_call_target="tpu_custom_call", output_to_operand_aliasing={{}: (6, {})} | custom-call | tf_op jit(solution)/shard_map/head_attention/pallas_call | solution.py:580
  144.1 9.4 %head_attention.7 = f32[4,2,4,32,256]{4,3,2,1,0:T(8,128)} custom-call(s32[3]{0:T(128)} %get-tuple-element.120.at_ref, bf16[2,4,4,256,128]{4,3,2,1,0:T(8,128)(2,1)} %get-tuple-element.96.q_ref, bf16[2,4,128,1024]{3,2,1,0:T(8,128)(2,1)} %get-tuple-element.97.k_ref, bf16[2,4,1024,128]{3,2,1,0:T(8,128)(2,1)} %get-tuple-element.98.v_ref, ...), custom_call_target="tpu_custom_call", output_to_operand_aliasing={{}: (6, {})} | custom-call | tf_op jit(solution)/shard_map/head_attention/pallas_call | solution.py:580
  167.8 2.8 collective-permute-done.22.refs_4_
  171.4 6.5 %head_merge.1 = (f32[4,256,256]{2,1,0:T(8,128)}, f32[4,32,128]{2,1,0:T(8,128)}, f32[4,32,128]{2,1,0:T(8,128)}, f32[4,32,256]{2,1,0:T(8,128)}) custom-call(s32[2]{0:T(128)} %pad_add_fusion.me_ref, f32[4,32,256]{2,1,0:T(8,128)} %get-tuple-element.113.refs_0_, f32[4,32,256]{2,1,0:T(8,128)} %copy-done.17, f32[4,32,256]{2,1,0:T(8,128)} %copy-done.16, ...), custom_call_target="tpu_custom_call" | custom-call | tf_op jit(solution)/shard_map/head_merge/pallas_call | solution.py:640
  177.9 27.1 %collective-permute-start.32 = (f32[4,32,256]{2,1,0:T(8,128)}, f32[4,32,256]{2,1,0:T(8,128)S(1)}, u32[]{:S(2)}, u32[]{:S(2)}) collective-permute-start(f32[4,32,256]{2,1,0:T(8,128)} %get-tuple-element.103), channel_id=1, source_target_pairs={{0,8},{1,9},{2,10},{3,11},{4,12},{5,13},{6,14},{7,15},{8,0},{9,1},... | collective-permute-start | bytes 393224 | tf_op jit(solution)/shard_map/ppermute | solution.py:392
  205.7 3.1 collective-permute-done.32
  212.0 7.1 %collective-permute-done.34 = f32[4,32,256]{2,1,0:T(8,128)S(1)} collective-permute-done((f32[4,32,256]{2,1,0:T(8,128)S(1)}, f32[4,32,256]{2,1,0:T(8,128)S(1)}, u32[]{:S(2)}, u32[]{:S(2)}) %collective-permute-start.34) | collective-permute-done | bytes 131104 | tf_op jit(solution)/shard_map/ppermute | solution.py:392
  219.1 2.4 collective-permute-done.36
  227.0 12.5 %collective-permute-start.31 = (f32[2,4,32,128]{3,2,1,0:T(8,128)S(1)}, f32[2,4,32,128]{3,2,1,0:T(8,128)S(1)}, u32[]{:S(2)}, u32[]{:S(2)}) collective-permute-start(f32[2,4,32,128]{3,2,1,0:T(8,128)S(1)} %pad_maximum_fusion.2.refs_0_), channel_id=1, source_target_pairs={{0,3},{1,2},{2,1},{3,0},{4,7},{5,6},{6,5},{7,4},{8,11},{9,10},{10,... | collective-permute-start | bytes 393224 | tf_op jit(solution)/shard_map/ppermute | solution.py:392
  246.2 4.7 %pack.1 = (f32[4096,32]{1,0:T(8,128)}, f32[256,1024]{1,0:T(8,128)}) custom-call(s32[4]{0:T(128)} %get-tuple-element.114.slots_ref, f32[2,4,32,128]{3,2,1,0:T(8,128)} %copy-done.6, f32[2,4,32,128]{3,2,1,0:T(8,128)} %copy-done.20, f32[2,4,32,128]{3,2,1,0:T(8,128)} %copy-done.19, f32[2,4,32,128]{3,2,1,0:T(8,128)} %copy-done.18, f32[4,4,32,256]{3,2,1,0:T(8,128)} %copy-done.3, ...), custom_call_target="tpu_custom_call" | custom-call | tf_op jit(solution)/shard_map/pack/pallas_call | solution.py:689
  250.9 82.7 %pair_update.1 = f32[128,256,128]{2,1,0:T(8,128)} custom-call(f32[4096,32]{1,0:T(8,128)} %get-tuple-element.104.left_ref, f32[256,1024]{1,0:T(8,128)} %get-tuple-element.105.right_ref, f32[32,4096]{1,0:T(8,128)} %reshape.82.w_ref, f32[128,256,128]{2,1,0:T(8,128)} %pair_ref.3, f32[1,128]{1,0:T(1,128)} %bitcast.76, f32[128,512]{1,0:T(8,128)} %up_ref.1, ...), custom_call_target="tpu_custom_call" | custom-call | tf_op jit(solution)/shard_map/pair_update/pallas_call | solution.py:295
  (136 shorter events, 57.1 us)
Async XLA Ops:
  25.4 13.4 %collective-permute-start.2 = (f32[128,256]{1,0:T(8,128)}, f32[128,256]{1,0:T(8,128)S(1)}, u32[]{:S(2)}, u32[]{:S(2)}) collective-permute-start(f32[128,256]{1,0:T(8,128)} %get-tuple-element.66), channel_id=1, source_target_pairs={{0,5},{1,4},{2,7},{3,6},{4,1},{5,0},{6,3},{7,2},{8,13},{9,12},{10,... | collective-permute-start | bytes 393224 | tf_op jit(solution)/shard_map/ppermute | solution.py:392
  25.4 13.4 %collective-permute-start.3 = (f32[128,256]{1,0:T(8,128)}, f32[128,256]{1,0:T(8,128)S(1)}, u32[]{:S(2)}, u32[]{:S(2)}) collective-permute-start(f32[128,256]{1,0:T(8,128)} %get-tuple-element.67), channel_id=1, source_target_pairs={{0,2},{1,3},{2,0},{3,1},{4,6},{5,7},{6,4},{7,5},{8,10},{9,11},{10,... | collective-permute-start | bytes 393224 | tf_op jit(solution)/shard_map/ppermute | solution.py:392
  27.2 12.0 %collective-permute-start.4 = (f32[128,256]{1,0:T(8,128)}, f32[128,256]{1,0:T(8,128)S(1)}, u32[]{:S(2)}, u32[]{:S(2)}) collective-permute-start(f32[128,256]{1,0:T(8,128)} %get-tuple-element.68), channel_id=1, source_target_pairs={{0,6},{1,7},{2,4},{3,5},{4,2},{5,3},{6,0},{7,1},{8,14},{9,15},{10,... | collective-permute-start | bytes 393224 | tf_op jit(solution)/shard_map/ppermute | solution.py:392
  27.2 12.0 %collective-permute-start.5 = (f32[128,256]{1,0:T(8,128)}, f32[128,256]{1,0:T(8,128)S(1)}, u32[]{:S(2)}, u32[]{:S(2)}) collective-permute-start(f32[128,256]{1,0:T(8,128)} %get-tuple-element.69), channel_id=1, source_target_pairs={{0,3},{1,2},{2,1},{3,0},{4,7},{5,6},{6,5},{7,4},{8,11},{9,10},{10,... | collective-permute-start | bytes 393224 | tf_op jit(solution)/shard_map/ppermute | solution.py:392
  29.9 9.3 %collective-permute-start.6 = (f32[128,256]{1,0:T(8,128)}, f32[128,256]{1,0:T(8,128)S(1)}, u32[]{:S(2)}, u32[]{:S(2)}) collective-permute-start(f32[128,256]{1,0:T(8,128)} %get-tuple-element.70), channel_id=1, source_target_pairs={{0,7},{1,6},{2,5},{3,4},{4,3},{5,2},{6,1},{7,0},{8,15},{9,14},{10,... | collective-permute-start | bytes 393224 | tf_op jit(solution)/shard_map/ppermute | solution.py:392
  39.5 25.9 %collective-permute-start.14 = (f32[2,4,128,256]{3,2,1,0:T(8,128)S(1)}, f32[2,4,128,256]{3,2,1,0:T(8,128)S(1)}, u32[]{:S(2)}, u32[]{:S(2)}) collective-permute-start(f32[2,4,128,256]{3,2,1,0:T(8,128)S(1)} %pad_maximum_fusion.refs_0_), channel_id=1, source_target_pairs={{0,8},{1,9},{2,10},{3,11},{4,12},{5,13},{6,14},{7,15},{8,0},{9,1},... | collective-permute-start | bytes 3145736 | tf_op jit(solution)/shard_map/ppermute | solution.py:392
  41.3 25.0 %collective-permute-start.15 = (f32[2,4,128,256]{3,2,1,0:T(8,128)S(1)}, f32[2,4,128,256]{3,2,1,0:T(8,128)}, u32[]{:S(2)}, u32[]{:S(2)}) collective-permute-start(f32[2,4,128,256]{3,2,1,0:T(8,128)S(1)} %pad_maximum_fusion.refs_0_), channel_id=1, source_target_pairs={{8,16},{9,17},{10,18},{11,19},{12,20},{13,21},{14,22},{15,23},{16,... | collective-permute-start | bytes 3145736 | tf_op jit(solution)/shard_map/ppermute | solution.py:392
  66.3 49.3 %collective-permute-start.18 = (f32[2,4,128,256]{3,2,1,0:T(8,128)}, f32[2,4,128,256]{3,2,1,0:T(8,128)}, u32[]{:S(2)}, u32[]{:S(2)}) collective-permute-start(f32[2,4,128,256]{3,2,1,0:T(8,128)} %collective-permute-done.15.refs_0_), channel_id=1, source_target_pairs={{8,0},{9,1},{10,2},{11,3},{12,4},{13,5},{14,6},{15,7},{16,24},{17,... | collective-permute-start | bytes 3145736 | tf_op jit(solution)/shard_map/ppermute | solution.py:392
  67.6 76.5 %collective-permute-start.17 = (f32[2,4,128,256]{3,2,1,0:T(8,128)S(1)}, f32[2,4,128,256]{3,2,1,0:T(8,128)}, u32[]{:S(2)}, u32[]{:S(2)}) collective-permute-start(f32[2,4,128,256]{3,2,1,0:T(8,128)S(1)} %collective-permute-done.16.refs_0_), channel_id=1, source_target_pairs={{8,0},{9,1},{10,2},{11,3},{12,4},{13,5},{14,6},{15,7},{16,24},{17,... | collective-permute-start | bytes 3145736 | tf_op jit(solution)/shard_map/ppermute | solution.py:392
  68.9 12.4 %collective-permute-start.8 = (f32[3,4,32,256]{3,2,1,0:T(8,128)}, f32[3,4,32,256]{3,2,1,0:T(8,128)}, u32[]{:S(2)}, u32[]{:S(2)}) collective-permute-start(f32[3,4,32,256]{3,2,1,0:T(8,128)} %get-tuple-element.82), channel_id=1, source_target_pairs={{0,1},{1,0},{2,3},{3,2},{4,5},{5,4},{6,7},{7,6},{8,9},{9,8},{10,11... | collective-permute-start | bytes 1179656 | tf_op jit(solution)/shard_map/ppermute | solution.py:392
  70.3 18.3 %collective-permute-start.9 = (f32[3,4,32,256]{3,2,1,0:T(8,128)}, f32[3,4,32,256]{3,2,1,0:T(8,128)}, u32[]{:S(2)}, u32[]{:S(2)}) collective-permute-start(f32[3,4,32,256]{3,2,1,0:T(8,128)} %get-tuple-element.83), channel_id=1, source_target_pairs={{0,5},{1,4},{2,7},{3,6},{4,1},{5,0},{6,3},{7,2},{8,13},{9,12},{10,... | collective-permute-start | bytes 1179656 | tf_op jit(solution)/shard_map/ppermute | solution.py:392
  70.7 20.2 %collective-permute-start.10 = (f32[3,4,32,256]{3,2,1,0:T(8,128)}, f32[3,4,32,256]{3,2,1,0:T(8,128)}, u32[]{:S(2)}, u32[]{:S(2)}) collective-permute-start(f32[3,4,32,256]{3,2,1,0:T(8,128)} %get-tuple-element.84), channel_id=1, source_target_pairs={{0,2},{1,3},{2,0},{3,1},{4,6},{5,7},{6,4},{7,5},{8,10},{9,11},{10,... | collective-permute-start | bytes 1179656 | tf_op jit(solution)/shard_map/ppermute | solution.py:392
  81.3 18.2 %collective-permute-start.11 = (f32[3,4,32,256]{3,2,1,0:T(8,128)}, f32[3,4,32,256]{3,2,1,0:T(8,128)}, u32[]{:S(2)}, u32[]{:S(2)}) collective-permute-start(f32[3,4,32,256]{3,2,1,0:T(8,128)} %get-tuple-element.85), channel_id=1, source_target_pairs={{0,6},{1,7},{2,4},{3,5},{4,2},{5,3},{6,0},{7,1},{8,14},{9,15},{10,... | collective-permute-start | bytes 1179656 | tf_op jit(solution)/shard_map/ppermute | solution.py:392
  88.6 13.2 %collective-permute-start.12 = (f32[3,4,32,256]{3,2,1,0:T(8,128)}, f32[3,4,32,256]{3,2,1,0:T(8,128)}, u32[]{:S(2)}, u32[]{:S(2)}) collective-permute-start(f32[3,4,32,256]{3,2,1,0:T(8,128)} %get-tuple-element.86), channel_id=1, source_target_pairs={{0,3},{1,2},{2,1},{3,0},{4,7},{5,6},{6,5},{7,4},{8,11},{9,10},{10,... | collective-permute-start | bytes 1179656 | tf_op jit(solution)/shard_map/ppermute | solution.py:392
  91.0 18.7 %collective-permute-start.13 = (f32[3,4,32,256]{3,2,1,0:T(8,128)}, f32[3,4,32,256]{3,2,1,0:T(8,128)}, u32[]{:S(2)}, u32[]{:S(2)}) collective-permute-start(f32[3,4,32,256]{3,2,1,0:T(8,128)} %get-tuple-element.87), channel_id=1, source_target_pairs={{0,7},{1,6},{2,5},{3,4},{4,3},{5,2},{6,1},{7,0},{8,15},{9,14},{10,... | collective-permute-start | bytes 1179656 | tf_op jit(solution)/shard_map/ppermute | solution.py:392
  158.1 9.6 %collective-permute-start.23 = (f32[4,32,256]{2,1,0:T(8,128)S(1)}, f32[4,32,256]{2,1,0:T(8,128)S(1)}, u32[]{:S(2)}, u32[]{:S(2)}) collective-permute-start(f32[4,32,256]{2,1,0:T(8,128)S(1)} %get-tuple-element.108), channel_id=1, source_target_pairs={{0,6},{1,7},{2,4},{3,5},{4,2},{5,3},{6,0},{7,1},{8,14},{9,15},{10,... | collective-permute-start | bytes 393224 | tf_op jit(solution)/shard_map/ppermute | solution.py:392
  159.2 11.4 %collective-permute-start.22 = (f32[4,32,256]{2,1,0:T(8,128)S(1)}, f32[4,32,256]{2,1,0:T(8,128)S(1)}, u32[]{:S(2)}, u32[]{:S(2)}) collective-permute-start(f32[4,32,256]{2,1,0:T(8,128)S(1)} %get-tuple-element.109), channel_id=1, source_target_pairs={{0,2},{1,3},{2,0},{3,1},{4,6},{5,7},{6,4},{7,5},{8,10},{9,11},{10,... | collective-permute-start | bytes 393224 | tf_op jit(solution)/shard_map/ppermute | solution.py:392
  159.9 10.7 %collective-permute-start.21 = (f32[4,32,256]{2,1,0:T(8,128)S(1)}, f32[4,32,256]{2,1,0:T(8,128)S(1)}, u32[]{:S(2)}, u32[]{:S(2)}) collective-permute-start(f32[4,32,256]{2,1,0:T(8,128)S(1)} %get-tuple-element.110), channel_id=1, source_target_pairs={{0,5},{1,4},{2,7},{3,6},{4,1},{5,0},{6,3},{7,2},{8,13},{9,12},{10,... | collective-permute-start | bytes 393224 | tf_op jit(solution)/shard_map/ppermute | solution.py:392
  162.0 8.6 %collective-permute-start.20 = (f32[4,32,256]{2,1,0:T(8,128)S(1)}, f32[4,32,256]{2,1,0:T(8,128)S(1)}, u32[]{:S(2)}, u32[]{:S(2)}) collective-permute-start(f32[4,32,256]{2,1,0:T(8,128)S(1)} %get-tuple-element.111), channel_id=1, source_target_pairs={{0,1},{1,0},{2,3},{3,2},{4,5},{5,4},{6,7},{7,6},{8,9},{9,8},{10,11... | collective-permute-start | bytes 393224 | tf_op jit(solution)/shard_map/ppermute | solution.py:392
  177.9 30.8 %collective-permute-start.32 = (f32[4,32,256]{2,1,0:T(8,128)}, f32[4,32,256]{2,1,0:T(8,128)S(1)}, u32[]{:S(2)}, u32[]{:S(2)}) collective-permute-start(f32[4,32,256]{2,1,0:T(8,128)} %get-tuple-element.103), channel_id=1, source_target_pairs={{0,8},{1,9},{2,10},{3,11},{4,12},{5,13},{6,14},{7,15},{8,0},{9,1},... | collective-permute-start | bytes 393224 | tf_op jit(solution)/shard_map/ppermute | solution.py:392
  209.4 9.7 %collective-permute-start.34 = (f32[4,32,256]{2,1,0:T(8,128)S(1)}, f32[4,32,256]{2,1,0:T(8,128)S(1)}, u32[]{:S(2)}, u32[]{:S(2)}) collective-permute-start(f32[4,32,256]{2,1,0:T(8,128)S(1)} %collective-permute-done.33), channel_id=1, source_target_pairs={{8,0},{9,1},{10,2},{11,3},{12,4},{13,5},{14,6},{15,7},{16,24},{17,... | collective-permute-start | bytes 393224 | tf_op jit(solution)/shard_map/ppermute | solution.py:392
  210.7 10.8 %collective-permute-start.36 = (f32[4,32,256]{2,1,0:T(8,128)S(1)}, f32[4,32,256]{2,1,0:T(8,128)S(1)}, u32[]{:S(2)}, u32[]{:S(2)}) collective-permute-start(f32[4,32,256]{2,1,0:T(8,128)S(1)} %collective-permute-done.35), channel_id=1, source_target_pairs={{8,0},{9,1},{10,2},{11,3},{12,4},{13,5},{14,6},{15,7},{16,24},{17,... | collective-permute-start | bytes 393224 | tf_op jit(solution)/shard_map/ppermute | solution.py:392
  222.5 22.8 %collective-permute-start.37 = (f32[4,4,32,256]{3,2,1,0:T(8,128)S(1)}, f32[4,4,32,256]{3,2,1,0:T(8,128)S(1)}, u32[]{:S(2)}, u32[]{:S(2)}) collective-permute-start(f32[4,4,32,256]{3,2,1,0:T(8,128)S(1)} %pad_maximum_fusion.1.refs_4_), channel_id=1, source_target_pairs={{0,4},{1,5},{2,6},{3,7},{4,0},{5,1},{6,2},{7,3},{8,12},{9,13},{10,... | collective-permute-start | bytes 1572872 | tf_op jit(solution)/shard_map/ppermute | solution.py:392
  227.0 15.9 %collective-permute-start.31 = (f32[2,4,32,128]{3,2,1,0:T(8,128)S(1)}, f32[2,4,32,128]{3,2,1,0:T(8,128)S(1)}, u32[]{:S(2)}, u32[]{:S(2)}) collective-permute-start(f32[2,4,32,128]{3,2,1,0:T(8,128)S(1)} %pad_maximum_fusion.2.refs_0_), channel_id=1, source_target_pairs={{0,3},{1,2},{2,1},{3,0},{4,7},{5,6},{6,5},{7,4},{8,11},{9,10},{10,... | collective-permute-start | bytes 393224 | tf_op jit(solution)/shard_map/ppermute | solution.py:392
  (39 other events, 593.7 us)

commit v3 on v2

--- a/solution.py
+++ b/solution.py
@@ -8,6 +8,7 @@
 from jax.experimental.pallas import tpu as pltpu
 from jax.sharding import PartitionSpec as P
 
+
 F32, BF16 = jnp.float32, jnp.bfloat16
 PARAMS = pltpu.CompilerParams(vmem_limit_bytes=60 * 2**20)
 
@@ -38,7 +39,7 @@
 
 
 def bias_kernel(pair_ref, w_ref, out_ref):
-    rows, cols, cz = pair_ref.shape
+    rows, _, _ = pair_ref.shape
     heads = w_ref.shape[1]
     wh, wl = split(w_ref[...].T)
     lhs = jnp.concatenate(
@@ -142,8 +143,8 @@
 
 
 def attention(qkv, bias, head, hw):
-    parts, _, seqs, own, span = qkv.shape
-    wide, _, rows, _ = bias.shape
+    parts, _, seqs, _, span = qkv.shape
+    _, _, rows, _ = bias.shape
     per = span // rows
     return pl.pallas_call(
         functools.partial(attention_kernel, hw),
@@ -169,8 +170,7 @@
     heads = len(refs) - 12
     att = refs[:heads]
     gate_ref, x_ref, wm_ref, bm_ref, f1_ref, f2_ref, next_ref, left_ref, right_ref, m_hi, m_lo, f_st = refs[heads:]
-    parts, _, hw, span = att[0].shape
-    ch = x_ref.shape[-1]
+    parts, _, _, _ = att[0].shape
     hid = f1_ref.shape[1]
     blocks, _, _, rows = left_ref.shape
 
@@ -335,7 +335,7 @@
     expand_bias,
     down_weight,
 ):
-    seqs, span, ch = homolog_embedding.shape
+    _, _, ch = homolog_embedding.shape
     rows, cols, cz = pair_state.shape
     heads = pair_bias_weight.shape[1]
     hw = ch // heads
@@ -412,7 +412,7 @@
 
 def head_bias_kernel(group, pair_ref, w_ref, *refs):
     out_refs, w_st = refs[:-1], refs[-1]
-    rows, cols, cz = pair_ref.shape
+    rows, _, cz = pair_ref.shape
     heads = len(out_refs)
     lanes = heads * group
 
@@ -557,7 +557,7 @@
 
 def head_attention_kernel(hw, at_ref, q_ref, k_ref, v_ref, *refs):
     bias_refs, out_ref = refs[:-2], refs[-1]
-    _, parts, rows, _ = bias_refs[0].shape
+    _, parts, _, _ = bias_refs[0].shape
     cores, seqs = q_ref.shape[:2]
     bias = jnp.concatenate(
         [
@@ -726,7 +726,7 @@
     down_weight,
 ):
     seqs, span, ch = homolog_embedding.shape
-    rows, cols, cz = pair_state.shape
+    _, _, cz = pair_state.shape
     heads = pair_bias_weight.shape[1]
     hw = ch // heads
     hid = first_factor_projector.shape[1]
@@ -762,13 +762,11 @@
         first_factor_projector, second_factor_projector,
     )
     turn = lambda z0, c0, n0: (n0, c0, z0)
-    left_a, left_b = send(left_a, parts, turn), send(left_b, parts, turn)
+    left_b, left_a = send(left_b, parts, turn), send(left_a, parts, turn)
     sibling = lambda z0, c0, n0: (z0, c0 ^ 1, n0)
     left = jnp.stack([left_a, send(left_b, parts, sibling)])
     near, second, third = line_gather(right, parts)
-    lefts = [left] + [
-        send(left, parts, lambda z0, c0, n0, d=d: (z0, c0, n0 ^ d)) for d in range(1, parts)
-    ]
+    lefts = [left] + [send(left, parts, lambda z0, c0, n0, d=d: (z0, c0, n0 ^ d)) for d in range(1, parts)]
     own = jnp.stack([right, near, sum(second), sum(third)])
     left_rows, right_cols = pack(order ^ n, lefts, own, send(own, parts, sibling))
     pair_state_next = pair_update(
@@ -778,10 +776,14 @@
     return (alignment_state_next, pair_state_next)
 
 
+def lines(mesh):
+    return mesh.shape["wide"] == PLANES * CORES and mesh.shape["narrow"] == PLANES
+
+
 def step(mesh, *args):
-    wide, parts = mesh.shape["wide"], mesh.shape["narrow"]
+    parts = mesh.shape["narrow"]
     heads = args[7].shape[1]
-    if wide == PLANES * CORES and parts == PLANES and heads == CORES * parts:
+    if lines(mesh) and heads == CORES * parts:
         return per_head(parts, *args)
     return spread_heads(parts, *args)
 

time: 335 us -> 335 us (level)
  no operation moved by 1% of the time
where the time goes in v3:
time: 335 us; the launch traced here: 334 us
  Pallas kernels  163 us (49%)
  starting transfers between devices  76.9 us (23%)
  waiting for transfers between devices  72 us (21%)
  local copies, waits for them, and re-layouts  10.1 us (3%)
  other arithmetic  8.34 us (2%)
  between operations  3.66 us (1%)
    pallas_call x1, Pallas kernels, pair_update(): pl.pallas_call(functools.partial(pair_kernel, step_rows, group, seqs), ou...  82.7 us
    ppermute x38, starting transfers between devices, send(): return lax.ppermute(x, AXES, pairs)  76.9 us
    ppermute x38, waiting for transfers between devices, send(): return lax.ppermute(x, AXES, pairs)  72 us
    pallas_call x4, Pallas kernels, head_attention(): pl.pallas_call(functools.partial(head_attention_kernel, hw), out_shape=ja...  36.7 us
    pallas_call x1, Pallas kernels, head_bias(): pl.pallas_call(functools.partial(head_bias_kernel, group), out_shape=(jax...  19.5 us
  transfers between devices with their start and end apart: 38, of which 18 were waited for; matrix products, arithmetic and copies ran while one was open for 3% of the time, Pallas kernels for 12%

profile of v3, /device:TPU:0, one launch (start us, length us, event | category | flops | bytes accessed | tf_op | source)
XLA Modules:
  0.0 333.6 jit_solution(17623750177990592721)
XLA Ops:
  2.7 19.5 %head_bias.1 = (f32[128,256]{1,0:T(8,128)}, f32[128,256]{1,0:T(8,128)}, f32[128,256]{1,0:T(8,128)}, f32[128,256]{1,0:T(8,128)}, f32[128,256]{1,0:T(8,128)}, /*in...) custom-call(f32[128,256,128]{2,1,0:T(8,128)} %pair_ref.3, f32[128,128]{1,0:T(8,128)} %select_bitcast_fusion.w_ref), custom_call_target="tpu_custom_call" | custom-call | tf_op jit(solution)/shard_map/head_bias/pallas_call | solution.py:445
  22.8 2.6 collective-permute-start.1
  27.2 2.6 collective-permute-start.5
  32.3 6.5 %head_project.1 = (f32[3,4,32,256]{3,2,1,0:T(8,128)}, f32[3,4,32,256]{3,2,1,0:T(8,128)}, f32[3,4,32,256]{3,2,1,0:T(8,128)}, f32[3,4,32,256]{3,2,1,0:T(8,128)}, f...) custom-call(s32[1]{0:T(128)} %bitcast.me_ref, ...), custom_call_target="tpu_custom_call" | custom-call | tf_op jit(solution)/shard_map/head_project/pallas_call | solution.py:489
  43.0 22.4 %collective-permute-done.14.refs_0_ = f32[2,4,128,256]{3,2,1,0:T(8,128)S(1)} collective-permute-done((f32[2,4,128,256]{3,2,1,0:T(8,128)S(1)}, f32[2,4,128,256]{3,2,1,0:T(8,128)S(1)}, u32[]{:S(2)}, u32[]{:S(2)}) %collective-permute-start.14) | collective-permute-done | bytes 1048608 | tf_op jit(solution)/shard_map/ppermute | solution.py:392
  73.3 8.0 %collective-permute-done.8.refs_2_ = f32[3,4,32,256]{3,2,1,0:T(8,128)} collective-permute-done((f32[3,4,32,256]{3,2,1,0:T(8,128)}, f32[3,4,32,256]{3,2,1,0:T(8,128)}, u32[]{:S(2)}, u32[]{:S(2)}) %collective-permute-start.8) | collective-permute-done | bytes 393248 | tf_op jit(solution)/shard_map/ppermute | solution.py:392
  81.3 7.2 %collective-permute-done.9.refs_3_ = f32[3,4,32,256]{3,2,1,0:T(8,128)} collective-permute-done((f32[3,4,32,256]{3,2,1,0:T(8,128)}, f32[3,4,32,256]{3,2,1,0:T(8,128)}, u32[]{:S(2)}, u32[]{:S(2)}) %collective-permute-start.9) | collective-permute-done | bytes 393248 | tf_op jit(solution)/shard_map/ppermute | solution.py:392
  88.6 2.4 collective-permute-start.12
  99.5 2.3 collective-permute-done.12.refs_6_
  101.8 7.9 %collective-permute-done.13.refs_7_ = f32[3,4,32,256]{3,2,1,0:T(8,128)} collective-permute-done((f32[3,4,32,256]{3,2,1,0:T(8,128)}, f32[3,4,32,256]{3,2,1,0:T(8,128)}, u32[]{:S(2)}, u32[]{:S(2)}) %collective-permute-start.13) | collective-permute-done | bytes 393248 | tf_op jit(solution)/shard_map/ppermute | solution.py:392
  109.6 6.0 %stage.1 = (bf16[2,4,4,256,128]{4,3,2,1,0:T(8,128)(2,1)}, bf16[2,4,128,1024]{3,2,1,0:T(8,128)(2,1)}, bf16[2,4,1024,128]{3,2,1,0:T(8,128)(2,1)}) custom-call(s32[1]{0:T(128)} %bitcast.5.n_ref, f32[3,4,32,256]{3,2,1,0:T(8,128)} %get-tuple-element.88.refs_0_, f32[3,4,32,256]{3,2,1,0:T(8,128)} %copy-done.9, f32[3,4,32,256]{3,2,1,0:T(8,128)} %collective-permute-done.8.refs_2_, ...), custom_call_target="tpu_custom_call" | custom-call | tf_op jit(solution)/shard_map/stage/pallas_call | solution.py:536
  116.7 9.0 %head_attention.4.refs_1_ = f32[4,2,4,32,256]{4,3,2,1,0:T(8,128)} custom-call(s32[3]{0:T(128)} %add_add_fusion.3.at_ref, bf16[2,4,4,256,128]{4,3,2,1,0:T(8,128)(2,1)} %get-tuple-element.96.q_ref, bf16[2,4,128,1024]{3,2,1,0:T(8,128)(2,1)} %get-tuple-element.97.k_ref, ...), custom_call_target="tpu_custom_call", output_to_operand_aliasing={{}: (5, {})} | custom-call | tf_op jit(solution)/shard_map/head_attention/pallas_call | solution.py:580
  125.7 9.0 %head_attention.5.refs_2_ = f32[4,2,4,32,256]{4,3,2,1,0:T(8,128)} custom-call(s32[3]{0:T(128)} %add_add_fusion.2.at_ref, bf16[2,4,4,256,128]{4,3,2,1,0:T(8,128)(2,1)} %get-tuple-element.96.q_ref, bf16[2,4,128,1024]{3,2,1,0:T(8,128)(2,1)} %get-tuple-element.97.k_ref, ...), custom_call_target="tpu_custom_call", output_to_operand_aliasing={{}: (5, {})} | custom-call | tf_op jit(solution)/shard_map/head_attention/pallas_call | solution.py:580
  134.7 9.4 %head_attention.6.refs_2_ = f32[4,2,4,32,256]{4,3,2,1,0:T(8,128)} custom-call(s32[3]{0:T(128)} %get-tuple-element.121.at_ref, bf16[2,4,4,256,128]{4,3,2,1,0:T(8,128)(2,1)} %get-tuple-element.96.q_ref, bf16[2,4,128,1024]{3,2,1,0:T(8,128)(2,1)} %get-tuple-element.97.k_ref, ...), custom_call_target="tpu_custom_call", output_to_operand_aliasing={{}: (6, {})} | custom-call | tf_op jit(solution)/shard_map/head_attention/pallas_call | solution.py:580
  144.1 9.4 %head_attention.7 = f32[4,2,4,32,256]{4,3,2,1,0:T(8,128)} custom-call(s32[3]{0:T(128)} %get-tuple-element.120.at_ref, bf16[2,4,4,256,128]{4,3,2,1,0:T(8,128)(2,1)} %get-tuple-element.96.q_ref, bf16[2,4,128,1024]{3,2,1,0:T(8,128)(2,1)} %get-tuple-element.97.k_ref, bf16[2,4,1024,128]{3,2,1,0:T(8,128)(2,1)} %get-tuple-element.98.v_ref, ...), custom_call_target="tpu_custom_call", output_to_operand_aliasing={{}: (6, {})} | custom-call | tf_op jit(solution)/shard_map/head_attention/pallas_call | solution.py:580
  167.8 2.8 collective-permute-done.22.refs_4_
  171.4 6.5 %head_merge.1 = (f32[4,256,256]{2,1,0:T(8,128)}, f32[4,32,128]{2,1,0:T(8,128)}, f32[4,32,128]{2,1,0:T(8,128)}, f32[4,32,256]{2,1,0:T(8,128)}) custom-call(s32[2]{0:T(128)} %pad_add_fusion.me_ref, f32[4,32,256]{2,1,0:T(8,128)} %get-tuple-element.113.refs_0_, f32[4,32,256]{2,1,0:T(8,128)} %copy-done.17, f32[4,32,256]{2,1,0:T(8,128)} %copy-done.16, ...), custom_call_target="tpu_custom_call" | custom-call | tf_op jit(solution)/shard_map/head_merge/pallas_call | solution.py:640
  177.9 27.1 %collective-permute-start.32 = (f32[4,32,256]{2,1,0:T(8,128)}, f32[4,32,256]{2,1,0:T(8,128)S(1)}, u32[]{:S(2)}, u32[]{:S(2)}) collective-permute-start(f32[4,32,256]{2,1,0:T(8,128)} %get-tuple-element.103), channel_id=1, source_target_pairs={{0,8},{1,9},{2,10},{3,11},{4,12},{5,13},{6,14},{7,15},{8,0},{9,1},... | collective-permute-start | bytes 393224 | tf_op jit(solution)/shard_map/ppermute | solution.py:392
  205.7 3.1 collective-permute-done.32
  212.0 7.1 %collective-permute-done.34 = f32[4,32,256]{2,1,0:T(8,128)S(1)} collective-permute-done((f32[4,32,256]{2,1,0:T(8,128)S(1)}, f32[4,32,256]{2,1,0:T(8,128)S(1)}, u32[]{:S(2)}, u32[]{:S(2)}) %collective-permute-start.34) | collective-permute-done | bytes 131104 | tf_op jit(solution)/shard_map/ppermute | solution.py:392
  219.1 2.4 collective-permute-done.36
  227.0 12.5 %collective-permute-start.31 = (f32[2,4,32,128]{3,2,1,0:T(8,128)S(1)}, f32[2,4,32,128]{3,2,1,0:T(8,128)S(1)}, u32[]{:S(2)}, u32[]{:S(2)}) collective-permute-start(f32[2,4,32,128]{3,2,1,0:T(8,128)S(1)} %pad_maximum_fusion.2.refs_0_), channel_id=1, source_target_pairs={{0,3},{1,2},{2,1},{3,0},{4,7},{5,6},{6,5},{7,4},{8,11},{9,10},{10,... | collective-permute-start | bytes 393224 | tf_op jit(solution)/shard_map/ppermute | solution.py:392
  246.2 4.7 %pack.1 = (f32[4096,32]{1,0:T(8,128)}, f32[256,1024]{1,0:T(8,128)}) custom-call(s32[4]{0:T(128)} %get-tuple-element.114.slots_ref, f32[2,4,32,128]{3,2,1,0:T(8,128)} %copy-done.6, f32[2,4,32,128]{3,2,1,0:T(8,128)} %copy-done.20, f32[2,4,32,128]{3,2,1,0:T(8,128)} %copy-done.19, f32[2,4,32,128]{3,2,1,0:T(8,128)} %copy-done.18, f32[4,4,32,256]{3,2,1,0:T(8,128)} %copy-done.3, ...), custom_call_target="tpu_custom_call" | custom-call | tf_op jit(solution)/shard_map/pack/pallas_call | solution.py:689
  250.9 82.7 %pair_update.1 = f32[128,256,128]{2,1,0:T(8,128)} custom-call(f32[4096,32]{1,0:T(8,128)} %get-tuple-element.104.left_ref, f32[256,1024]{1,0:T(8,128)} %get-tuple-element.105.right_ref, f32[32,4096]{1,0:T(8,128)} %reshape.82.w_ref, f32[128,256,128]{2,1,0:T(8,128)} %pair_ref.3, f32[1,128]{1,0:T(1,128)} %bitcast.76, f32[128,512]{1,0:T(8,128)} %up_ref.1, ...), custom_call_target="tpu_custom_call" | custom-call | tf_op jit(solution)/shard_map/pair_update/pallas_call | solution.py:295
  (136 shorter events, 57.1 us)
Async XLA Ops:
  25.4 13.4 %collective-permute-start.2 = (f32[128,256]{1,0:T(8,128)}, f32[128,256]{1,0:T(8,128)S(1)}, u32[]{:S(2)}, u32[]{:S(2)}) collective-permute-start(f32[128,256]{1,0:T(8,128)} %get-tuple-element.66), channel_id=1, source_target_pairs={{0,5},{1,4},{2,7},{3,6},{4,1},{5,0},{6,3},{7,2},{8,13},{9,12},{10,... | collective-permute-start | bytes 393224 | tf_op jit(solution)/shard_map/ppermute | solution.py:392
  25.4 13.4 %collective-permute-start.3 = (f32[128,256]{1,0:T(8,128)}, f32[128,256]{1,0:T(8,128)S(1)}, u32[]{:S(2)}, u32[]{:S(2)}) collective-permute-start(f32[128,256]{1,0:T(8,128)} %get-tuple-element.67), channel_id=1, source_target_pairs={{0,2},{1,3},{2,0},{3,1},{4,6},{5,7},{6,4},{7,5},{8,10},{9,11},{10,... | collective-permute-start | bytes 393224 | tf_op jit(solution)/shard_map/ppermute | solution.py:392
  27.2 12.0 %collective-permute-start.4 = (f32[128,256]{1,0:T(8,128)}, f32[128,256]{1,0:T(8,128)S(1)}, u32[]{:S(2)}, u32[]{:S(2)}) collective-permute-start(f32[128,256]{1,0:T(8,128)} %get-tuple-element.68), channel_id=1, source_target_pairs={{0,6},{1,7},{2,4},{3,5},{4,2},{5,3},{6,0},{7,1},{8,14},{9,15},{10,... | collective-permute-start | bytes 393224 | tf_op jit(solution)/shard_map/ppermute | solution.py:392
  27.2 12.0 %collective-permute-start.5 = (f32[128,256]{1,0:T(8,128)}, f32[128,256]{1,0:T(8,128)S(1)}, u32[]{:S(2)}, u32[]{:S(2)}) collective-permute-start(f32[128,256]{1,0:T(8,128)} %get-tuple-element.69), channel_id=1, source_target_pairs={{0,3},{1,2},{2,1},{3,0},{4,7},{5,6},{6,5},{7,4},{8,11},{9,10},{10,... | collective-permute-start | bytes 393224 | tf_op jit(solution)/shard_map/ppermute | solution.py:392
  29.9 9.3 %collective-permute-start.6 = (f32[128,256]{1,0:T(8,128)}, f32[128,256]{1,0:T(8,128)S(1)}, u32[]{:S(2)}, u32[]{:S(2)}) collective-permute-start(f32[128,256]{1,0:T(8,128)} %get-tuple-element.70), channel_id=1, source_target_pairs={{0,7},{1,6},{2,5},{3,4},{4,3},{5,2},{6,1},{7,0},{8,15},{9,14},{10,... | collective-permute-start | bytes 393224 | tf_op jit(solution)/shard_map/ppermute | solution.py:392
  39.5 25.9 %collective-permute-start.14 = (f32[2,4,128,256]{3,2,1,0:T(8,128)S(1)}, f32[2,4,128,256]{3,2,1,0:T(8,128)S(1)}, u32[]{:S(2)}, u32[]{:S(2)}) collective-permute-start(f32[2,4,128,256]{3,2,1,0:T(8,128)S(1)} %pad_maximum_fusion.refs_0_), channel_id=1, source_target_pairs={{0,8},{1,9},{2,10},{3,11},{4,12},{5,13},{6,14},{7,15},{8,0},{9,1},... | collective-permute-start | bytes 3145736 | tf_op jit(solution)/shard_map/ppermute | solution.py:392
  41.3 25.0 %collective-permute-start.15 = (f32[2,4,128,256]{3,2,1,0:T(8,128)S(1)}, f32[2,4,128,256]{3,2,1,0:T(8,128)}, u32[]{:S(2)}, u32[]{:S(2)}) collective-permute-start(f32[2,4,128,256]{3,2,1,0:T(8,128)S(1)} %pad_maximum_fusion.refs_0_), channel_id=1, source_target_pairs={{8,16},{9,17},{10,18},{11,19},{12,20},{13,21},{14,22},{15,23},{16,... | collective-permute-start | bytes 3145736 | tf_op jit(solution)/shard_map/ppermute | solution.py:392
  66.3 49.3 %collective-permute-start.18 = (f32[2,4,128,256]{3,2,1,0:T(8,128)}, f32[2,4,128,256]{3,2,1,0:T(8,128)}, u32[]{:S(2)}, u32[]{:S(2)}) collective-permute-start(f32[2,4,128,256]{3,2,1,0:T(8,128)} %collective-permute-done.15.refs_0_), channel_id=1, source_target_pairs={{8,0},{9,1},{10,2},{11,3},{12,4},{13,5},{14,6},{15,7},{16,24},{17,... | collective-permute-start | bytes 3145736 | tf_op jit(solution)/shard_map/ppermute | solution.py:392
  67.6 76.5 %collective-permute-start.17 = (f32[2,4,128,256]{3,2,1,0:T(8,128)S(1)}, f32[2,4,128,256]{3,2,1,0:T(8,128)}, u32[]{:S(2)}, u32[]{:S(2)}) collective-permute-start(f32[2,4,128,256]{3,2,1,0:T(8,128)S(1)} %collective-permute-done.16.refs_0_), channel_id=1, source_target_pairs={{8,0},{9,1},{10,2},{11,3},{12,4},{13,5},{14,6},{15,7},{16,24},{17,... | collective-permute-start | bytes 3145736 | tf_op jit(solution)/shard_map/ppermute | solution.py:392
  68.9 12.4 %collective-permute-start.8 = (f32[3,4,32,256]{3,2,1,0:T(8,128)}, f32[3,4,32,256]{3,2,1,0:T(8,128)}, u32[]{:S(2)}, u32[]{:S(2)}) collective-permute-start(f32[3,4,32,256]{3,2,1,0:T(8,128)} %get-tuple-element.82), channel_id=1, source_target_pairs={{0,1},{1,0},{2,3},{3,2},{4,5},{5,4},{6,7},{7,6},{8,9},{9,8},{10,11... | collective-permute-start | bytes 1179656 | tf_op jit(solution)/shard_map/ppermute | solution.py:392
  70.3 18.3 %collective-permute-start.9 = (f32[3,4,32,256]{3,2,1,0:T(8,128)}, f32[3,4,32,256]{3,2,1,0:T(8,128)}, u32[]{:S(2)}, u32[]{:S(2)}) collective-permute-start(f32[3,4,32,256]{3,2,1,0:T(8,128)} %get-tuple-element.83), channel_id=1, source_target_pairs={{0,5},{1,4},{2,7},{3,6},{4,1},{5,0},{6,3},{7,2},{8,13},{9,12},{10,... | collective-permute-start | bytes 1179656 | tf_op jit(solution)/shard_map/ppermute | solution.py:392
  70.7 20.2 %collective-permute-start.10 = (f32[3,4,32,256]{3,2,1,0:T(8,128)}, f32[3,4,32,256]{3,2,1,0:T(8,128)}, u32[]{:S(2)}, u32[]{:S(2)}) collective-permute-start(f32[3,4,32,256]{3,2,1,0:T(8,128)} %get-tuple-element.84), channel_id=1, source_target_pairs={{0,2},{1,3},{2,0},{3,1},{4,6},{5,7},{6,4},{7,5},{8,10},{9,11},{10,... | collective-permute-start | bytes 1179656 | tf_op jit(solution)/shard_map/ppermute | solution.py:392
  81.3 18.2 %collective-permute-start.11 = (f32[3,4,32,256]{3,2,1,0:T(8,128)}, f32[3,4,32,256]{3,2,1,0:T(8,128)}, u32[]{:S(2)}, u32[]{:S(2)}) collective-permute-start(f32[3,4,32,256]{3,2,1,0:T(8,128)} %get-tuple-element.85), channel_id=1, source_target_pairs={{0,6},{1,7},{2,4},{3,5},{4,2},{5,3},{6,0},{7,1},{8,14},{9,15},{10,... | collective-permute-start | bytes 1179656 | tf_op jit(solution)/shard_map/ppermute | solution.py:392
  88.6 13.2 %collective-permute-start.12 = (f32[3,4,32,256]{3,2,1,0:T(8,128)}, f32[3,4,32,256]{3,2,1,0:T(8,128)}, u32[]{:S(2)}, u32[]{:S(2)}) collective-permute-start(f32[3,4,32,256]{3,2,1,0:T(8,128)} %get-tuple-element.86), channel_id=1, source_target_pairs={{0,3},{1,2},{2,1},{3,0},{4,7},{5,6},{6,5},{7,4},{8,11},{9,10},{10,... | collective-permute-start | bytes 1179656 | tf_op jit(solution)/shard_map/ppermute | solution.py:392
  91.0 18.7 %collective-permute-start.13 = (f32[3,4,32,256]{3,2,1,0:T(8,128)}, f32[3,4,32,256]{3,2,1,0:T(8,128)}, u32[]{:S(2)}, u32[]{:S(2)}) collective-permute-start(f32[3,4,32,256]{3,2,1,0:T(8,128)} %get-tuple-element.87), channel_id=1, source_target_pairs={{0,7},{1,6},{2,5},{3,4},{4,3},{5,2},{6,1},{7,0},{8,15},{9,14},{10,... | collective-permute-start | bytes 1179656 | tf_op jit(solution)/shard_map/ppermute | solution.py:392
  158.1 9.6 %collective-permute-start.23 = (f32[4,32,256]{2,1,0:T(8,128)S(1)}, f32[4,32,256]{2,1,0:T(8,128)S(1)}, u32[]{:S(2)}, u32[]{:S(2)}) collective-permute-start(f32[4,32,256]{2,1,0:T(8,128)S(1)} %get-tuple-element.108), channel_id=1, source_target_pairs={{0,6},{1,7},{2,4},{3,5},{4,2},{5,3},{6,0},{7,1},{8,14},{9,15},{10,... | collective-permute-start | bytes 393224 | tf_op jit(solution)/shard_map/ppermute | solution.py:392
  159.2 11.4 %collective-permute-start.22 = (f32[4,32,256]{2,1,0:T(8,128)S(1)}, f32[4,32,256]{2,1,0:T(8,128)S(1)}, u32[]{:S(2)}, u32[]{:S(2)}) collective-permute-start(f32[4,32,256]{2,1,0:T(8,128)S(1)} %get-tuple-element.109), channel_id=1, source_target_pairs={{0,2},{1,3},{2,0},{3,1},{4,6},{5,7},{6,4},{7,5},{8,10},{9,11},{10,... | collective-permute-start | bytes 393224 | tf_op jit(solution)/shard_map/ppermute | solution.py:392
  159.9 10.7 %collective-permute-start.21 = (f32[4,32,256]{2,1,0:T(8,128)S(1)}, f32[4,32,256]{2,1,0:T(8,128)S(1)}, u32[]{:S(2)}, u32[]{:S(2)}) collective-permute-start(f32[4,32,256]{2,1,0:T(8,128)S(1)} %get-tuple-element.110), channel_id=1, source_target_pairs={{0,5},{1,4},{2,7},{3,6},{4,1},{5,0},{6,3},{7,2},{8,13},{9,12},{10,... | collective-permute-start | bytes 393224 | tf_op jit(solution)/shard_map/ppermute | solution.py:392
  162.0 8.6 %collective-permute-start.20 = (f32[4,32,256]{2,1,0:T(8,128)S(1)}, f32[4,32,256]{2,1,0:T(8,128)S(1)}, u32[]{:S(2)}, u32[]{:S(2)}) collective-permute-start(f32[4,32,256]{2,1,0:T(8,128)S(1)} %get-tuple-element.111), channel_id=1, source_target_pairs={{0,1},{1,0},{2,3},{3,2},{4,5},{5,4},{6,7},{7,6},{8,9},{9,8},{10,11... | collective-permute-start | bytes 393224 | tf_op jit(solution)/shard_map/ppermute | solution.py:392
  177.9 30.8 %collective-permute-start.32 = (f32[4,32,256]{2,1,0:T(8,128)}, f32[4,32,256]{2,1,0:T(8,128)S(1)}, u32[]{:S(2)}, u32[]{:S(2)}) collective-permute-start(f32[4,32,256]{2,1,0:T(8,128)} %get-tuple-element.103), channel_id=1, source_target_pairs={{0,8},{1,9},{2,10},{3,11},{4,12},{5,13},{6,14},{7,15},{8,0},{9,1},... | collective-permute-start | bytes 393224 | tf_op jit(solution)/shard_map/ppermute | solution.py:392
  209.4 9.7 %collective-permute-start.34 = (f32[4,32,256]{2,1,0:T(8,128)S(1)}, f32[4,32,256]{2,1,0:T(8,128)S(1)}, u32[]{:S(2)}, u32[]{:S(2)}) collective-permute-start(f32[4,32,256]{2,1,0:T(8,128)S(1)} %collective-permute-done.33), channel_id=1, source_target_pairs={{8,0},{9,1},{10,2},{11,3},{12,4},{13,5},{14,6},{15,7},{16,24},{17,... | collective-permute-start | bytes 393224 | tf_op jit(solution)/shard_map/ppermute | solution.py:392
  210.7 10.8 %collective-permute-start.36 = (f32[4,32,256]{2,1,0:T(8,128)S(1)}, f32[4,32,256]{2,1,0:T(8,128)S(1)}, u32[]{:S(2)}, u32[]{:S(2)}) collective-permute-start(f32[4,32,256]{2,1,0:T(8,128)S(1)} %collective-permute-done.35), channel_id=1, source_target_pairs={{8,0},{9,1},{10,2},{11,3},{12,4},{13,5},{14,6},{15,7},{16,24},{17,... | collective-permute-start | bytes 393224 | tf_op jit(solution)/shard_map/ppermute | solution.py:392
  222.5 22.8 %collective-permute-start.37 = (f32[4,4,32,256]{3,2,1,0:T(8,128)S(1)}, f32[4,4,32,256]{3,2,1,0:T(8,128)S(1)}, u32[]{:S(2)}, u32[]{:S(2)}) collective-permute-start(f32[4,4,32,256]{3,2,1,0:T(8,128)S(1)} %pad_maximum_fusion.1.refs_4_), channel_id=1, source_target_pairs={{0,4},{1,5},{2,6},{3,7},{4,0},{5,1},{6,2},{7,3},{8,12},{9,13},{10,... | collective-permute-start | bytes 1572872 | tf_op jit(solution)/shard_map/ppermute | solution.py:392
  227.0 15.9 %collective-permute-start.31 = (f32[2,4,32,128]{3,2,1,0:T(8,128)S(1)}, f32[2,4,32,128]{3,2,1,0:T(8,128)S(1)}, u32[]{:S(2)}, u32[]{:S(2)}) collective-permute-start(f32[2,4,32,128]{3,2,1,0:T(8,128)S(1)} %pad_maximum_fusion.2.refs_0_), channel_id=1, source_target_pairs={{0,3},{1,2},{2,1},{3,0},{4,7},{5,6},{6,5},{7,4},{8,11},{9,10},{10,... | collective-permute-start | bytes 393224 | tf_op jit(solution)/shard_map/ppermute | solution.py:392
  (39 other events, 593.7 us)

commit v4 on v3

--- a/solution.py
+++ b/solution.py
@@ -410,45 +410,31 @@
     return near, (across, out2), (far, out3)
 
 
-def head_bias_kernel(group, pair_ref, w_ref, *refs):
-    out_refs, w_st = refs[:-1], refs[-1]
-    rows, _, cz = pair_ref.shape
-    heads = len(out_refs)
-    lanes = heads * group
-
-    @pl.when(pl.program_id(0) == 0)
-    def _():
-        w = w_ref[...]
-        hi = w.astype(BF16).astype(F32)
-        row_of = lax.broadcasted_iota(jnp.int32, w.shape, 1) % group
-        for i in range(group):
-            h = jnp.where(row_of == i, hi, 0.0).astype(BF16)
-            l = jnp.where(row_of == i, w - hi, 0.0).astype(BF16)
-            for t in range(2):
-                w_st[i, t * cz:(t + 1) * cz, 0:lanes] = h
-                w_st[i, t * cz:(t + 1) * cz, lanes:2 * lanes] = l
-
-    for g in range(0, rows, group):
-        ys = []
-        for i in range(group):
-            yh, yl = split(norm_rows(pair_ref[g + i]))
-            ys += [yh, yl]
-        r = mm(jnp.concatenate(ys, axis=1), w_st[...].reshape(group * 2 * cz, 2 * lanes))
-        t = (r[:, :lanes] + r[:, lanes:]).T
-        for k in range(heads):
-            out_refs[k][g:g + group, :] = t[k * group:(k + 1) * group]
-
-
-def head_bias(pair, w, heads, step=32):
+def head_bias_kernel(group, pair_ref, w_ref, *out_refs):
+    rows, cols, cz = pair_ref.shape
+    heads = w_ref.shape[1]
+    wh, wl = split(w_ref[...].T)
+    lhs = jnp.concatenate(
+        [jnp.concatenate([wh, wh], axis=1), jnp.concatenate([wl, wl], axis=1)], axis=0
+    )
+    for i in range(0, rows, group):
+        yh, yl = split(norm_rows(pair_ref[i:i + group].reshape(group * cols, cz)))
+        r = mm_nt(lhs, jnp.concatenate([yh, yl], axis=1))
+        r = r[:heads] + r[heads:]
+        for g in range(group):
+            for k in range(heads):
+                out_refs[k][i + g:i + g + 1, :] = r[k:k + 1, g * cols:(g + 1) * cols]
+
+
+def head_bias(pair, w, step=32, group=4):
     rows, cols, cz = pair.shape
-    group = w.shape[1] // heads
+    heads = w.shape[1]
     return pl.pallas_call(
         functools.partial(head_bias_kernel, group),
         out_shape=(jax.ShapeDtypeStruct((rows, cols), F32),) * heads,
         grid=(rows // step,),
         in_specs=[pl.BlockSpec((step, cols, cz), lambda i: (i, 0, 0)), whole(w)],
         out_specs=(pl.BlockSpec((step, cols), lambda i: (i, 0)),) * heads,
-        scratch_shapes=[pltpu.VMEM((group, 2 * cz, 2 * heads * group), BF16)],
         compiler_params=PARAMS,
         name="head_bias",
     )(pair, w)
@@ -517,7 +503,7 @@
         at = slice(part * span, (part + 1) * span)
         q = ref[0, 0]
         qh = q.astype(BF16).astype(F32)
-        q_ref[core, 0, n_ref[0] ^ part] = (
+        q_ref[core, 0, (n_ref[0] - 1) ^ part] = (
             jnp.concatenate([qh, qh, q - qh, jnp.zeros_like(q)], axis=0).T.astype(BF16)
         )
         hi, lo = split(ref[1, 0])
@@ -555,13 +541,14 @@
     )(n, *pieces)
 
 
-def head_attention_kernel(hw, at_ref, q_ref, k_ref, v_ref, *refs):
-    bias_refs, out_ref = refs[:-2], refs[-1]
-    _, parts, _, _ = bias_refs[0].shape
+def head_attention_kernel(hw, turn, tiles, at_ref, q_ref, k_ref, v_ref, *refs):
+    bias_refs, out_ref = refs[:tiles], refs[-1]
+    parts = bias_refs[0].shape[1]
     cores, seqs = q_ref.shape[:2]
+    core = at_ref[3 * turn + 2]
     bias = jnp.concatenate(
         [
-            jnp.concatenate([sum(b[h ^ at_ref[2], n] for b in bias_refs) for n in range(parts)], axis=1)
+            jnp.concatenate([sum(b[h ^ core, n] for b in bias_refs) for n in range(parts)], axis=1)
             for h in range(CORES)
         ],
         axis=0,
@@ -575,27 +562,28 @@
             out_ref[0, g, s] = (t[0:hw] + t[hw:2 * hw]) / t[2 * hw:2 * hw + 1]
 
 
-def head_attention(at, q, k, v, tiles, prev, hw, step=2):
+def head_attention(at, turn, q, k, v, tiles, prev, hw, step=2):
     cores, seqs, parts, span, _ = q.shape
-    return pl.pallas_call(
-        functools.partial(head_attention_kernel, hw),
-        out_shape=jax.ShapeDtypeStruct(prev.shape, F32),
+    before = () if prev is None else (prev,)
+    return pl.pallas_call(
+        functools.partial(head_attention_kernel, hw, turn, len(tiles)),
+        out_shape=jax.ShapeDtypeStruct((parts, cores, seqs, hw, span), F32),
         grid_spec=pltpu.PrefetchScalarGridSpec(
             num_scalar_prefetch=1,
             grid=(seqs // step,),
             in_specs=[
-                pl.BlockSpec((cores, step, 1, span, 4 * hw), lambda s, at: (0, s, at[0], 0, 0)),
+                pl.BlockSpec((cores, step, 1, span, 4 * hw), lambda s, at: (0, s, at[3 * turn], 0, 0)),
                 pl.BlockSpec((cores, step, 4 * hw, parts * span), lambda s, at: (0, s, 0, 0)),
                 pl.BlockSpec((cores, step, parts * span, 4 * hw), lambda s, at: (0, s, 0, 0)),
             ]
             + [whole(b) for b in tiles]
-            + [pl.BlockSpec(memory_space=pl.ANY)],
-            out_specs=pl.BlockSpec((1, cores, step, hw, span), lambda s, at: (at[1], 0, s, 0, 0)),
-        ),
-        input_output_aliases={4 + len(tiles): 0},
+            + [pl.BlockSpec(memory_space=pl.ANY) for _ in before],
+            out_specs=pl.BlockSpec((1, cores, step, hw, span), lambda s, at: (at[3 * turn + 1], 0, s, 0, 0)),
+        ),
+        input_output_aliases={4 + len(tiles): 0} if before else {},
         compiler_params=PARAMS,
         name="head_attention",
-    )(at, q, k, v, *tiles, prev)
+    )(at, q, k, v, *tiles, *before)
 
 
 def head_merge_kernel(heads, me_ref, *refs):
@@ -725,7 +713,7 @@
     expand_bias,
     down_weight,
 ):
-    seqs, span, ch = homolog_embedding.shape
+    _, _, ch = homolog_embedding.shape
     _, _, cz = pair_state.shape
     heads = pair_bias_weight.shape[1]
     hw = ch // heads
@@ -736,12 +724,12 @@
     me = n * CORES + c
     order = jnp.asarray(ORDER, jnp.int32)[z]
 
-    group = 16
-    lane = jnp.arange(heads * group, dtype=jnp.int32) // group
-    own_first = jnp.take(pair_bias_weight, lane ^ me, axis=1)
-    tiles = head_bias(pair_state, own_first, heads)
+    own_first = jnp.take(pair_bias_weight, jnp.arange(heads, dtype=jnp.int32) ^ me, axis=1)
+    at = jnp.stack([order, order ^ n, jnp.full_like(order, c)], axis=1).reshape(-1)
+    own_first, at = after(own_first, at), after(at, own_first)
+    tiles = head_bias(pair_state, own_first)
     *qkv, gate = head_project(
-        me[None], after(homolog_embedding, tiles[0]), probe_projector, lookup_projector, content_projector,
+        me[None], after(homolog_embedding, tiles[0], at), probe_projector, lookup_projector, content_projector,
         sigmoid_projector, sigmoid_offset, heads,
     )
     tiles = after(exchange(tiles, parts), gate)
@@ -750,12 +738,12 @@
     )
     near, second, third = line_gather(bias, parts)
     qkv = exchange(after(qkv, bias), parts)
-    q, k, v = stage(n[None], after(qkv, near, second[0]), parts)
-    att = jnp.zeros((parts, CORES, seqs, hw, span), F32)
+    marked = after(n[None], near, second[0]) + 1
+    q, k, v = stage(marked, after(qkv, near, second[0]), parts)
     bias = after(bias, second[1], third[0])
+    att = None
     for i, tile in enumerate(((bias,), (near,), second, third)):
-        at = jnp.stack([order[i], order[i] ^ n, c])
-        att = head_attention(at, q, k, v, tile, att, hw)
+        att = head_attention(at, i, q, k, v, tile, att, hw)
     pieces = exchange([att[p, r] for p in range(parts) for r in range(CORES)], parts)
     alignment_state_next, left_a, left_b, right = head_merge(
         jnp.stack([me, c]), pieces, gate, homolog_embedding, mixing_projector, mixing_offset,

time: 335 us -> 328 us (0.979)
  waiting for transfers between devices: 72 us -> 80.5 us
  Pallas kernels: 163 us -> 156 us
  other arithmetic: 8.34 us -> 3.94 us
    ppermute x38, waiting for transfers between devices: 72 us -> 80.5 us  [send(): return lax.ppermute(x, AXES, pairs)]
    pallas_call x1, Pallas kernels: 19.5 us -> 13 us  [head_bias(): pl.pallas_call(functools.partial(head_bias_kernel, group), out_shape=(jax...]
    another operation x3 -> x1, other arithmetic: 4.63 us -> 0.07 us  [per_head(): jnp.stack([order, order ^ n, jnp.full_like(order, c)], axis=1).reshape(-1)]
  transfers between devices with their start and end apart: 38 -> 38, of which waited for: 18 -> 19; matrix products, arithmetic and copies ran while one was open for 3% -> 1% of each run, Pallas kernels for 12% -> 12%
where the time goes in v4:
time: 328 us; the launch traced here: 327 us
  Pallas kernels  156 us (48%)
  waiting for transfers between devices  80.5 us (25%)
  starting transfers between devices  77.1 us (24%)
  local copies, waits for them, and re-layouts  8.93 us (3%)
  other arithmetic  3.94 us (1%)
    pallas_call x1, Pallas kernels, pair_update(): pl.pallas_call(functools.partial(pair_kernel, step_rows, group, seqs), ou...  82.7 us
    ppermute x38, waiting for transfers between devices, send(): return lax.ppermute(x, AXES, pairs)  80.5 us
    ppermute x38, starting transfers between devices, send(): return lax.ppermute(x, AXES, pairs)  77.1 us
    pallas_call x4, Pallas kernels, head_attention(): pl.pallas_call(functools.partial(head_attention_kernel, hw, turn, len(til...  36.7 us
    pallas_call x1, Pallas kernels, head_bias(): pl.pallas_call(functools.partial(head_bias_kernel, group), out_shape=(jax...  13 us
  transfers between devices with their start and end apart: 38, of which 19 were waited for; matrix products, arithmetic and copies ran while one was open for 1% of the time, Pallas kernels for 12%

profile of v4, /device:TPU:0, one launch (start us, length us, event | category | flops | bytes accessed | tf_op | source)
XLA Modules:
  0.0 327.5 jit_solution(5589714398073191171)
XLA Ops:
  4.9 13.0 %head_bias.1 = (f32[128,256]{1,0:T(8,128)}, f32[128,256]{1,0:T(8,128)}, f32[128,256]{1,0:T(8,128)}, f32[128,256]{1,0:T(8,128)}, f32[128,256]{1,0:T(8,128)}, /*in...) custom-call(f32[128,256,128]{2,1,0:T(8,128)} %pair_ref.3, f32[128,8]{1,0:T(8,128)} %bitcast.53), custom_call_target="tpu_custom_call" | custom-call | tf_op jit(solution)/shard_map/head_bias/pallas_call | solution.py:432
  18.5 2.6 collective-permute-start.1
  22.9 2.6 collective-permute-start.5
  28.0 6.5 %head_project.1 = (f32[3,4,32,256]{3,2,1,0:T(8,128)}, f32[3,4,32,256]{3,2,1,0:T(8,128)}, f32[3,4,32,256]{3,2,1,0:T(8,128)}, f32[3,4,32,256]{3,2,1,0:T(8,128)}, f...) custom-call(s32[1]{0:T(128)} %bitcast.me_ref, ...), custom_call_target="tpu_custom_call" | custom-call | tf_op jit(solution)/shard_map/head_project/pallas_call | solution.py:475
  38.7 22.4 %collective-permute-done.7.refs_0_ = f32[2,4,128,256]{3,2,1,0:T(8,128)S(1)} collective-permute-done((f32[2,4,128,256]{3,2,1,0:T(8,128)S(1)}, f32[2,4,128,256]{3,2,1,0:T(8,128)S(1)}, u32[]{:S(2)}, u32[]{:S(2)}) %collective-permute-start.7) | collective-permute-done | bytes 1048608 | tf_op jit(solution)/shard_map/ppermute | solution.py:392
  68.1 8.8 %collective-permute-done.10.refs_2_ = f32[3,4,32,256]{3,2,1,0:T(8,128)S(1)} collective-permute-done((f32[3,4,32,256]{3,2,1,0:T(8,128)S(1)}, f32[3,4,32,256]{3,2,1,0:T(8,128)S(1)}, u32[]{:S(2)}, u32[]{:S(2)}) %collective-permute-start.10) | collective-permute-done | bytes 393248 | tf_op jit(solution)/shard_map/ppermute | solution.py:392
  77.0 7.2 %collective-permute-done.11.refs_3_ = f32[3,4,32,256]{3,2,1,0:T(8,128)} collective-permute-done((f32[3,4,32,256]{3,2,1,0:T(8,128)S(1)}, f32[3,4,32,256]{3,2,1,0:T(8,128)}, u32[]{:S(2)}, u32[]{:S(2)}) %collective-permute-start.11) | collective-permute-done | bytes 393248 | tf_op jit(solution)/shard_map/ppermute | solution.py:392
  84.2 2.4 collective-permute-start.14
  88.3 9.0 %collective-permute-done.14.refs_6_ = f32[3,4,32,256]{3,2,1,0:T(8,128)} collective-permute-done((f32[3,4,32,256]{3,2,1,0:T(8,128)S(1)}, f32[3,4,32,256]{3,2,1,0:T(8,128)}, u32[]{:S(2)}, u32[]{:S(2)}) %collective-permute-start.14) | collective-permute-done | bytes 393248 | tf_op jit(solution)/shard_map/ppermute | solution.py:392
  97.2 7.9 %collective-permute-done.15.refs_7_ = f32[3,4,32,256]{3,2,1,0:T(8,128)} collective-permute-done((f32[3,4,32,256]{3,2,1,0:T(8,128)S(1)}, f32[3,4,32,256]{3,2,1,0:T(8,128)}, u32[]{:S(2)}, u32[]{:S(2)}) %collective-permute-start.15) | collective-permute-done | bytes 393248 | tf_op jit(solution)/shard_map/ppermute | solution.py:392
  105.1 5.8 %stage.1 = (bf16[2,4,4,256,128]{4,3,2,1,0:T(8,128)(2,1)}, bf16[2,4,128,1024]{3,2,1,0:T(8,128)(2,1)}, bf16[2,4,1024,128]{3,2,1,0:T(8,128)(2,1)}) custom-call(s32[1]{0:T(128)S(6)} %add.40.n_ref, f32[3,4,32,256]{3,2,1,0:T(8,128)} %get-tuple-element.94.refs_0_, f32[3,4,32,256]{3,2,1,0:T(8,128)} %copy-done.9, f32[3,4,32,256]{3,2,1,0:T(8,128)} %copy-done.10, ...), custom_call_target="tpu_custom_call" | custom-call | tf_op jit(solution)/shard_map/stage/pallas_call | solution.py:522
  110.9 9.0 %head_attention.4.refs_1_ = f32[4,2,4,32,256]{4,3,2,1,0:T(8,128)} custom-call(s32[12]{0:T(128)} %reshape.55.at_ref, bf16[2,4,4,256,128]{4,3,2,1,0:T(8,128)(2,1)} %get-tuple-element.102.q_ref, bf16[2,4,128,1024]{3,2,1,0:T(8,128)(2,1)} %get-tuple-element.103.k_ref, bf16[2,4,1024,128]{3,2,1,0:T(8,128)(2,1)} %get-tuple-element.104.v_ref, ...), custom_call_target="tpu_custom_call" | custom-call | tf_op jit(solution)/shard_map/head_attention/pallas_call | solution.py:568
  119.9 9.0 %head_attention.5.refs_2_ = f32[4,2,4,32,256]{4,3,2,1,0:T(8,128)} custom-call(s32[12]{0:T(128)} %reshape.55.at_ref, bf16[2,4,4,256,128]{4,3,2,1,0:T(8,128)(2,1)} %get-tuple-element.102.q_ref, bf16[2,4,128,1024]{3,2,1,0:T(8,128)(2,1)} %get-tuple-element.103.k_ref, bf16[2,4,1024,128]{3,2,1,0:T(8,128)(2,1)} %get-tuple-element.104.v_ref, ...), custom_call_target="tpu_custom_call", output_to_operand_aliasing={{}: (5, {})} | custom-call | tf_op jit(solution)/shard_map/head_attention/pallas_call | solution.py:568
  128.9 9.4 %head_attention.6.refs_2_ = f32[4,2,4,32,256]{4,3,2,1,0:T(8,128)} custom-call(s32[12]{0:T(128)} %reshape.55.at_ref, bf16[2,4,4,256,128]{4,3,2,1,0:T(8,128)(2,1)} %get-tuple-element.102.q_ref, bf16[2,4,128,1024]{3,2,1,0:T(8,128)(2,1)} %get-tuple-element.103.k_ref, bf16[2,4,1024,128]{3,2,1,0:T(8,128)(2,1)} %get-tuple-element.104.v_ref, ...), custom_call_target="tpu_custom_call", output_to_operand_aliasing={{}: (6, {})} | custom-call | tf_op jit(solution)/shard_map/head_attention/pallas_call | solution.py:568
  138.3 9.3 %head_attention.7 = f32[4,2,4,32,256]{4,3,2,1,0:T(8,128)} custom-call(s32[12]{0:T(128)} %reshape.55.at_ref, bf16[2,4,4,256,128]{4,3,2,1,0:T(8,128)(2,1)} %get-tuple-element.102.q_ref, bf16[2,4,128,1024]{3,2,1,0:T(8,128)(2,1)} %get-tuple-element.103.k_ref, bf16[2,4,1024,128]{3,2,1,0:T(8,128)(2,1)} %get-tuple-element.104.v_ref, ...), custom_call_target="tpu_custom_call", output_to_operand_aliasing={{}: (6, {})} | custom-call | tf_op jit(solution)/shard_map/head_attention/pallas_call | solution.py:568
  162.0 2.8 collective-permute-done.22.refs_4_
  165.6 6.5 %head_merge.1 = (f32[4,256,256]{2,1,0:T(8,128)}, f32[4,32,128]{2,1,0:T(8,128)}, f32[4,32,128]{2,1,0:T(8,128)}, f32[4,32,256]{2,1,0:T(8,128)}) custom-call(s32[2]{0:T(128)} %pad_add_fusion.me_ref, f32[4,32,256]{2,1,0:T(8,128)} %get-tuple-element.119.refs_0_, f32[4,32,256]{2,1,0:T(8,128)} %copy-done.18, f32[4,32,256]{2,1,0:T(8,128)} %copy-done.17, ...), custom_call_target="tpu_custom_call" | custom-call | tf_op jit(solution)/shard_map/head_merge/pallas_call | solution.py:628
  172.1 26.8 %collective-permute-start.32 = (f32[4,32,256]{2,1,0:T(8,128)}, f32[4,32,256]{2,1,0:T(8,128)S(1)}, u32[]{:S(2)}, u32[]{:S(2)}) collective-permute-start(f32[4,32,256]{2,1,0:T(8,128)} %get-tuple-element.109), channel_id=1, source_target_pairs={{0,8},{1,9},{2,10},{3,11},{4,12},{5,13},{6,14},{7,15},{8,0},{9,1},... | collective-permute-start | bytes 393224 | tf_op jit(solution)/shard_map/ppermute | solution.py:392
  199.6 3.0 collective-permute-done.32
  205.9 7.1 %collective-permute-done.34 = f32[4,32,256]{2,1,0:T(8,128)S(1)} collective-permute-done((f32[4,32,256]{2,1,0:T(8,128)S(1)}, f32[4,32,256]{2,1,0:T(8,128)S(1)}, u32[]{:S(2)}, u32[]{:S(2)}) %collective-permute-start.34) | collective-permute-done | bytes 131104 | tf_op jit(solution)/shard_map/ppermute | solution.py:392
  213.0 2.4 collective-permute-done.36
  220.9 12.5 %collective-permute-start.31 = (f32[2,4,32,128]{3,2,1,0:T(8,128)S(1)}, f32[2,4,32,128]{3,2,1,0:T(8,128)S(1)}, u32[]{:S(2)}, u32[]{:S(2)}) collective-permute-start(f32[2,4,32,128]{3,2,1,0:T(8,128)S(1)} %pad_maximum_fusion.2.refs_0_), channel_id=1, source_target_pairs={{0,3},{1,2},{2,1},{3,0},{4,7},{5,6},{6,5},{7,4},{8,11},{9,10},{10,... | collective-permute-start | bytes 393224 | tf_op jit(solution)/shard_map/ppermute | solution.py:392
  240.0 4.7 %pack.1 = (f32[4096,32]{1,0:T(8,128)}, f32[256,1024]{1,0:T(8,128)}) custom-call(s32[4]{0:T(128)} %get-tuple-element.120.slots_ref, f32[2,4,32,128]{3,2,1,0:T(8,128)} %copy-done.6, f32[2,4,32,128]{3,2,1,0:T(8,128)} %copy-done.21, f32[2,4,32,128]{3,2,1,0:T(8,128)} %copy-done.20, f32[2,4,32,128]{3,2,1,0:T(8,128)} %copy-done.19, f32[4,4,32,256]{3,2,1,0:T(8,128)} %copy-done.3, ...), custom_call_target="tpu_custom_call" | custom-call | tf_op jit(solution)/shard_map/pack/pallas_call | solution.py:677
  244.7 82.7 %pair_update.1 = f32[128,256,128]{2,1,0:T(8,128)} custom-call(f32[4096,32]{1,0:T(8,128)} %get-tuple-element.110.left_ref, f32[256,1024]{1,0:T(8,128)} %get-tuple-element.111.right_ref, f32[32,4096]{1,0:T(8,128)} %reshape.58.w_ref, f32[128,256,128]{2,1,0:T(8,128)} %pair_ref.3, f32[1,128]{1,0:T(1,128)} %bitcast.69, f32[128,512]{1,0:T(8,128)} %up_ref.1, ...), custom_call_target="tpu_custom_call" | custom-call | tf_op jit(solution)/shard_map/pair_update/pallas_call | solution.py:295
  (150 shorter events, 53.1 us)
Async XLA Ops:
  21.0 13.5 %collective-permute-start.2 = (f32[128,256]{1,0:T(8,128)}, f32[128,256]{1,0:T(8,128)S(1)}, u32[]{:S(2)}, u32[]{:S(2)}) collective-permute-start(f32[128,256]{1,0:T(8,128)} %get-tuple-element.62), channel_id=1, source_target_pairs={{0,5},{1,4},{2,7},{3,6},{4,1},{5,0},{6,3},{7,2},{8,13},{9,12},{10,... | collective-permute-start | bytes 393224 | tf_op jit(solution)/shard_map/ppermute | solution.py:392
  21.1 13.4 %collective-permute-start.3 = (f32[128,256]{1,0:T(8,128)}, f32[128,256]{1,0:T(8,128)S(1)}, u32[]{:S(2)}, u32[]{:S(2)}) collective-permute-start(f32[128,256]{1,0:T(8,128)} %get-tuple-element.63), channel_id=1, source_target_pairs={{0,2},{1,3},{2,0},{3,1},{4,6},{5,7},{6,4},{7,5},{8,10},{9,11},{10,... | collective-permute-start | bytes 393224 | tf_op jit(solution)/shard_map/ppermute | solution.py:392
  22.8 12.0 %collective-permute-start.4 = (f32[128,256]{1,0:T(8,128)}, f32[128,256]{1,0:T(8,128)S(1)}, u32[]{:S(2)}, u32[]{:S(2)}) collective-permute-start(f32[128,256]{1,0:T(8,128)} %get-tuple-element.64), channel_id=1, source_target_pairs={{0,6},{1,7},{2,4},{3,5},{4,2},{5,3},{6,0},{7,1},{8,14},{9,15},{10,... | collective-permute-start | bytes 393224 | tf_op jit(solution)/shard_map/ppermute | solution.py:392
  22.9 12.0 %collective-permute-start.5 = (f32[128,256]{1,0:T(8,128)}, f32[128,256]{1,0:T(8,128)S(1)}, u32[]{:S(2)}, u32[]{:S(2)}) collective-permute-start(f32[128,256]{1,0:T(8,128)} %get-tuple-element.65), channel_id=1, source_target_pairs={{0,3},{1,2},{2,1},{3,0},{4,7},{5,6},{6,5},{7,4},{8,11},{9,10},{10,... | collective-permute-start | bytes 393224 | tf_op jit(solution)/shard_map/ppermute | solution.py:392
  25.6 9.3 %collective-permute-start.6 = (f32[128,256]{1,0:T(8,128)}, f32[128,256]{1,0:T(8,128)S(1)}, u32[]{:S(2)}, u32[]{:S(2)}) collective-permute-start(f32[128,256]{1,0:T(8,128)} %get-tuple-element.66), channel_id=1, source_target_pairs={{0,7},{1,6},{2,5},{3,4},{4,3},{5,2},{6,1},{7,0},{8,15},{9,14},{10,... | collective-permute-start | bytes 393224 | tf_op jit(solution)/shard_map/ppermute | solution.py:392
  35.2 25.9 %collective-permute-start.7 = (f32[2,4,128,256]{3,2,1,0:T(8,128)S(1)}, f32[2,4,128,256]{3,2,1,0:T(8,128)S(1)}, u32[]{:S(2)}, u32[]{:S(2)}) collective-permute-start(f32[2,4,128,256]{3,2,1,0:T(8,128)S(1)} %pad_maximum_fusion.refs_0_), channel_id=1, source_target_pairs={{0,8},{1,9},{2,10},{3,11},{4,12},{5,13},{6,14},{7,15},{8,0},{9,1},... | collective-permute-start | bytes 3145736 | tf_op jit(solution)/shard_map/ppermute | solution.py:392
  37.0 25.0 %collective-permute-start.8 = (f32[2,4,128,256]{3,2,1,0:T(8,128)S(1)}, f32[2,4,128,256]{3,2,1,0:T(8,128)}, u32[]{:S(2)}, u32[]{:S(2)}) collective-permute-start(f32[2,4,128,256]{3,2,1,0:T(8,128)S(1)} %pad_maximum_fusion.refs_0_), channel_id=1, source_target_pairs={{8,16},{9,17},{10,18},{11,19},{12,20},{13,21},{14,22},{15,23},{16,... | collective-permute-start | bytes 3145736 | tf_op jit(solution)/shard_map/ppermute | solution.py:392
  62.0 48.9 %collective-permute-start.18 = (f32[2,4,128,256]{3,2,1,0:T(8,128)}, f32[2,4,128,256]{3,2,1,0:T(8,128)}, u32[]{:S(2)}, u32[]{:S(2)}) collective-permute-start(f32[2,4,128,256]{3,2,1,0:T(8,128)} %collective-permute-done.8.refs_0_), channel_id=1, source_target_pairs={{8,0},{9,1},{10,2},{11,3},{12,4},{13,5},{14,6},{15,7},{16,24},{17,... | collective-permute-start | bytes 3145736 | tf_op jit(solution)/shard_map/ppermute | solution.py:392
  63.3 75.0 %collective-permute-start.17 = (f32[2,4,128,256]{3,2,1,0:T(8,128)S(1)}, f32[2,4,128,256]{3,2,1,0:T(8,128)}, u32[]{:S(2)}, u32[]{:S(2)}) collective-permute-start(f32[2,4,128,256]{3,2,1,0:T(8,128)S(1)} %collective-permute-done.16.refs_0_), channel_id=1, source_target_pairs={{8,0},{9,1},{10,2},{11,3},{12,4},{13,5},{14,6},{15,7},{16,24},{17,... | collective-permute-start | bytes 3145736 | tf_op jit(solution)/shard_map/ppermute | solution.py:392
  64.8 12.1 %collective-permute-start.10 = (f32[3,4,32,256]{3,2,1,0:T(8,128)S(1)}, f32[3,4,32,256]{3,2,1,0:T(8,128)S(1)}, u32[]{:S(2)}, u32[]{:S(2)}) collective-permute-start(f32[3,4,32,256]{3,2,1,0:T(8,128)S(1)} %copy-done.30), channel_id=1, source_target_pairs={{0,1},{1,0},{2,3},{3,2},{4,5},{5,4},{6,7},{7,6},{8,9},{9,8},{10,11... | collective-permute-start | bytes 1179656 | tf_op jit(solution)/shard_map/ppermute | solution.py:392
  66.2 18.1 %collective-permute-start.11 = (f32[3,4,32,256]{3,2,1,0:T(8,128)S(1)}, f32[3,4,32,256]{3,2,1,0:T(8,128)}, u32[]{:S(2)}, u32[]{:S(2)}) collective-permute-start(f32[3,4,32,256]{3,2,1,0:T(8,128)S(1)} %copy-done.29), channel_id=1, source_target_pairs={{0,5},{1,4},{2,7},{3,6},{4,1},{5,0},{6,3},{7,2},{8,13},{9,12},{10,... | collective-permute-start | bytes 1179656 | tf_op jit(solution)/shard_map/ppermute | solution.py:392
  66.6 20.0 %collective-permute-start.12 = (f32[3,4,32,256]{3,2,1,0:T(8,128)S(1)}, f32[3,4,32,256]{3,2,1,0:T(8,128)}, u32[]{:S(2)}, u32[]{:S(2)}) collective-permute-start(f32[3,4,32,256]{3,2,1,0:T(8,128)S(1)} %copy-done.28), channel_id=1, source_target_pairs={{0,2},{1,3},{2,0},{3,1},{4,6},{5,7},{6,4},{7,5},{8,10},{9,11},{10,... | collective-permute-start | bytes 1179656 | tf_op jit(solution)/shard_map/ppermute | solution.py:392
  76.9 11.4 %collective-permute-start.13 = (f32[3,4,32,256]{3,2,1,0:T(8,128)S(1)}, f32[3,4,32,256]{3,2,1,0:T(8,128)}, u32[]{:S(2)}, u32[]{:S(2)}) collective-permute-start(f32[3,4,32,256]{3,2,1,0:T(8,128)S(1)} %copy-done.27), channel_id=1, source_target_pairs={{0,6},{1,7},{2,4},{3,5},{4,2},{5,3},{6,0},{7,1},{8,14},{9,15},{10,... | collective-permute-start | bytes 1179656 | tf_op jit(solution)/shard_map/ppermute | solution.py:392
  84.2 13.0 %collective-permute-start.14 = (f32[3,4,32,256]{3,2,1,0:T(8,128)S(1)}, f32[3,4,32,256]{3,2,1,0:T(8,128)}, u32[]{:S(2)}, u32[]{:S(2)}) collective-permute-start(f32[3,4,32,256]{3,2,1,0:T(8,128)S(1)} %copy-done.26), channel_id=1, source_target_pairs={{0,3},{1,2},{2,1},{3,0},{4,7},{5,6},{6,5},{7,4},{8,11},{9,10},{10,... | collective-permute-start | bytes 1179656 | tf_op jit(solution)/shard_map/ppermute | solution.py:392
  86.7 18.4 %collective-permute-start.15 = (f32[3,4,32,256]{3,2,1,0:T(8,128)S(1)}, f32[3,4,32,256]{3,2,1,0:T(8,128)}, u32[]{:S(2)}, u32[]{:S(2)}) collective-permute-start(f32[3,4,32,256]{3,2,1,0:T(8,128)S(1)} %copy-done.25), channel_id=1, source_target_pairs={{0,7},{1,6},{2,5},{3,4},{4,3},{5,2},{6,1},{7,0},{8,15},{9,14},{10,... | collective-permute-start | bytes 1179656 | tf_op jit(solution)/shard_map/ppermute | solution.py:392
  152.3 9.6 %collective-permute-start.23 = (f32[4,32,256]{2,1,0:T(8,128)S(1)}, f32[4,32,256]{2,1,0:T(8,128)S(1)}, u32[]{:S(2)}, u32[]{:S(2)}) collective-permute-start(f32[4,32,256]{2,1,0:T(8,128)S(1)} %get-tuple-element.114), channel_id=1, source_target_pairs={{0,6},{1,7},{2,4},{3,5},{4,2},{5,3},{6,0},{7,1},{8,14},{9,15},{10,... | collective-permute-start | bytes 393224 | tf_op jit(solution)/shard_map/ppermute | solution.py:392
  153.4 11.4 %collective-permute-start.22 = (f32[4,32,256]{2,1,0:T(8,128)S(1)}, f32[4,32,256]{2,1,0:T(8,128)S(1)}, u32[]{:S(2)}, u32[]{:S(2)}) collective-permute-start(f32[4,32,256]{2,1,0:T(8,128)S(1)} %get-tuple-element.115), channel_id=1, source_target_pairs={{0,2},{1,3},{2,0},{3,1},{4,6},{5,7},{6,4},{7,5},{8,10},{9,11},{10,... | collective-permute-start | bytes 393224 | tf_op jit(solution)/shard_map/ppermute | solution.py:392
  154.1 10.7 %collective-permute-start.21 = (f32[4,32,256]{2,1,0:T(8,128)S(1)}, f32[4,32,256]{2,1,0:T(8,128)S(1)}, u32[]{:S(2)}, u32[]{:S(2)}) collective-permute-start(f32[4,32,256]{2,1,0:T(8,128)S(1)} %get-tuple-element.116), channel_id=1, source_target_pairs={{0,5},{1,4},{2,7},{3,6},{4,1},{5,0},{6,3},{7,2},{8,13},{9,12},{10,... | collective-permute-start | bytes 393224 | tf_op jit(solution)/shard_map/ppermute | solution.py:392
  156.2 8.6 %collective-permute-start.20 = (f32[4,32,256]{2,1,0:T(8,128)S(1)}, f32[4,32,256]{2,1,0:T(8,128)S(1)}, u32[]{:S(2)}, u32[]{:S(2)}) collective-permute-start(f32[4,32,256]{2,1,0:T(8,128)S(1)} %get-tuple-element.117), channel_id=1, source_target_pairs={{0,1},{1,0},{2,3},{3,2},{4,5},{5,4},{6,7},{7,6},{8,9},{9,8},{10,11... | collective-permute-start | bytes 393224 | tf_op jit(solution)/shard_map/ppermute | solution.py:392
  172.1 30.5 %collective-permute-start.32 = (f32[4,32,256]{2,1,0:T(8,128)}, f32[4,32,256]{2,1,0:T(8,128)S(1)}, u32[]{:S(2)}, u32[]{:S(2)}) collective-permute-start(f32[4,32,256]{2,1,0:T(8,128)} %get-tuple-element.109), channel_id=1, source_target_pairs={{0,8},{1,9},{2,10},{3,11},{4,12},{5,13},{6,14},{7,15},{8,0},{9,1},... | collective-permute-start | bytes 393224 | tf_op jit(solution)/shard_map/ppermute | solution.py:392
  203.3 9.7 %collective-permute-start.34 = (f32[4,32,256]{2,1,0:T(8,128)S(1)}, f32[4,32,256]{2,1,0:T(8,128)S(1)}, u32[]{:S(2)}, u32[]{:S(2)}) collective-permute-start(f32[4,32,256]{2,1,0:T(8,128)S(1)} %collective-permute-done.33), channel_id=1, source_target_pairs={{8,0},{9,1},{10,2},{11,3},{12,4},{13,5},{14,6},{15,7},{16,24},{17,... | collective-permute-start | bytes 393224 | tf_op jit(solution)/shard_map/ppermute | solution.py:392
  204.6 10.8 %collective-permute-start.36 = (f32[4,32,256]{2,1,0:T(8,128)S(1)}, f32[4,32,256]{2,1,0:T(8,128)S(1)}, u32[]{:S(2)}, u32[]{:S(2)}) collective-permute-start(f32[4,32,256]{2,1,0:T(8,128)S(1)} %collective-permute-done.35), channel_id=1, source_target_pairs={{8,0},{9,1},{10,2},{11,3},{12,4},{13,5},{14,6},{15,7},{16,24},{17,... | collective-permute-start | bytes 393224 | tf_op jit(solution)/shard_map/ppermute | solution.py:392
  216.4 22.8 %collective-permute-start.37 = (f32[4,4,32,256]{3,2,1,0:T(8,128)S(1)}, f32[4,4,32,256]{3,2,1,0:T(8,128)S(1)}, u32[]{:S(2)}, u32[]{:S(2)}) collective-permute-start(f32[4,4,32,256]{3,2,1,0:T(8,128)S(1)} %pad_maximum_fusion.1.refs_4_), channel_id=1, source_target_pairs={{0,4},{1,5},{2,6},{3,7},{4,0},{5,1},{6,2},{7,3},{8,12},{9,13},{10,... | collective-permute-start | bytes 1572872 | tf_op jit(solution)/shard_map/ppermute | solution.py:392
  220.9 15.9 %collective-permute-start.31 = (f32[2,4,32,128]{3,2,1,0:T(8,128)S(1)}, f32[2,4,32,128]{3,2,1,0:T(8,128)S(1)}, u32[]{:S(2)}, u32[]{:S(2)}) collective-permute-start(f32[2,4,32,128]{3,2,1,0:T(8,128)S(1)} %pad_maximum_fusion.2.refs_0_), channel_id=1, source_target_pairs={{0,3},{1,2},{2,1},{3,0},{4,7},{5,6},{6,5},{7,4},{8,11},{9,10},{10,... | collective-permute-start | bytes 393224 | tf_op jit(solution)/shard_map/ppermute | solution.py:392
  (46 other events, 866.2 us)

commit v5 on v4

--- a/solution.py
+++ b/solution.py
@@ -410,44 +410,58 @@
     return near, (across, out2), (far, out3)
 
 
-def head_bias_kernel(group, pair_ref, w_ref, *out_refs):
+def own_head(ids_ref):
+    return ids_ref[1] * CORES + ids_ref[0] % CORES
+
+
+def head_bias_kernel(group, ids_ref, pair_ref, w_ref, *refs):
+    out_refs, lhs = refs[:-1], refs[-1]
     rows, cols, cz = pair_ref.shape
-    heads = w_ref.shape[1]
-    wh, wl = split(w_ref[...].T)
-    lhs = jnp.concatenate(
-        [jnp.concatenate([wh, wh], axis=1), jnp.concatenate([wl, wl], axis=1)], axis=0
-    )
+    heads = w_ref.shape[0]
+
+    @pl.when(pl.program_id(0) == 0)
+    def _():
+        me = own_head(ids_ref)
+        own = jnp.concatenate([w_ref[pl.ds(me ^ k, 1), :] for k in range(heads)], axis=0)
+        hi = own.astype(BF16).astype(F32)
+        both = jnp.concatenate([hi, own - hi], axis=0)
+        lhs[...] = jnp.concatenate([both, both], axis=1).astype(BF16)
+
     for i in range(0, rows, group):
         yh, yl = split(norm_rows(pair_ref[i:i + group].reshape(group * cols, cz)))
-        r = mm_nt(lhs, jnp.concatenate([yh, yl], axis=1))
+        r = mm_nt(lhs[...], jnp.concatenate([yh, yl], axis=1))
         r = r[:heads] + r[heads:]
         for g in range(group):
             for k in range(heads):
                 out_refs[k][i + g:i + g + 1, :] = r[k:k + 1, g * cols:(g + 1) * cols]
 
 
-def head_bias(pair, w, step=32, group=4):
+def head_bias(ids, pair, w, step=32, group=4):
     rows, cols, cz = pair.shape
-    heads = w.shape[1]
+    heads = w.shape[0]
     return pl.pallas_call(
         functools.partial(head_bias_kernel, group),
         out_shape=(jax.ShapeDtypeStruct((rows, cols), F32),) * heads,
-        grid=(rows // step,),
-        in_specs=[pl.BlockSpec((step, cols, cz), lambda i: (i, 0, 0)), whole(w)],
-        out_specs=(pl.BlockSpec((step, cols), lambda i: (i, 0)),) * heads,
+        grid_spec=pltpu.PrefetchScalarGridSpec(
+            num_scalar_prefetch=1,
+            grid=(rows // step,),
+            in_specs=[pl.BlockSpec((step, cols, cz), lambda i, _: (i, 0, 0)), whole(w)],
+            out_specs=(pl.BlockSpec((step, cols), lambda i, _: (i, 0)),) * heads,
+            scratch_shapes=[pltpu.VMEM((2 * heads, 2 * cz), BF16)],
+        ),
         compiler_params=PARAMS,
         name="head_bias",
-    )(pair, w)
-
-
-def head_project_kernel(heads, scale, me_ref, x_ref, wq_ref, wk_ref, wv_ref, wg_ref, bg_ref, *refs):
+    )(ids, pair, w)
+
+
+def head_project_kernel(heads, scale, ids_ref, x_ref, wq_ref, wk_ref, wv_ref, wg_ref, bg_ref, *refs):
     qkv_refs, (gate_ref, w_t, b_p, w_hi, w_lo) = refs[:heads], refs[heads:]
     ch = x_ref.shape[-1]
     hw = ch // heads
 
     @pl.when(pl.program_id(0) == 0)
     def _():
-        me = me_ref[0]
+        me = own_head(ids_ref)
         for t, (ref, f) in enumerate(((wq_ref, scale), (wk_ref, 1.0), (wv_ref, 1.0), (wg_ref, 1.0))):
             w_t[...] = ref[...].T * f
             for k in range(heads):
@@ -586,22 +600,22 @@
     )(at, q, k, v, *tiles, *before)
 
 
-def head_merge_kernel(heads, me_ref, *refs):
+def head_merge_kernel(heads, ids_ref, *refs):
     pieces = refs[:heads]
     gate_ref, x_ref, wm_ref, bm_ref, f1_ref, f2_ref = refs[heads:heads + 6]
     next_ref, left_refs, right_ref = refs[heads + 6], refs[heads + 7:heads + 9], refs[heads + 9]
     m_hi, m_lo, f_st = refs[heads + 10:]
     _, hw, span = pieces[0].shape
-    hid = f1_ref.shape[1]
+    hid = f1_ref.shape[0]
     rows = span // CORES
 
     @pl.when(pl.program_id(0) == 0)
     def _():
         for k in range(heads):
-            hi, lo = split(wm_ref[pl.ds(pl.multiple_of((me_ref[0] ^ k) * hw, hw), hw), :])
+            hi, lo = split(wm_ref[pl.ds(pl.multiple_of((own_head(ids_ref) ^ k) * hw, hw), hw), :])
             m_hi[k * hw:(k + 1) * hw, :] = hi
             m_lo[k * hw:(k + 1) * hw, :] = lo
-        hi, lo = split(jnp.concatenate([f1_ref[...], f2_ref[...]], axis=1).T)
+        hi, lo = split(jnp.concatenate([f1_ref[...], f2_ref[...]], axis=0))
         f_st[0:2 * hid, :] = hi
         f_st[2 * hid:4 * hid, :] = lo
 
@@ -612,7 +626,7 @@
     zh, zl = split(norm_rows(y))
     p = mm_nt(f_st[...], zh)
     p = p[:2 * hid] + p[2 * hid:] + mm_nt(f_st[0:2 * hid, :], zl)
-    swap = me_ref[1] == 1
+    swap = ids_ref[0] % CORES == 1
     left_refs[0][0] = jnp.where(swap, p[:hid, rows:], p[:hid, :rows])
     left_refs[1][0] = jnp.where(swap, p[:hid, :rows], p[:hid, rows:])
     right_ref[0] = p[hid:]
@@ -622,7 +636,7 @@
     seqs, span, ch = x.shape
     heads = len(pieces)
     hw = ch // heads
-    hid = f1.shape[1]
+    hid = f1.shape[0]
     rows = span // CORES
     bm = bm.reshape(1, ch)
     return pl.pallas_call(
@@ -718,18 +732,15 @@
     heads = pair_bias_weight.shape[1]
     hw = ch // heads
     hid = first_factor_projector.shape[1]
-    wide = lax.axis_index("wide")
-    n = lax.axis_index("narrow")
-    z, c = wide // CORES, wide % CORES
-    me = n * CORES + c
+    ids = jnp.stack([lax.axis_index("wide"), lax.axis_index("narrow")])
+    tiles = head_bias(ids, pair_state, pair_bias_weight.T)
+    late = after(ids, tiles[0])
+    z, c, n = late[0] // CORES, late[0] % CORES, late[1]
     order = jnp.asarray(ORDER, jnp.int32)[z]
-
-    own_first = jnp.take(pair_bias_weight, jnp.arange(heads, dtype=jnp.int32) ^ me, axis=1)
     at = jnp.stack([order, order ^ n, jnp.full_like(order, c)], axis=1).reshape(-1)
-    own_first, at = after(own_first, at), after(at, own_first)
-    tiles = head_bias(pair_state, own_first)
+    slots = (jnp.arange(PLANES, dtype=jnp.int32) ^ z) ^ n
     *qkv, gate = head_project(
-        me[None], after(homolog_embedding, tiles[0], at), probe_projector, lookup_projector, content_projector,
+        ids, after(homolog_embedding, tiles[0], at, slots), probe_projector, lookup_projector, content_projector,
         sigmoid_projector, sigmoid_offset, heads,
     )
     tiles = after(exchange(tiles, parts), gate)
@@ -746,17 +757,17 @@
         att = head_attention(at, i, q, k, v, tile, att, hw)
     pieces = exchange([att[p, r] for p in range(parts) for r in range(CORES)], parts)
     alignment_state_next, left_a, left_b, right = head_merge(
-        jnp.stack([me, c]), pieces, gate, homolog_embedding, mixing_projector, mixing_offset,
-        first_factor_projector, second_factor_projector,
+        ids, pieces, gate, homolog_embedding, mixing_projector, mixing_offset,
+        first_factor_projector.T, second_factor_projector.T,
     )
     turn = lambda z0, c0, n0: (n0, c0, z0)
     left_b, left_a = send(left_b, parts, turn), send(left_a, parts, turn)
     sibling = lambda z0, c0, n0: (z0, c0 ^ 1, n0)
     left = jnp.stack([left_a, send(left_b, parts, sibling)])
-    near, second, third = line_gather(right, parts)
+    rights = [right] + [send(right, parts, lambda z0, c0, n0, d=d: (z0 ^ d, c0, n0)) for d in range(1, PLANES)]
     lefts = [left] + [send(left, parts, lambda z0, c0, n0, d=d: (z0, c0, n0 ^ d)) for d in range(1, parts)]
-    own = jnp.stack([right, near, sum(second), sum(third)])
-    left_rows, right_cols = pack(order ^ n, lefts, own, send(own, parts, sibling))
+    own = jnp.stack(rights)
+    left_rows, right_cols = pack(slots, lefts, own, send(own, parts, sibling))
     pair_state_next = pair_update(
         left_rows, right_cols, outer_product_weight.reshape(hid, hid * cz), pair_state,
         outer_product_bias, up_weight, expand_bias, down_weight,

time: 328 us -> 324 us (0.988)
    ppermute x38 -> x36, waiting for transfers between devices: 80.5 us -> 77.4 us  [send(): return lax.ppermute(x, AXES, pairs)]
    ppermute x38 -> x36, starting transfers between devices: 77.1 us -> 74.4 us  [send(): return lax.ppermute(x, AXES, pairs)]
  transfers between devices with their start and end apart: 38 -> 36, of which waited for: 19 -> 16; matrix products, arithmetic and copies ran while one was open for 1% -> 2% of each run, Pallas kernels for 12% -> 12%
where the time goes in v5:
time: 324 us; the launch traced here: 323 us
  Pallas kernels  156 us (48%)
  waiting for transfers between devices  77.4 us (24%)
  starting transfers between devices  74.4 us (23%)
  local copies, waits for them, and re-layouts  7.36 us (2%)
  between operations  4.14 us (1%)
  other arithmetic  3.46 us (1%)
    pallas_call x1, Pallas kernels, pair_update(): pl.pallas_call(functools.partial(pair_kernel, step_rows, group, seqs), ou...  82.2 us
    ppermute x36, waiting for transfers between devices, send(): return lax.ppermute(x, AXES, pairs)  77.4 us
    ppermute x36, starting transfers between devices, send(): return lax.ppermute(x, AXES, pairs)  74.4 us
    pallas_call x4, Pallas kernels, head_attention(): pl.pallas_call(functools.partial(head_attention_kernel, hw, turn, len(til...  36.3 us
    pallas_call x1, Pallas kernels, head_bias(): pl.pallas_call(functools.partial(head_bias_kernel, group), out_shape=(jax...  13.6 us
    pallas_call x1, Pallas kernels, head_project(): pl.pallas_call(functools.partial(head_project_kernel, heads, 1.0 / math.s...  7.14 us
  transfers between devices with their start and end apart: 36, of which 16 were waited for; matrix products, arithmetic and copies ran while one was open for 2% of the time, Pallas kernels for 12%

profile of v5, /device:TPU:0, one launch (start us, length us, event | category | flops | bytes accessed | tf_op | source)
XLA Modules:
  0.0 322.9 jit_solution(12040712679719463347)
XLA Ops:
  1.2 13.6 %head_bias.1 = (f32[128,256]{1,0:T(8,128)}, f32[128,256]{1,0:T(8,128)}, f32[128,256]{1,0:T(8,128)}, f32[128,256]{1,0:T(8,128)}, f32[128,256]{1,0:T(8,128)}, /*in...) custom-call(s32[2]{0:T(128)} %pad_add_fusion.ids_ref, f32[128,256,128]{2,1,0:T(8,128)} %pair_ref.3, ...), custom_call_target="tpu_custom_call" | custom-call | tf_op jit(solution)/shard_map/head_bias/pallas_call | solution.py:442
  15.4 2.6 collective-permute-start.1
  23.5 2.7 collective-permute-start.5
  29.1 7.1 %head_project.1 = (f32[3,4,32,256]{3,2,1,0:T(8,128)}, f32[3,4,32,256]{3,2,1,0:T(8,128)}, f32[3,4,32,256]{3,2,1,0:T(8,128)}, f32[3,4,32,256]{3,2,1,0:T(8,128)}, f...) custom-call(s32[2]{0:T(128)} %pad_add_fusion.ids_ref, ...), custom_call_target="tpu_custom_call" | custom-call | tf_op jit(solution)/shard_map/head_project/pallas_call | solution.py:489
  40.0 22.0 %collective-permute-done.7.refs_0_ = f32[2,4,128,256]{3,2,1,0:T(8,128)S(1)} collective-permute-done((f32[2,4,128,256]{3,2,1,0:T(8,128)S(1)}, f32[2,4,128,256]{3,2,1,0:T(8,128)S(1)}, u32[]{:S(2)}, u32[]{:S(2)}) %collective-permute-start.7) | collective-permute-done | bytes 1048608 | tf_op jit(solution)/shard_map/ppermute | solution.py:392
  69.1 8.4 %collective-permute-done.10.refs_2_ = f32[3,4,32,256]{3,2,1,0:T(8,128)S(1)} collective-permute-done((f32[3,4,32,256]{3,2,1,0:T(8,128)S(1)}, f32[3,4,32,256]{3,2,1,0:T(8,128)S(1)}, u32[]{:S(2)}, u32[]{:S(2)}) %collective-permute-start.10) | collective-permute-done | bytes 393248 | tf_op jit(solution)/shard_map/ppermute | solution.py:392
  78.1 7.0 %collective-permute-done.11.refs_3_ = f32[3,4,32,256]{3,2,1,0:T(8,128)} collective-permute-done((f32[3,4,32,256]{3,2,1,0:T(8,128)S(1)}, f32[3,4,32,256]{3,2,1,0:T(8,128)}, u32[]{:S(2)}, u32[]{:S(2)}) %collective-permute-start.11) | collective-permute-done | bytes 393248 | tf_op jit(solution)/shard_map/ppermute | solution.py:392
  85.1 2.6 collective-permute-start.14
  88.8 9.3 %collective-permute-done.14.refs_6_ = f32[3,4,32,256]{3,2,1,0:T(8,128)} collective-permute-done((f32[3,4,32,256]{3,2,1,0:T(8,128)S(1)}, f32[3,4,32,256]{3,2,1,0:T(8,128)}, u32[]{:S(2)}, u32[]{:S(2)}) %collective-permute-start.14) | collective-permute-done | bytes 393248 | tf_op jit(solution)/shard_map/ppermute | solution.py:392
  98.1 7.7 %collective-permute-done.15.refs_7_ = f32[3,4,32,256]{3,2,1,0:T(8,128)} collective-permute-done((f32[3,4,32,256]{3,2,1,0:T(8,128)S(1)}, f32[3,4,32,256]{3,2,1,0:T(8,128)}, u32[]{:S(2)}, u32[]{:S(2)}) %collective-permute-start.15) | collective-permute-done | bytes 393248 | tf_op jit(solution)/shard_map/ppermute | solution.py:392
  106.4 6.0 %stage.1 = (bf16[2,4,4,256,128]{4,3,2,1,0:T(8,128)(2,1)}, bf16[2,4,128,1024]{3,2,1,0:T(8,128)(2,1)}, bf16[2,4,1024,128]{3,2,1,0:T(8,128)(2,1)}) custom-call(s32[1]{0:T(128)S(6)} %add.13.n_ref, f32[3,4,32,256]{3,2,1,0:T(8,128)} %get-tuple-element.92.refs_0_, f32[3,4,32,256]{3,2,1,0:T(8,128)} %copy-done.7, f32[3,4,32,256]{3,2,1,0:T(8,128)} %copy-done.8, ...), custom_call_target="tpu_custom_call" | custom-call | tf_op jit(solution)/shard_map/stage/pallas_call | solution.py:536
  112.3 8.8 %head_attention.4.refs_1_ = f32[4,2,4,32,256]{4,3,2,1,0:T(8,128)} custom-call(s32[12]{0:T(128)} %reshape.32.at_ref, bf16[2,4,4,256,128]{4,3,2,1,0:T(8,128)(2,1)} %get-tuple-element.100.q_ref, bf16[2,4,128,1024]{3,2,1,0:T(8,128)(2,1)} %get-tuple-element.101.k_ref, bf16[2,4,1024,128]{3,2,1,0:T(8,128)(2,1)} %get-tuple-element.102.v_ref, f32[2,4,128,256]{3,2,1,0:T(8,128)} %copy-done), custom_call_target="tpu_custom_call" | custom-call | tf_op jit(solution)/shard_map/head_attention/pallas_call | solution.py:582
  121.2 8.8 %head_attention.5.refs_2_ = f32[4,2,4,32,256]{4,3,2,1,0:T(8,128)} custom-call(s32[12]{0:T(128)} %reshape.32.at_ref, bf16[2,4,4,256,128]{4,3,2,1,0:T(8,128)(2,1)} %get-tuple-element.100.q_ref, bf16[2,4,128,1024]{3,2,1,0:T(8,128)(2,1)} %get-tuple-element.101.k_ref, bf16[2,4,1024,128]{3,2,1,0:T(8,128)(2,1)} %get-tuple-element.102.v_ref, ...), custom_call_target="tpu_custom_call", output_to_operand_aliasing={{}: (5, {})} | custom-call | tf_op jit(solution)/shard_map/head_attention/pallas_call | solution.py:582
  130.0 9.3 %head_attention.6.refs_2_ = f32[4,2,4,32,256]{4,3,2,1,0:T(8,128)} custom-call(s32[12]{0:T(128)} %reshape.32.at_ref, bf16[2,4,4,256,128]{4,3,2,1,0:T(8,128)(2,1)} %get-tuple-element.100.q_ref, bf16[2,4,128,1024]{3,2,1,0:T(8,128)(2,1)} %get-tuple-element.101.k_ref, bf16[2,4,1024,128]{3,2,1,0:T(8,128)(2,1)} %get-tuple-element.102.v_ref, ...), custom_call_target="tpu_custom_call", output_to_operand_aliasing={{}: (6, {})} | custom-call | tf_op jit(solution)/shard_map/head_attention/pallas_call | solution.py:582
  139.3 9.3 %head_attention.7 = f32[4,2,4,32,256]{4,3,2,1,0:T(8,128)} custom-call(s32[12]{0:T(128)} %reshape.32.at_ref, bf16[2,4,4,256,128]{4,3,2,1,0:T(8,128)(2,1)} %get-tuple-element.100.q_ref, bf16[2,4,128,1024]{3,2,1,0:T(8,128)(2,1)} %get-tuple-element.101.k_ref, bf16[2,4,1024,128]{3,2,1,0:T(8,128)(2,1)} %get-tuple-element.102.v_ref, ...), custom_call_target="tpu_custom_call", output_to_operand_aliasing={{}: (6, {})} | custom-call | tf_op jit(solution)/shard_map/head_attention/pallas_call | solution.py:582
  150.7 2.4 collective-permute-start.25
  163.0 2.8 collective-permute-done.22.refs_4_
  166.8 6.3 %head_merge.1 = (f32[4,256,256]{2,1,0:T(8,128)}, f32[4,32,128]{2,1,0:T(8,128)}, f32[4,32,128]{2,1,0:T(8,128)}, f32[4,32,256]{2,1,0:T(8,128)}) custom-call(s32[2]{0:T(128)} %pad_add_fusion.ids_ref, f32[4,32,256]{2,1,0:T(8,128)} %get-tuple-element.117.refs_0_, f32[4,32,256]{2,1,0:T(8,128)} %copy-done.16, f32[4,32,256]{2,1,0:T(8,128)} %copy-done.15, ...), custom_call_target="tpu_custom_call" | custom-call | tf_op jit(solution)/shard_map/head_merge/pallas_call | solution.py:642
  173.1 3.7 %collective-permute-start.34 = (f32[4,32,256]{2,1,0:T(8,128)}, f32[4,32,256]{2,1,0:T(8,128)S(1)}, u32[]{:S(2)}, u32[]{:S(2)}) collective-permute-start(f32[4,32,256]{2,1,0:T(8,128)} %get-tuple-element.107), channel_id=1, source_target_pairs={{0,24},{1,25},{2,26},{3,27},{4,28},{5,29},{6,30},{7,31},{8,16},{9,... | collective-permute-start | bytes 393224 | tf_op jit(solution)/shard_map/ppermute | solution.py:392
  176.7 24.8 %collective-permute-start.33 = (f32[4,32,256]{2,1,0:T(8,128)}, f32[4,32,256]{2,1,0:T(8,128)S(1)}, u32[]{:S(2)}, u32[]{:S(2)}) collective-permute-start(f32[4,32,256]{2,1,0:T(8,128)} %get-tuple-element.107), channel_id=1, source_target_pairs={{0,16},{1,17},{2,18},{3,19},{4,20},{5,21},{6,22},{7,23},{8,24},{9,... | collective-permute-start | bytes 393224 | tf_op jit(solution)/shard_map/ppermute | solution.py:392
  201.7 9.2 %collective-permute-done.33 = f32[4,32,256]{2,1,0:T(8,128)S(1)} collective-permute-done((f32[4,32,256]{2,1,0:T(8,128)}, f32[4,32,256]{2,1,0:T(8,128)S(1)}, u32[]{:S(2)}, u32[]{:S(2)}) %collective-permute-start.33) | collective-permute-done | bytes 131104 | tf_op jit(solution)/shard_map/ppermute | solution.py:392
  216.3 12.5 %collective-permute-start.31 = (f32[2,4,32,128]{3,2,1,0:T(8,128)S(1)}, f32[2,4,32,128]{3,2,1,0:T(8,128)S(1)}, u32[]{:S(2)}, u32[]{:S(2)}) collective-permute-start(f32[2,4,32,128]{3,2,1,0:T(8,128)S(1)} %pad_maximum_fusion.2.refs_0_), channel_id=1, source_target_pairs={{0,3},{1,2},{2,1},{3,0},{4,7},{5,6},{6,5},{7,4},{8,11},{9,10},{10,... | collective-permute-start | bytes 393224 | tf_op jit(solution)/shard_map/ppermute | solution.py:392
  236.0 4.7 %pack.1 = (f32[4096,32]{1,0:T(8,128)}, f32[256,1024]{1,0:T(8,128)}) custom-call(s32[4]{0:T(128)} %xor_xor_fusion.slots_ref, f32[2,4,32,128]{3,2,1,0:T(8,128)} %copy-done.4, f32[2,4,32,128]{3,2,1,0:T(8,128)} %copy-done.19, f32[2,4,32,128]{3,2,1,0:T(8,128)} %copy-done.18, f32[2,4,32,128]{3,2,1,0:T(8,128)} %copy-done.17, f32[4,4,32,256]{3,2,1,0:T(8,128)} %copy-done.1, ...), custom_call_target="tpu_custom_call" | custom-call | tf_op jit(solution)/shard_map/pack/pallas_call | solution.py:691
  240.7 82.2 %pair_update.1 = f32[128,256,128]{2,1,0:T(8,128)} custom-call(f32[4096,32]{1,0:T(8,128)} %get-tuple-element.108.left_ref, f32[256,1024]{1,0:T(8,128)} %get-tuple-element.109.right_ref, f32[32,4096]{1,0:T(8,128)} %reshape.35.w_ref, f32[128,256,128]{2,1,0:T(8,128)} %pair_ref.3, f32[1,128]{1,0:T(1,128)} %bitcast.70, f32[128,512]{1,0:T(8,128)} %up_ref.1, ...), custom_call_target="tpu_custom_call" | custom-call | tf_op jit(solution)/shard_map/pair_update/pallas_call | solution.py:295
  (134 shorter events, 45.0 us)
Async XLA Ops:
  15.4 10.9 %collective-permute-start.1 = (f32[128,256]{1,0:T(8,128)}, f32[128,256]{1,0:T(8,128)S(1)}, u32[]{:S(2)}, u32[]{:S(2)}) collective-permute-start(f32[128,256]{1,0:T(8,128)} %get-tuple-element.59), channel_id=1, source_target_pairs={{0,1},{1,0},{2,3},{3,2},{4,5},{5,4},{6,7},{7,6},{8,9},{9,8},{10,11... | collective-permute-start | bytes 393224 | tf_op jit(solution)/shard_map/ppermute | solution.py:392
  17.9 18.3 %collective-permute-start.2 = (f32[128,256]{1,0:T(8,128)}, f32[128,256]{1,0:T(8,128)S(1)}, u32[]{:S(2)}, u32[]{:S(2)}) collective-permute-start(f32[128,256]{1,0:T(8,128)} %get-tuple-element.60), channel_id=1, source_target_pairs={{0,5},{1,4},{2,7},{3,6},{4,1},{5,0},{6,3},{7,2},{8,13},{9,12},{10,... | collective-permute-start | bytes 393224 | tf_op jit(solution)/shard_map/ppermute | solution.py:392
  18.0 18.3 %collective-permute-start.3 = (f32[128,256]{1,0:T(8,128)}, f32[128,256]{1,0:T(8,128)S(1)}, u32[]{:S(2)}, u32[]{:S(2)}) collective-permute-start(f32[128,256]{1,0:T(8,128)} %get-tuple-element.61), channel_id=1, source_target_pairs={{0,2},{1,3},{2,0},{3,1},{4,6},{5,7},{6,4},{7,5},{8,10},{9,11},{10,... | collective-permute-start | bytes 393224 | tf_op jit(solution)/shard_map/ppermute | solution.py:392
  19.7 16.5 %collective-permute-start.4 = (f32[128,256]{1,0:T(8,128)}, f32[128,256]{1,0:T(8,128)S(1)}, u32[]{:S(2)}, u32[]{:S(2)}) collective-permute-start(f32[128,256]{1,0:T(8,128)} %get-tuple-element.62), channel_id=1, source_target_pairs={{0,6},{1,7},{2,4},{3,5},{4,2},{5,3},{6,0},{7,1},{8,14},{9,15},{10,... | collective-permute-start | bytes 393224 | tf_op jit(solution)/shard_map/ppermute | solution.py:392
  23.5 12.7 %collective-permute-start.5 = (f32[128,256]{1,0:T(8,128)}, f32[128,256]{1,0:T(8,128)S(1)}, u32[]{:S(2)}, u32[]{:S(2)}) collective-permute-start(f32[128,256]{1,0:T(8,128)} %get-tuple-element.63), channel_id=1, source_target_pairs={{0,3},{1,2},{2,1},{3,0},{4,7},{5,6},{6,5},{7,4},{8,11},{9,10},{10,... | collective-permute-start | bytes 393224 | tf_op jit(solution)/shard_map/ppermute | solution.py:392
  26.2 10.1 %collective-permute-start.6 = (f32[128,256]{1,0:T(8,128)}, f32[128,256]{1,0:T(8,128)S(1)}, u32[]{:S(2)}, u32[]{:S(2)}) collective-permute-start(f32[128,256]{1,0:T(8,128)} %get-tuple-element.64), channel_id=1, source_target_pairs={{0,7},{1,6},{2,5},{3,4},{4,3},{5,2},{6,1},{7,0},{8,15},{9,14},{10,... | collective-permute-start | bytes 393224 | tf_op jit(solution)/shard_map/ppermute | solution.py:392
  36.6 25.4 %collective-permute-start.7 = (f32[2,4,128,256]{3,2,1,0:T(8,128)S(1)}, f32[2,4,128,256]{3,2,1,0:T(8,128)S(1)}, u32[]{:S(2)}, u32[]{:S(2)}) collective-permute-start(f32[2,4,128,256]{3,2,1,0:T(8,128)S(1)} %pad_maximum_fusion.refs_0_), channel_id=1, source_target_pairs={{0,8},{1,9},{2,10},{3,11},{4,12},{5,13},{6,14},{7,15},{8,0},{9,1},... | collective-permute-start | bytes 3145736 | tf_op jit(solution)/shard_map/ppermute | solution.py:392
  38.3 24.5 %collective-permute-start.8 = (f32[2,4,128,256]{3,2,1,0:T(8,128)S(1)}, f32[2,4,128,256]{3,2,1,0:T(8,128)}, u32[]{:S(2)}, u32[]{:S(2)}) collective-permute-start(f32[2,4,128,256]{3,2,1,0:T(8,128)S(1)} %pad_maximum_fusion.refs_0_), channel_id=1, source_target_pairs={{8,16},{9,17},{10,18},{11,19},{12,20},{13,21},{14,22},{15,23},{16,... | collective-permute-start | bytes 3145736 | tf_op jit(solution)/shard_map/ppermute | solution.py:392
  62.9 49.5 %collective-permute-start.18 = (f32[2,4,128,256]{3,2,1,0:T(8,128)}, f32[2,4,128,256]{3,2,1,0:T(8,128)}, u32[]{:S(2)}, u32[]{:S(2)}) collective-permute-start(f32[2,4,128,256]{3,2,1,0:T(8,128)} %collective-permute-done.8.refs_0_), channel_id=1, source_target_pairs={{8,0},{9,1},{10,2},{11,3},{12,4},{13,5},{14,6},{15,7},{16,24},{17,... | collective-permute-start | bytes 3145736 | tf_op jit(solution)/shard_map/ppermute | solution.py:392
  64.2 75.1 %collective-permute-start.17 = (f32[2,4,128,256]{3,2,1,0:T(8,128)S(1)}, f32[2,4,128,256]{3,2,1,0:T(8,128)}, u32[]{:S(2)}, u32[]{:S(2)}) collective-permute-start(f32[2,4,128,256]{3,2,1,0:T(8,128)S(1)} %collective-permute-done.16.refs_0_), channel_id=1, source_target_pairs={{8,0},{9,1},{10,2},{11,3},{12,4},{13,5},{14,6},{15,7},{16,24},{17,... | collective-permute-start | bytes 3145736 | tf_op jit(solution)/shard_map/ppermute | solution.py:392
  65.5 12.1 %collective-permute-start.10 = (f32[3,4,32,256]{3,2,1,0:T(8,128)S(1)}, f32[3,4,32,256]{3,2,1,0:T(8,128)S(1)}, u32[]{:S(2)}, u32[]{:S(2)}) collective-permute-start(f32[3,4,32,256]{3,2,1,0:T(8,128)S(1)} %copy-done.28), channel_id=1, source_target_pairs={{0,1},{1,0},{2,3},{3,2},{4,5},{5,4},{6,7},{7,6},{8,9},{9,8},{10,11... | collective-permute-start | bytes 1179656 | tf_op jit(solution)/shard_map/ppermute | solution.py:392
  67.2 17.9 %collective-permute-start.11 = (f32[3,4,32,256]{3,2,1,0:T(8,128)S(1)}, f32[3,4,32,256]{3,2,1,0:T(8,128)}, u32[]{:S(2)}, u32[]{:S(2)}) collective-permute-start(f32[3,4,32,256]{3,2,1,0:T(8,128)S(1)} %copy-done.27), channel_id=1, source_target_pairs={{0,5},{1,4},{2,7},{3,6},{4,1},{5,0},{6,3},{7,2},{8,13},{9,12},{10,... | collective-permute-start | bytes 1179656 | tf_op jit(solution)/shard_map/ppermute | solution.py:392
  67.4 20.3 %collective-permute-start.12 = (f32[3,4,32,256]{3,2,1,0:T(8,128)S(1)}, f32[3,4,32,256]{3,2,1,0:T(8,128)}, u32[]{:S(2)}, u32[]{:S(2)}) collective-permute-start(f32[3,4,32,256]{3,2,1,0:T(8,128)S(1)} %copy-done.26), channel_id=1, source_target_pairs={{0,2},{1,3},{2,0},{3,1},{4,6},{5,7},{6,4},{7,5},{8,10},{9,11},{10,... | collective-permute-start | bytes 1179656 | tf_op jit(solution)/shard_map/ppermute | solution.py:392
  77.5 11.3 %collective-permute-start.13 = (f32[3,4,32,256]{3,2,1,0:T(8,128)S(1)}, f32[3,4,32,256]{3,2,1,0:T(8,128)}, u32[]{:S(2)}, u32[]{:S(2)}) collective-permute-start(f32[3,4,32,256]{3,2,1,0:T(8,128)S(1)} %copy-done.25), channel_id=1, source_target_pairs={{0,6},{1,7},{2,4},{3,5},{4,2},{5,3},{6,0},{7,1},{8,14},{9,15},{10,... | collective-permute-start | bytes 1179656 | tf_op jit(solution)/shard_map/ppermute | solution.py:392
  85.1 13.0 %collective-permute-start.14 = (f32[3,4,32,256]{3,2,1,0:T(8,128)S(1)}, f32[3,4,32,256]{3,2,1,0:T(8,128)}, u32[]{:S(2)}, u32[]{:S(2)}) collective-permute-start(f32[3,4,32,256]{3,2,1,0:T(8,128)S(1)} %copy-done.24), channel_id=1, source_target_pairs={{0,3},{1,2},{2,1},{3,0},{4,7},{5,6},{6,5},{7,4},{8,11},{9,10},{10,... | collective-permute-start | bytes 1179656 | tf_op jit(solution)/shard_map/ppermute | solution.py:392
  87.7 18.1 %collective-permute-start.15 = (f32[3,4,32,256]{3,2,1,0:T(8,128)S(1)}, f32[3,4,32,256]{3,2,1,0:T(8,128)}, u32[]{:S(2)}, u32[]{:S(2)}) collective-permute-start(f32[3,4,32,256]{3,2,1,0:T(8,128)S(1)} %copy-done.23), channel_id=1, source_target_pairs={{0,7},{1,6},{2,5},{3,4},{4,3},{5,2},{6,1},{7,0},{8,15},{9,14},{10,... | collective-permute-start | bytes 1179656 | tf_op jit(solution)/shard_map/ppermute | solution.py:392
  153.4 9.6 %collective-permute-start.23 = (f32[4,32,256]{2,1,0:T(8,128)S(1)}, f32[4,32,256]{2,1,0:T(8,128)S(1)}, u32[]{:S(2)}, u32[]{:S(2)}) collective-permute-start(f32[4,32,256]{2,1,0:T(8,128)S(1)} %get-tuple-element.112), channel_id=1, source_target_pairs={{0,6},{1,7},{2,4},{3,5},{4,2},{5,3},{6,0},{7,1},{8,14},{9,15},{10,... | collective-permute-start | bytes 393224 | tf_op jit(solution)/shard_map/ppermute | solution.py:392
  154.7 11.1 %collective-permute-start.22 = (f32[4,32,256]{2,1,0:T(8,128)S(1)}, f32[4,32,256]{2,1,0:T(8,128)S(1)}, u32[]{:S(2)}, u32[]{:S(2)}) collective-permute-start(f32[4,32,256]{2,1,0:T(8,128)S(1)} %get-tuple-element.113), channel_id=1, source_target_pairs={{0,2},{1,3},{2,0},{3,1},{4,6},{5,7},{6,4},{7,5},{8,10},{9,11},{10,... | collective-permute-start | bytes 393224 | tf_op jit(solution)/shard_map/ppermute | solution.py:392
  155.1 10.7 %collective-permute-start.21 = (f32[4,32,256]{2,1,0:T(8,128)S(1)}, f32[4,32,256]{2,1,0:T(8,128)S(1)}, u32[]{:S(2)}, u32[]{:S(2)}) collective-permute-start(f32[4,32,256]{2,1,0:T(8,128)S(1)} %get-tuple-element.114), channel_id=1, source_target_pairs={{0,5},{1,4},{2,7},{3,6},{4,1},{5,0},{6,3},{7,2},{8,13},{9,12},{10,... | collective-permute-start | bytes 393224 | tf_op jit(solution)/shard_map/ppermute | solution.py:392
  173.1 28.6 %collective-permute-start.34 = (f32[4,32,256]{2,1,0:T(8,128)}, f32[4,32,256]{2,1,0:T(8,128)S(1)}, u32[]{:S(2)}, u32[]{:S(2)}) collective-permute-start(f32[4,32,256]{2,1,0:T(8,128)} %get-tuple-element.107), channel_id=1, source_target_pairs={{0,24},{1,25},{2,26},{3,27},{4,28},{5,29},{6,30},{7,31},{8,16},{9,... | collective-permute-start | bytes 393224 | tf_op jit(solution)/shard_map/ppermute | solution.py:392
  176.7 34.1 %collective-permute-start.33 = (f32[4,32,256]{2,1,0:T(8,128)}, f32[4,32,256]{2,1,0:T(8,128)S(1)}, u32[]{:S(2)}, u32[]{:S(2)}) collective-permute-start(f32[4,32,256]{2,1,0:T(8,128)} %get-tuple-element.107), channel_id=1, source_target_pairs={{0,16},{1,17},{2,18},{3,19},{4,20},{5,21},{6,22},{7,23},{8,24},{9,... | collective-permute-start | bytes 393224 | tf_op jit(solution)/shard_map/ppermute | solution.py:392
  201.6 9.3 %collective-permute-start.32 = (f32[4,32,256]{2,1,0:T(8,128)}, f32[4,32,256]{2,1,0:T(8,128)S(1)}, u32[]{:S(2)}, u32[]{:S(2)}) collective-permute-start(f32[4,32,256]{2,1,0:T(8,128)} %get-tuple-element.107), channel_id=1, source_target_pairs={{0,8},{1,9},{2,10},{3,11},{4,12},{5,13},{6,14},{7,15},{8,0},{9,1},... | collective-permute-start | bytes 393224 | tf_op jit(solution)/shard_map/ppermute | solution.py:392
  211.8 22.7 %collective-permute-start.35 = (f32[4,4,32,256]{3,2,1,0:T(8,128)S(1)}, f32[4,4,32,256]{3,2,1,0:T(8,128)S(1)}, u32[]{:S(2)}, u32[]{:S(2)}) collective-permute-start(f32[4,4,32,256]{3,2,1,0:T(8,128)S(1)} %pad_maximum_fusion.1.refs_4_), channel_id=1, source_target_pairs={{0,4},{1,5},{2,6},{3,7},{4,0},{5,1},{6,2},{7,3},{8,12},{9,13},{10,... | collective-permute-start | bytes 1572872 | tf_op jit(solution)/shard_map/ppermute | solution.py:392
  216.3 16.0 %collective-permute-start.31 = (f32[2,4,32,128]{3,2,1,0:T(8,128)S(1)}, f32[2,4,32,128]{3,2,1,0:T(8,128)S(1)}, u32[]{:S(2)}, u32[]{:S(2)}) collective-permute-start(f32[2,4,32,128]{3,2,1,0:T(8,128)S(1)} %pad_maximum_fusion.2.refs_0_), channel_id=1, source_target_pairs={{0,3},{1,2},{2,1},{3,0},{4,7},{5,6},{6,5},{7,4},{8,11},{9,10},{10,... | collective-permute-start | bytes 393224 | tf_op jit(solution)/shard_map/ppermute | solution.py:392
  (42 other events, 794.6 us)

commit v6 on v5

--- a/solution.py
+++ b/solution.py
@@ -567,13 +567,17 @@
         ],
         axis=0,
     )
-    for g in range(cores):
-        for s in range(seqs):
-            scores = mm(q_ref[g, s, 0], k_ref[g, s]) + bias
-            top = jnp.max(scores, axis=1, keepdims=True)
-            ph, plo = split(jnp.exp(scores - top))
-            t = (mm(ph, v_ref[g, s]) + mm(plo, v_ref[g, s])).T
-            out_ref[0, g, s] = (t[0:hw] + t[hw:2 * hw]) / t[2 * hw:2 * hw + 1]
+    score = lambda g, s: mm(q_ref[g, s, 0], k_ref[g, s]) + bias
+    items = [(g, s) for s in range(seqs) for g in range(cores)]
+    ahead = score(*items[0])
+    for i, (g, s) in enumerate(items):
+        scores = ahead
+        if i + 1 < len(items):
+            ahead = score(*items[i + 1])
+        top = jnp.max(scores, axis=1, keepdims=True)
+        ph, plo = split(jnp.exp(scores - top))
+        t = (mm(ph, v_ref[g, s]) + mm(plo, v_ref[g, s])).T
+        out_ref[0, g, s] = (t[0:hw] + t[hw:2 * hw]) / t[2 * hw:2 * hw + 1]
 
 
 def head_attention(at, turn, q, k, v, tiles, prev, hw, step=2):
@@ -603,8 +607,7 @@
 def head_merge_kernel(heads, ids_ref, *refs):
     pieces = refs[:heads]
     gate_ref, x_ref, wm_ref, bm_ref, f1_ref, f2_ref = refs[heads:heads + 6]
-    next_ref, left_refs, right_ref = refs[heads + 6], refs[heads + 7:heads + 9], refs[heads + 9]
-    m_hi, m_lo, f_st = refs[heads + 10:]
+    next_ref, left_ref, right_ref, m_hi, m_lo, f_st = refs[heads + 6:]
     _, hw, span = pieces[0].shape
     hid = f1_ref.shape[0]
     rows = span // CORES
@@ -619,20 +622,21 @@
         f_st[0:2 * hid, :] = hi
         f_st[2 * hid:4 * hid, :] = lo
 
-    a = jnp.concatenate([p[0] for p in pieces], axis=0)
-    ah, al = split((a * gate_ref[0]).T)
-    y = x_ref[0] + (mm(ah, m_hi[...]) + mm(al, m_hi[...]) + mm(ah, m_lo[...])) + bm_ref[...]
-    next_ref[0] = y
-    zh, zl = split(norm_rows(y))
-    p = mm_nt(f_st[...], zh)
-    p = p[:2 * hid] + p[2 * hid:] + mm_nt(f_st[0:2 * hid, :], zl)
     swap = ids_ref[0] % CORES == 1
-    left_refs[0][0] = jnp.where(swap, p[:hid, rows:], p[:hid, :rows])
-    left_refs[1][0] = jnp.where(swap, p[:hid, :rows], p[:hid, rows:])
-    right_ref[0] = p[hid:]
-
-
-def head_merge(me, pieces, gate, x, wm, bm, f1, f2):
+    for s in range(x_ref.shape[0]):
+        a = jnp.concatenate([p[s] for p in pieces], axis=0)
+        ah, al = split((a * gate_ref[s]).T)
+        y = x_ref[s] + (mm(ah, m_hi[...]) + mm(al, m_hi[...]) + mm(ah, m_lo[...])) + bm_ref[...]
+        next_ref[s] = y
+        zh, zl = split(norm_rows(y))
+        p = mm_nt(f_st[...], zh)
+        p = p[:2 * hid] + p[2 * hid:] + mm_nt(f_st[0:2 * hid, :], zl)
+        left_ref[0, s] = jnp.where(swap, p[:hid, rows:], p[:hid, :rows])
+        left_ref[1, s] = jnp.where(swap, p[:hid, :rows], p[:hid, rows:])
+        right_ref[s] = p[hid:]
+
+
+def head_merge(me, pieces, gate, x, wm, bm, f1, f2, step=2):
     seqs, span, ch = x.shape
     heads = len(pieces)
     hw = ch // heads
@@ -642,20 +646,22 @@
     return pl.pallas_call(
         functools.partial(head_merge_kernel, heads),
         out_shape=(jax.ShapeDtypeStruct(x.shape, F32),)
-        + (jax.ShapeDtypeStruct((seqs, hid, rows), F32),) * CORES
+        + (jax.ShapeDtypeStruct((CORES, seqs, hid, rows), F32),)
         + (jax.ShapeDtypeStruct((seqs, hid, span), F32),),
         grid_spec=pltpu.PrefetchScalarGridSpec(
             num_scalar_prefetch=1,
-            grid=(seqs,),
-            in_specs=[pl.BlockSpec((1, hw, span), lambda s, _: (s, 0, 0)) for _ in pieces]
+            grid=(seqs // step,),
+            in_specs=[pl.BlockSpec((step, hw, span), lambda s, _: (s, 0, 0)) for _ in pieces]
             + [
-                pl.BlockSpec((1, ch, span), lambda s, _: (s, 0, 0)),
-                pl.BlockSpec((1, span, ch), lambda s, _: (s, 0, 0)),
+                pl.BlockSpec((step, ch, span), lambda s, _: (s, 0, 0)),
+                pl.BlockSpec((step, span, ch), lambda s, _: (s, 0, 0)),
             ]
             + [whole(a) for a in (wm, bm, f1, f2)],
-            out_specs=(pl.BlockSpec((1, span, ch), lambda s, _: (s, 0, 0)),)
-            + (pl.BlockSpec((1, hid, rows), lambda s, _: (s, 0, 0)),) * CORES
-            + (pl.BlockSpec((1, hid, span), lambda s, _: (s, 0, 0)),),
+            out_specs=(
+                pl.BlockSpec((step, span, ch), lambda s, _: (s, 0, 0)),
+                pl.BlockSpec((CORES, step, hid, rows), lambda s, _: (0, s, 0, 0)),
+                pl.BlockSpec((step, hid, span), lambda s, _: (s, 0, 0)),
+            ),
             scratch_shapes=[
                 pltpu.VMEM((ch, ch), BF16),
                 pltpu.VMEM((ch, ch), BF16),
@@ -756,14 +762,14 @@
     for i, tile in enumerate(((bias,), (near,), second, third)):
         att = head_attention(at, i, q, k, v, tile, att, hw)
     pieces = exchange([att[p, r] for p in range(parts) for r in range(CORES)], parts)
-    alignment_state_next, left_a, left_b, right = head_merge(
+    alignment_state_next, left, right = head_merge(
         ids, pieces, gate, homolog_embedding, mixing_projector, mixing_offset,
         first_factor_projector.T, second_factor_projector.T,
     )
     turn = lambda z0, c0, n0: (n0, c0, z0)
-    left_b, left_a = send(left_b, parts, turn), send(left_a, parts, turn)
+    left = send(left, parts, turn)
     sibling = lambda z0, c0, n0: (z0, c0 ^ 1, n0)
-    left = jnp.stack([left_a, send(left_b, parts, sibling)])
+    left = jnp.stack([left[0], send(left[1], parts, sibling)])
     rights = [right] + [send(right, parts, lambda z0, c0, n0, d=d: (z0 ^ d, c0, n0)) for d in range(1, PLANES)]
     lefts = [left] + [send(left, parts, lambda z0, c0, n0, d=d: (z0, c0, n0 ^ d)) for d in range(1, parts)]
     own = jnp.stack(rights)

time: 324 us -> 312 us (0.963)
  starting transfers between devices: 74.4 us -> 64.5 us
  Pallas kernels: 156 us -> 151 us
    ppermute x36 -> x35, starting transfers between devices: 74.4 us -> 64.5 us  [send(): return lax.ppermute(x, AXES, pairs)]
    pallas_call x4, Pallas kernels: 36.3 us -> 31.9 us  [head_attention(): pl.pallas_call(functools.partial(head_attention_kernel, hw, turn, len(til...]
    ppermute x36 -> x35, waiting for transfers between devices: 77.4 us -> 80.2 us  [send(): return lax.ppermute(x, AXES, pairs)]
  transfers between devices with their start and end apart: 36 -> 35, of which waited for: 16 -> 16; matrix products, arithmetic and copies ran while one was open for 2% -> 2% of each run, Pallas kernels for 12% -> 12%
where the time goes in v6:
time: 312 us; the launch traced here: 311 us
  Pallas kernels  151 us (48%)
  waiting for transfers between devices  80.2 us (26%)
  starting transfers between devices  64.5 us (21%)
  local copies, waits for them, and re-layouts  7.37 us (2%)
  between operations  4.16 us (1%)
  other arithmetic  3.46 us (1%)
    pallas_call x1, Pallas kernels, pair_update(): pl.pallas_call(functools.partial(pair_kernel, step_rows, group, seqs), ou...  82.2 us
    ppermute x35, waiting for transfers between devices, send(): return lax.ppermute(x, AXES, pairs)  80.2 us
    ppermute x35, starting transfers between devices, send(): return lax.ppermute(x, AXES, pairs)  64.5 us
    pallas_call x4, Pallas kernels, head_attention(): pl.pallas_call(functools.partial(head_attention_kernel, hw, turn, len(til...  31.9 us
    pallas_call x1, Pallas kernels, head_bias(): pl.pallas_call(functools.partial(head_bias_kernel, group), out_shape=(jax...  13.6 us
    pallas_call x1, Pallas kernels, head_project(): pl.pallas_call(functools.partial(head_project_kernel, heads, 1.0 / math.s...  7.14 us
  transfers between devices with their start and end apart: 35, of which 16 were waited for; matrix products, arithmetic and copies ran while one was open for 2% of the time, Pallas kernels for 12%

profile of v6, /device:TPU:0, one launch (start us, length us, event | category | flops | bytes accessed | tf_op | source)
XLA Modules:
  0.0 311.0 jit_solution(7040344946590799764)
XLA Ops:
  1.2 13.6 %head_bias.1 = (f32[128,256]{1,0:T(8,128)}, f32[128,256]{1,0:T(8,128)}, f32[128,256]{1,0:T(8,128)}, f32[128,256]{1,0:T(8,128)}, f32[128,256]{1,0:T(8,128)}, /*in...) custom-call(s32[2]{0:T(128)} %pad_add_fusion.ids_ref, f32[128,256,128]{2,1,0:T(8,128)} %pair_ref.3, ...), custom_call_target="tpu_custom_call" | custom-call | tf_op jit(solution)/shard_map/head_bias/pallas_call | solution.py:442
  15.4 2.6 collective-permute-start.1
  23.5 2.7 collective-permute-start.5
  29.1 7.1 %head_project.1 = (f32[3,4,32,256]{3,2,1,0:T(8,128)}, f32[3,4,32,256]{3,2,1,0:T(8,128)}, f32[3,4,32,256]{3,2,1,0:T(8,128)}, f32[3,4,32,256]{3,2,1,0:T(8,128)}, f...) custom-call(s32[2]{0:T(128)} %pad_add_fusion.ids_ref, ...), custom_call_target="tpu_custom_call" | custom-call | tf_op jit(solution)/shard_map/head_project/pallas_call | solution.py:489
  40.0 22.0 %collective-permute-done.7.refs_0_ = f32[2,4,128,256]{3,2,1,0:T(8,128)S(1)} collective-permute-done((f32[2,4,128,256]{3,2,1,0:T(8,128)S(1)}, f32[2,4,128,256]{3,2,1,0:T(8,128)S(1)}, u32[]{:S(2)}, u32[]{:S(2)}) %collective-permute-start.7) | collective-permute-done | bytes 1048608 | tf_op jit(solution)/shard_map/ppermute | solution.py:392
  69.3 8.4 %collective-permute-done.10.refs_2_ = f32[3,4,32,256]{3,2,1,0:T(8,128)S(1)} collective-permute-done((f32[3,4,32,256]{3,2,1,0:T(8,128)S(1)}, f32[3,4,32,256]{3,2,1,0:T(8,128)S(1)}, u32[]{:S(2)}, u32[]{:S(2)}) %collective-permute-start.10) | collective-permute-done | bytes 393248 | tf_op jit(solution)/shard_map/ppermute | solution.py:392
  78.3 7.0 %collective-permute-done.11.refs_3_ = f32[3,4,32,256]{3,2,1,0:T(8,128)} collective-permute-done((f32[3,4,32,256]{3,2,1,0:T(8,128)S(1)}, f32[3,4,32,256]{3,2,1,0:T(8,128)}, u32[]{:S(2)}, u32[]{:S(2)}) %collective-permute-start.11) | collective-permute-done | bytes 393248 | tf_op jit(solution)/shard_map/ppermute | solution.py:392
  85.3 2.6 collective-permute-start.14
  89.0 9.3 %collective-permute-done.14.refs_6_ = f32[3,4,32,256]{3,2,1,0:T(8,128)} collective-permute-done((f32[3,4,32,256]{3,2,1,0:T(8,128)S(1)}, f32[3,4,32,256]{3,2,1,0:T(8,128)}, u32[]{:S(2)}, u32[]{:S(2)}) %collective-permute-start.14) | collective-permute-done | bytes 393248 | tf_op jit(solution)/shard_map/ppermute | solution.py:392
  98.3 7.7 %collective-permute-done.15.refs_7_ = f32[3,4,32,256]{3,2,1,0:T(8,128)} collective-permute-done((f32[3,4,32,256]{3,2,1,0:T(8,128)S(1)}, f32[3,4,32,256]{3,2,1,0:T(8,128)}, u32[]{:S(2)}, u32[]{:S(2)}) %collective-permute-start.15) | collective-permute-done | bytes 393248 | tf_op jit(solution)/shard_map/ppermute | solution.py:392
  106.5 5.8 %stage.1 = (bf16[2,4,4,256,128]{4,3,2,1,0:T(8,128)(2,1)}, bf16[2,4,128,1024]{3,2,1,0:T(8,128)(2,1)}, bf16[2,4,1024,128]{3,2,1,0:T(8,128)(2,1)}) custom-call(s32[1]{0:T(128)S(6)} %add.13.n_ref, f32[3,4,32,256]{3,2,1,0:T(8,128)} %get-tuple-element.91.refs_0_, f32[3,4,32,256]{3,2,1,0:T(8,128)} %copy-done.7, f32[3,4,32,256]{3,2,1,0:T(8,128)} %copy-done.8, ...), custom_call_target="tpu_custom_call" | custom-call | tf_op jit(solution)/shard_map/stage/pallas_call | solution.py:536
  112.3 7.7 %head_attention.4.refs_1_ = f32[4,2,4,32,256]{4,3,2,1,0:T(8,128)} custom-call(s32[12]{0:T(128)} %reshape.32.at_ref, bf16[2,4,4,256,128]{4,3,2,1,0:T(8,128)(2,1)} %get-tuple-element.99.q_ref, bf16[2,4,128,1024]{3,2,1,0:T(8,128)(2,1)} %get-tuple-element.100.k_ref, bf16[2,4,1024,128]{3,2,1,0:T(8,128)(2,1)} %get-tuple-element.101.v_ref, f32[2,4,128,256]{3,2,1,0:T(8,128)} %copy-done), custom_call_target="tpu_custom_call" | custom-call | tf_op jit(solution)/shard_map/head_attention/pallas_call | solution.py:586
  120.1 7.7 %head_attention.5.refs_2_ = f32[4,2,4,32,256]{4,3,2,1,0:T(8,128)} custom-call(s32[12]{0:T(128)} %reshape.32.at_ref, bf16[2,4,4,256,128]{4,3,2,1,0:T(8,128)(2,1)} %get-tuple-element.99.q_ref, bf16[2,4,128,1024]{3,2,1,0:T(8,128)(2,1)} %get-tuple-element.100.k_ref, bf16[2,4,1024,128]{3,2,1,0:T(8,128)(2,1)} %get-tuple-element.101.v_ref, ...), custom_call_target="tpu_custom_call", output_to_operand_aliasing={{}: (5, {})} | custom-call | tf_op jit(solution)/shard_map/head_attention/pallas_call | solution.py:586
  127.8 8.2 %head_attention.6.refs_2_ = f32[4,2,4,32,256]{4,3,2,1,0:T(8,128)} custom-call(s32[12]{0:T(128)} %reshape.32.at_ref, bf16[2,4,4,256,128]{4,3,2,1,0:T(8,128)(2,1)} %get-tuple-element.99.q_ref, bf16[2,4,128,1024]{3,2,1,0:T(8,128)(2,1)} %get-tuple-element.100.k_ref, bf16[2,4,1024,128]{3,2,1,0:T(8,128)(2,1)} %get-tuple-element.101.v_ref, ...), custom_call_target="tpu_custom_call", output_to_operand_aliasing={{}: (6, {})} | custom-call | tf_op jit(solution)/shard_map/head_attention/pallas_call | solution.py:586
  136.0 8.2 %head_attention.7 = f32[4,2,4,32,256]{4,3,2,1,0:T(8,128)} custom-call(s32[12]{0:T(128)} %reshape.32.at_ref, bf16[2,4,4,256,128]{4,3,2,1,0:T(8,128)(2,1)} %get-tuple-element.99.q_ref, bf16[2,4,128,1024]{3,2,1,0:T(8,128)(2,1)} %get-tuple-element.100.k_ref, bf16[2,4,1024,128]{3,2,1,0:T(8,128)(2,1)} %get-tuple-element.101.v_ref, ...), custom_call_target="tpu_custom_call", output_to_operand_aliasing={{}: (6, {})} | custom-call | tf_op jit(solution)/shard_map/head_attention/pallas_call | solution.py:586
  158.6 2.8 collective-permute-done.22.refs_4_
  162.4 6.1 %head_merge.1 = (f32[4,256,256]{2,1,0:T(8,128)}, f32[2,4,32,128]{3,2,1,0:T(8,128)}, f32[4,32,256]{2,1,0:T(8,128)}) custom-call(s32[2]{0:T(128)} %pad_add_fusion.ids_ref, f32[4,32,256]{2,1,0:T(8,128)} %get-tuple-element.115.refs_0_, f32[4,32,256]{2,1,0:T(8,128)} %copy-done.16, f32[4,32,256]{2,1,0:T(8,128)} %copy-done.15, f32[4,32,256]{2,1,0:T(8,128)} %copy-done.14, ...), custom_call_target="tpu_custom_call" | custom-call | tf_op jit(solution)/shard_map/head_merge/pallas_call | solution.py:646
  168.5 3.7 %collective-permute-start.33 = (f32[4,32,256]{2,1,0:T(8,128)}, f32[4,32,256]{2,1,0:T(8,128)S(1)}, u32[]{:S(2)}, u32[]{:S(2)}) collective-permute-start(f32[4,32,256]{2,1,0:T(8,128)} %get-tuple-element.105), channel_id=1, source_target_pairs={{0,24},{1,25},{2,26},{3,27},{4,28},{5,29},{6,30},{7,31},{8,16},{9,... | collective-permute-start | bytes 393224 | tf_op jit(solution)/shard_map/ppermute | solution.py:392
  172.1 24.6 %collective-permute-start.32 = (f32[4,32,256]{2,1,0:T(8,128)}, f32[4,32,256]{2,1,0:T(8,128)S(1)}, u32[]{:S(2)}, u32[]{:S(2)}) collective-permute-start(f32[4,32,256]{2,1,0:T(8,128)} %get-tuple-element.105), channel_id=1, source_target_pairs={{0,16},{1,17},{2,18},{3,19},{4,20},{5,21},{6,22},{7,23},{8,24},{9,... | collective-permute-start | bytes 393224 | tf_op jit(solution)/shard_map/ppermute | solution.py:392
  198.5 11.4 %collective-permute-done.32 = f32[4,32,256]{2,1,0:T(8,128)S(1)} collective-permute-done((f32[4,32,256]{2,1,0:T(8,128)}, f32[4,32,256]{2,1,0:T(8,128)S(1)}, u32[]{:S(2)}, u32[]{:S(2)}) %collective-permute-start.32) | collective-permute-done | bytes 131104 | tf_op jit(solution)/shard_map/ppermute | solution.py:392
  213.0 4.5 %collective-permute-start.29 = (f32[2,4,32,128]{3,2,1,0:T(8,128)S(1)}, f32[2,4,32,128]{3,2,1,0:T(8,128)S(1)}, u32[]{:S(2)}, u32[]{:S(2)}) collective-permute-start(f32[2,4,32,128]{3,2,1,0:T(8,128)S(1)} %pad_maximum_fusion.2.refs_0_), channel_id=1, source_target_pairs={{0,2},{1,3},{2,0},{3,1},{4,6},{5,7},{6,4},{7,5},{8,10},{9,11},{10,... | collective-permute-start | bytes 393224 | tf_op jit(solution)/shard_map/ppermute | solution.py:392
  219.5 2.7 collective-permute-done.29.refs_2_
  224.1 4.7 %pack.1 = (f32[4096,32]{1,0:T(8,128)}, f32[256,1024]{1,0:T(8,128)}) custom-call(s32[4]{0:T(128)} %xor_xor_fusion.slots_ref, f32[2,4,32,128]{3,2,1,0:T(8,128)} %copy-done.4, f32[2,4,32,128]{3,2,1,0:T(8,128)} %copy-done.19, f32[2,4,32,128]{3,2,1,0:T(8,128)} %copy-done.18, f32[2,4,32,128]{3,2,1,0:T(8,128)} %copy-done.17, f32[4,4,32,256]{3,2,1,0:T(8,128)} %copy-done.1, ...), custom_call_target="tpu_custom_call" | custom-call | tf_op jit(solution)/shard_map/pack/pallas_call | solution.py:697
  228.8 82.2 %pair_update.1 = f32[128,256,128]{2,1,0:T(8,128)} custom-call(f32[4096,32]{1,0:T(8,128)} %get-tuple-element.106.left_ref, f32[256,1024]{1,0:T(8,128)} %get-tuple-element.107.right_ref, f32[32,4096]{1,0:T(8,128)} %reshape.35.w_ref, f32[128,256,128]{2,1,0:T(8,128)} %pair_ref.3, f32[1,128]{1,0:T(1,128)} %bitcast.70, f32[128,512]{1,0:T(8,128)} %up_ref.1, ...), custom_call_target="tpu_custom_call" | custom-call | tf_op jit(solution)/shard_map/pair_update/pallas_call | solution.py:295
  (133 shorter events, 43.5 us)
Async XLA Ops:
  15.4 10.9 %collective-permute-start.1 = (f32[128,256]{1,0:T(8,128)}, f32[128,256]{1,0:T(8,128)S(1)}, u32[]{:S(2)}, u32[]{:S(2)}) collective-permute-start(f32[128,256]{1,0:T(8,128)} %get-tuple-element.58), channel_id=1, source_target_pairs={{0,1},{1,0},{2,3},{3,2},{4,5},{5,4},{6,7},{7,6},{8,9},{9,8},{10,11... | collective-permute-start | bytes 393224 | tf_op jit(solution)/shard_map/ppermute | solution.py:392
  17.9 18.3 %collective-permute-start.2 = (f32[128,256]{1,0:T(8,128)}, f32[128,256]{1,0:T(8,128)S(1)}, u32[]{:S(2)}, u32[]{:S(2)}) collective-permute-start(f32[128,256]{1,0:T(8,128)} %get-tuple-element.59), channel_id=1, source_target_pairs={{0,5},{1,4},{2,7},{3,6},{4,1},{5,0},{6,3},{7,2},{8,13},{9,12},{10,... | collective-permute-start | bytes 393224 | tf_op jit(solution)/shard_map/ppermute | solution.py:392
  18.0 18.3 %collective-permute-start.3 = (f32[128,256]{1,0:T(8,128)}, f32[128,256]{1,0:T(8,128)S(1)}, u32[]{:S(2)}, u32[]{:S(2)}) collective-permute-start(f32[128,256]{1,0:T(8,128)} %get-tuple-element.60), channel_id=1, source_target_pairs={{0,2},{1,3},{2,0},{3,1},{4,6},{5,7},{6,4},{7,5},{8,10},{9,11},{10,... | collective-permute-start | bytes 393224 | tf_op jit(solution)/shard_map/ppermute | solution.py:392
  19.7 16.5 %collective-permute-start.4 = (f32[128,256]{1,0:T(8,128)}, f32[128,256]{1,0:T(8,128)S(1)}, u32[]{:S(2)}, u32[]{:S(2)}) collective-permute-start(f32[128,256]{1,0:T(8,128)} %get-tuple-element.61), channel_id=1, source_target_pairs={{0,6},{1,7},{2,4},{3,5},{4,2},{5,3},{6,0},{7,1},{8,14},{9,15},{10,... | collective-permute-start | bytes 393224 | tf_op jit(solution)/shard_map/ppermute | solution.py:392
  23.5 12.7 %collective-permute-start.5 = (f32[128,256]{1,0:T(8,128)}, f32[128,256]{1,0:T(8,128)S(1)}, u32[]{:S(2)}, u32[]{:S(2)}) collective-permute-start(f32[128,256]{1,0:T(8,128)} %get-tuple-element.62), channel_id=1, source_target_pairs={{0,3},{1,2},{2,1},{3,0},{4,7},{5,6},{6,5},{7,4},{8,11},{9,10},{10,... | collective-permute-start | bytes 393224 | tf_op jit(solution)/shard_map/ppermute | solution.py:392
  26.2 10.1 %collective-permute-start.6 = (f32[128,256]{1,0:T(8,128)}, f32[128,256]{1,0:T(8,128)S(1)}, u32[]{:S(2)}, u32[]{:S(2)}) collective-permute-start(f32[128,256]{1,0:T(8,128)} %get-tuple-element.63), channel_id=1, source_target_pairs={{0,7},{1,6},{2,5},{3,4},{4,3},{5,2},{6,1},{7,0},{8,15},{9,14},{10,... | collective-permute-start | bytes 393224 | tf_op jit(solution)/shard_map/ppermute | solution.py:392
  36.6 25.4 %collective-permute-start.7 = (f32[2,4,128,256]{3,2,1,0:T(8,128)S(1)}, f32[2,4,128,256]{3,2,1,0:T(8,128)S(1)}, u32[]{:S(2)}, u32[]{:S(2)}) collective-permute-start(f32[2,4,128,256]{3,2,1,0:T(8,128)S(1)} %pad_maximum_fusion.refs_0_), channel_id=1, source_target_pairs={{0,8},{1,9},{2,10},{3,11},{4,12},{5,13},{6,14},{7,15},{8,0},{9,1},... | collective-permute-start | bytes 3145736 | tf_op jit(solution)/shard_map/ppermute | solution.py:392
  38.3 24.5 %collective-permute-start.8 = (f32[2,4,128,256]{3,2,1,0:T(8,128)S(1)}, f32[2,4,128,256]{3,2,1,0:T(8,128)}, u32[]{:S(2)}, u32[]{:S(2)}) collective-permute-start(f32[2,4,128,256]{3,2,1,0:T(8,128)S(1)} %pad_maximum_fusion.refs_0_), channel_id=1, source_target_pairs={{8,16},{9,17},{10,18},{11,19},{12,20},{13,21},{14,22},{15,23},{16,... | collective-permute-start | bytes 3145736 | tf_op jit(solution)/shard_map/ppermute | solution.py:392
  62.9 49.5 %collective-permute-start.18 = (f32[2,4,128,256]{3,2,1,0:T(8,128)}, f32[2,4,128,256]{3,2,1,0:T(8,128)}, u32[]{:S(2)}, u32[]{:S(2)}) collective-permute-start(f32[2,4,128,256]{3,2,1,0:T(8,128)} %collective-permute-done.8.refs_0_), channel_id=1, source_target_pairs={{8,0},{9,1},{10,2},{11,3},{12,4},{13,5},{14,6},{15,7},{16,24},{17,... | collective-permute-start | bytes 3145736 | tf_op jit(solution)/shard_map/ppermute | solution.py:392
  64.2 71.9 %collective-permute-start.17 = (f32[2,4,128,256]{3,2,1,0:T(8,128)S(1)}, f32[2,4,128,256]{3,2,1,0:T(8,128)}, u32[]{:S(2)}, u32[]{:S(2)}) collective-permute-start(f32[2,4,128,256]{3,2,1,0:T(8,128)S(1)} %collective-permute-done.16.refs_0_), channel_id=1, source_target_pairs={{8,0},{9,1},{10,2},{11,3},{12,4},{13,5},{14,6},{15,7},{16,24},{17,... | collective-permute-start | bytes 3145736 | tf_op jit(solution)/shard_map/ppermute | solution.py:392
  65.7 12.1 %collective-permute-start.10 = (f32[3,4,32,256]{3,2,1,0:T(8,128)S(1)}, f32[3,4,32,256]{3,2,1,0:T(8,128)S(1)}, u32[]{:S(2)}, u32[]{:S(2)}) collective-permute-start(f32[3,4,32,256]{3,2,1,0:T(8,128)S(1)} %copy-done.28), channel_id=1, source_target_pairs={{0,1},{1,0},{2,3},{3,2},{4,5},{5,4},{6,7},{7,6},{8,9},{9,8},{10,11... | collective-permute-start | bytes 1179656 | tf_op jit(solution)/shard_map/ppermute | solution.py:392
  67.4 17.9 %collective-permute-start.11 = (f32[3,4,32,256]{3,2,1,0:T(8,128)S(1)}, f32[3,4,32,256]{3,2,1,0:T(8,128)}, u32[]{:S(2)}, u32[]{:S(2)}) collective-permute-start(f32[3,4,32,256]{3,2,1,0:T(8,128)S(1)} %copy-done.27), channel_id=1, source_target_pairs={{0,5},{1,4},{2,7},{3,6},{4,1},{5,0},{6,3},{7,2},{8,13},{9,12},{10,... | collective-permute-start | bytes 1179656 | tf_op jit(solution)/shard_map/ppermute | solution.py:392
  67.6 20.3 %collective-permute-start.12 = (f32[3,4,32,256]{3,2,1,0:T(8,128)S(1)}, f32[3,4,32,256]{3,2,1,0:T(8,128)}, u32[]{:S(2)}, u32[]{:S(2)}) collective-permute-start(f32[3,4,32,256]{3,2,1,0:T(8,128)S(1)} %copy-done.26), channel_id=1, source_target_pairs={{0,2},{1,3},{2,0},{3,1},{4,6},{5,7},{6,4},{7,5},{8,10},{9,11},{10,... | collective-permute-start | bytes 1179656 | tf_op jit(solution)/shard_map/ppermute | solution.py:392
  77.7 11.3 %collective-permute-start.13 = (f32[3,4,32,256]{3,2,1,0:T(8,128)S(1)}, f32[3,4,32,256]{3,2,1,0:T(8,128)}, u32[]{:S(2)}, u32[]{:S(2)}) collective-permute-start(f32[3,4,32,256]{3,2,1,0:T(8,128)S(1)} %copy-done.25), channel_id=1, source_target_pairs={{0,6},{1,7},{2,4},{3,5},{4,2},{5,3},{6,0},{7,1},{8,14},{9,15},{10,... | collective-permute-start | bytes 1179656 | tf_op jit(solution)/shard_map/ppermute | solution.py:392
  85.3 13.0 %collective-permute-start.14 = (f32[3,4,32,256]{3,2,1,0:T(8,128)S(1)}, f32[3,4,32,256]{3,2,1,0:T(8,128)}, u32[]{:S(2)}, u32[]{:S(2)}) collective-permute-start(f32[3,4,32,256]{3,2,1,0:T(8,128)S(1)} %copy-done.24), channel_id=1, source_target_pairs={{0,3},{1,2},{2,1},{3,0},{4,7},{5,6},{6,5},{7,4},{8,11},{9,10},{10,... | collective-permute-start | bytes 1179656 | tf_op jit(solution)/shard_map/ppermute | solution.py:392
  87.9 18.1 %collective-permute-start.15 = (f32[3,4,32,256]{3,2,1,0:T(8,128)S(1)}, f32[3,4,32,256]{3,2,1,0:T(8,128)}, u32[]{:S(2)}, u32[]{:S(2)}) collective-permute-start(f32[3,4,32,256]{3,2,1,0:T(8,128)S(1)} %copy-done.23), channel_id=1, source_target_pairs={{0,7},{1,6},{2,5},{3,4},{4,3},{5,2},{6,1},{7,0},{8,15},{9,14},{10,... | collective-permute-start | bytes 1179656 | tf_op jit(solution)/shard_map/ppermute | solution.py:392
  149.0 9.6 %collective-permute-start.23 = (f32[4,32,256]{2,1,0:T(8,128)S(1)}, f32[4,32,256]{2,1,0:T(8,128)S(1)}, u32[]{:S(2)}, u32[]{:S(2)}) collective-permute-start(f32[4,32,256]{2,1,0:T(8,128)S(1)} %get-tuple-element.110), channel_id=1, source_target_pairs={{0,6},{1,7},{2,4},{3,5},{4,2},{5,3},{6,0},{7,1},{8,14},{9,15},{10,... | collective-permute-start | bytes 393224 | tf_op jit(solution)/shard_map/ppermute | solution.py:392
  150.4 11.1 %collective-permute-start.22 = (f32[4,32,256]{2,1,0:T(8,128)S(1)}, f32[4,32,256]{2,1,0:T(8,128)S(1)}, u32[]{:S(2)}, u32[]{:S(2)}) collective-permute-start(f32[4,32,256]{2,1,0:T(8,128)S(1)} %get-tuple-element.111), channel_id=1, source_target_pairs={{0,2},{1,3},{2,0},{3,1},{4,6},{5,7},{6,4},{7,5},{8,10},{9,11},{10,... | collective-permute-start | bytes 393224 | tf_op jit(solution)/shard_map/ppermute | solution.py:392
  150.7 10.7 %collective-permute-start.21 = (f32[4,32,256]{2,1,0:T(8,128)S(1)}, f32[4,32,256]{2,1,0:T(8,128)S(1)}, u32[]{:S(2)}, u32[]{:S(2)}) collective-permute-start(f32[4,32,256]{2,1,0:T(8,128)S(1)} %get-tuple-element.112), channel_id=1, source_target_pairs={{0,5},{1,4},{2,7},{3,6},{4,1},{5,0},{6,3},{7,2},{8,13},{9,12},{10,... | collective-permute-start | bytes 393224 | tf_op jit(solution)/shard_map/ppermute | solution.py:392
  168.5 30.0 %collective-permute-start.33 = (f32[4,32,256]{2,1,0:T(8,128)}, f32[4,32,256]{2,1,0:T(8,128)S(1)}, u32[]{:S(2)}, u32[]{:S(2)}) collective-permute-start(f32[4,32,256]{2,1,0:T(8,128)} %get-tuple-element.105), channel_id=1, source_target_pairs={{0,24},{1,25},{2,26},{3,27},{4,28},{5,29},{6,30},{7,31},{8,16},{9,... | collective-permute-start | bytes 393224 | tf_op jit(solution)/shard_map/ppermute | solution.py:392
  172.1 37.7 %collective-permute-start.32 = (f32[4,32,256]{2,1,0:T(8,128)}, f32[4,32,256]{2,1,0:T(8,128)S(1)}, u32[]{:S(2)}, u32[]{:S(2)}) collective-permute-start(f32[4,32,256]{2,1,0:T(8,128)} %get-tuple-element.105), channel_id=1, source_target_pairs={{0,16},{1,17},{2,18},{3,19},{4,20},{5,21},{6,22},{7,23},{8,24},{9,... | collective-permute-start | bytes 393224 | tf_op jit(solution)/shard_map/ppermute | solution.py:392
  196.8 13.1 %collective-permute-start.31 = (f32[4,32,256]{2,1,0:T(8,128)}, f32[4,32,256]{2,1,0:T(8,128)S(1)}, u32[]{:S(2)}, u32[]{:S(2)}) collective-permute-start(f32[4,32,256]{2,1,0:T(8,128)} %get-tuple-element.105), channel_id=1, source_target_pairs={{0,8},{1,9},{2,10},{3,11},{4,12},{5,13},{6,14},{7,15},{8,0},{9,1},... | collective-permute-start | bytes 393224 | tf_op jit(solution)/shard_map/ppermute | solution.py:392
  196.9 14.0 %collective-permute-start.26 = (f32[2,4,32,128]{3,2,1,0:T(8,128)}, f32[2,4,32,128]{3,2,1,0:T(8,128)S(1)}, u32[]{:S(2)}, u32[]{:S(2)}) collective-permute-start(f32[2,4,32,128]{3,2,1,0:T(8,128)} %get-tuple-element.104), channel_id=1, source_target_pairs={{0,0},{1,8},{2,16},{3,24},{4,4},{5,12},{6,20},{7,28},{8,1},{9,9},{... | collective-permute-start | bytes 393224 | tf_op jit(solution)/shard_map/ppermute | solution.py:392
  210.8 11.9 %collective-permute-start.34 = (f32[4,4,32,256]{3,2,1,0:T(8,128)S(1)}, f32[4,4,32,256]{3,2,1,0:T(8,128)S(1)}, u32[]{:S(2)}, u32[]{:S(2)}) collective-permute-start(f32[4,4,32,256]{3,2,1,0:T(8,128)S(1)} %pad_maximum_fusion.1.refs_4_), channel_id=1, source_target_pairs={{0,4},{1,5},{2,6},{3,7},{4,0},{5,1},{6,2},{7,3},{8,12},{9,13},{10,... | collective-permute-start | bytes 1572872 | tf_op jit(solution)/shard_map/ppermute | solution.py:392
  (41 other events, 773.5 us)

commit v7 on v6

--- a/solution.py
+++ b/solution.py
@@ -230,33 +230,14 @@
     )(*att, gate, x, wm, bm, f1, f2)
 
 
-def pair_kernel(
-    step_rows, group, seqs, left_ref, right_ref, w_ref, pair_ref, ob_ref, up_ref, eb_ref, dn_ref,
-    out_ref, r_hi, r_lo, w_st, up_st, dn_st,
+def pair_rows(
+    step_rows, group, seqs, first, left_ref, pair_ref, ob_ref, eb_ref, out_ref, r_hi, r_lo, w_st, up_st, dn_st
 ):
     _, cols, cz = pair_ref.shape
-    c_n = w_ref.shape[0]
-    d_n = w_ref.shape[1] // cz
-
-    @pl.when(pl.program_id(0) == 0)
-    def _():
-        hi, lo = split(right_ref[...])
-        r_hi[...] = hi
-        r_lo[...] = lo
-        hi, lo = split(w_ref[...])
-        w_st[0:c_n, :] = hi
-        w_st[c_n:2 * c_n, :] = lo
-        w_st[2 * c_n:3 * c_n, :] = hi
-        hi, lo = split(up_ref[...])
-        up_st[0:cz, :] = hi
-        up_st[cz:2 * cz, :] = hi
-        up_st[2 * cz:3 * cz, :] = lo
-        hi, lo = split(dn_ref[...])
-        dn_st[:, 0:cz] = hi
-        dn_st[:, cz:2 * cz] = lo
+    d_n = w_st.shape[1] // cz
 
     def body(p, carry):
-        lrow = left_ref[pl.ds(pl.multiple_of(p * group * seqs, group * seqs), group * seqs), :]
+        lrow = left_ref[pl.ds(pl.multiple_of((first + p * group) * seqs, group * seqs), group * seqs), :]
         lhi = lrow.astype(BF16).astype(F32)
         u = mm(jnp.concatenate([lhi, lhi, lrow - lhi], axis=1).astype(BF16), w_st[...])
         his, los = [], []
@@ -284,6 +265,36 @@
         return carry
 
     lax.fori_loop(0, step_rows // group, body, 0)
+
+
+def pair_weights(w_ref, up_ref, dn_ref, w_st, up_st, dn_st):
+    c_n = w_ref.shape[0]
+    cz = up_ref.shape[0]
+    hi, lo = split(w_ref[...])
+    w_st[0:c_n, :] = hi
+    w_st[c_n:2 * c_n, :] = lo
+    w_st[2 * c_n:3 * c_n, :] = hi
+    hi, lo = split(up_ref[...])
+    up_st[0:cz, :] = hi
+    up_st[cz:2 * cz, :] = hi
+    up_st[2 * cz:3 * cz, :] = lo
+    hi, lo = split(dn_ref[...])
+    dn_st[:, 0:cz] = hi
+    dn_st[:, cz:2 * cz] = lo
+
+
+def pair_kernel(
+    step_rows, group, seqs, left_ref, right_ref, w_ref, pair_ref, ob_ref, up_ref, eb_ref, dn_ref,
+    out_ref, r_hi, r_lo, w_st, up_st, dn_st,
+):
+    @pl.when(pl.program_id(0) == 0)
+    def _():
+        r_hi[...], r_lo[...] = split(right_ref[...])
+        pair_weights(w_ref, up_ref, dn_ref, w_st, up_st, dn_st)
+
+    pair_rows(
+        step_rows, group, seqs, 0, left_ref, pair_ref, ob_ref, eb_ref, out_ref, r_hi, r_lo, w_st, up_st, dn_st
+    )
 
 
 def pair_update(left_rows, right_cols, w2, pair, ob, up, eb, dn, step_rows=8, group=4):
@@ -607,7 +618,7 @@
 def head_merge_kernel(heads, ids_ref, *refs):
     pieces = refs[:heads]
     gate_ref, x_ref, wm_ref, bm_ref, f1_ref, f2_ref = refs[heads:heads + 6]
-    next_ref, left_ref, right_ref, m_hi, m_lo, f_st = refs[heads + 6:]
+    next_ref, left_a, left_b, right_ref, m_hi, m_lo, f_st = refs[heads + 6:]
     _, hw, span = pieces[0].shape
     hid = f1_ref.shape[0]
     rows = span // CORES
@@ -631,8 +642,8 @@
         zh, zl = split(norm_rows(y))
         p = mm_nt(f_st[...], zh)
         p = p[:2 * hid] + p[2 * hid:] + mm_nt(f_st[0:2 * hid, :], zl)
-        left_ref[0, s] = jnp.where(swap, p[:hid, rows:], p[:hid, :rows])
-        left_ref[1, s] = jnp.where(swap, p[:hid, :rows], p[:hid, rows:])
+        left_a[s] = jnp.where(swap, p[:hid, rows:], p[:hid, :rows])
+        left_b[s] = jnp.where(swap, p[:hid, :rows], p[:hid, rows:])
         right_ref[s] = p[hid:]
 
 
@@ -646,7 +657,7 @@
     return pl.pallas_call(
         functools.partial(head_merge_kernel, heads),
         out_shape=(jax.ShapeDtypeStruct(x.shape, F32),)
-        + (jax.ShapeDtypeStruct((CORES, seqs, hid, rows), F32),)
+        + (jax.ShapeDtypeStruct((seqs, hid, rows), F32),) * CORES
         + (jax.ShapeDtypeStruct((seqs, hid, span), F32),),
         grid_spec=pltpu.PrefetchScalarGridSpec(
             num_scalar_prefetch=1,
@@ -659,7 +670,8 @@
             + [whole(a) for a in (wm, bm, f1, f2)],
             out_specs=(
                 pl.BlockSpec((step, span, ch), lambda s, _: (s, 0, 0)),
-                pl.BlockSpec((CORES, step, hid, rows), lambda s, _: (0, s, 0, 0)),
+                pl.BlockSpec((step, hid, rows), lambda s, _: (s, 0, 0)),
+                pl.BlockSpec((step, hid, rows), lambda s, _: (s, 0, 0)),
                 pl.BlockSpec((step, hid, span), lambda s, _: (s, 0, 0)),
             ),
             scratch_shapes=[
@@ -673,40 +685,60 @@
     )(me, *pieces, gate, x, wm, bm, f1, f2)
 
 
-def pack_kernel(slots_ref, *refs):
-    left_refs, (own_ref, sib_ref, lr_ref, rc_ref, right) = refs[:-5], refs[-5:]
+def packed_pair_kernel(step_rows, group, lefts, slots_ref, *refs):
+    left_refs, (own_ref, sib_ref, w_ref, pair_ref, ob_ref, up_ref, eb_ref, dn_ref) = refs[:lefts], refs[lefts:lefts + 8]
+    out_ref, r_hi, r_lo, w_st, up_st, dn_st, left, right = refs[lefts + 8:]
     cores, seqs, hid, rows = left_refs[0].shape
-    slots = len(left_refs) * cores
-    for i in range(own_ref.shape[0]):
-        at = slots_ref[i] * cores
-        for t, ref in enumerate((own_ref, sib_ref)):
-            right[pl.ds((at + t) * seqs, seqs)] = ref[i]
-    rt = jnp.concatenate([right[:, d, :] for d in range(hid)], axis=0)
-    rc_ref[...] = rt.T
-    for p, ref in enumerate(left_refs):
-        for t in range(cores):
-            for s in range(seqs):
-                at = (p * cores + t) * seqs + s
-                lr_ref[pl.ds(at, rows, stride=slots * seqs), :] = ref[t, s].T
-
-
-def pack(slots, lefts, own, sib):
-    cores, seqs, hid, rows = lefts[0].shape
-    planes, _, _, cols = own.shape
-    total = planes * cores * seqs
-    return pl.pallas_call(
-        pack_kernel,
-        out_shape=(
-            jax.ShapeDtypeStruct((rows * total, hid), F32),
-            jax.ShapeDtypeStruct((cols, hid * total), F32),
-        ),
-        in_specs=[pl.BlockSpec(memory_space=pltpu.SMEM)]
-        + [pl.BlockSpec(memory_space=pltpu.VMEM)] * (len(lefts) + 2),
-        out_specs=(pl.BlockSpec(memory_space=pltpu.VMEM),) * 2,
-        scratch_shapes=[pltpu.VMEM((total, hid, cols), F32)],
-        compiler_params=PARAMS,
-        name="pack",
-    )(slots, *lefts, own, sib)
+    total = lefts * cores * seqs
+
+    @pl.when(pl.program_id(0) == 0)
+    def _():
+        pair_weights(w_ref, up_ref, dn_ref, w_st, up_st, dn_st)
+        for i in range(own_ref.shape[0]):
+            at = slots_ref[i] * cores
+            for t, ref in enumerate((own_ref, sib_ref)):
+                right[pl.ds((at + t) * seqs, seqs)] = ref[i]
+        r_hi[...], r_lo[...] = split(jnp.concatenate([right[:, d, :] for d in range(hid)], axis=0).T)
+        for p, ref in enumerate(left_refs):
+            for t in range(cores):
+                for s in range(seqs):
+                    at = (p * cores + t) * seqs + s
+                    left[pl.ds(at, rows, stride=total), :] = ref[t, s].T
+
+    pair_rows(
+        step_rows, group, total, pl.program_id(0) * step_rows, left, pair_ref, ob_ref, eb_ref, out_ref,
+        r_hi, r_lo, w_st, up_st, dn_st,
+    )
+
+
+def packed_pair_update(slots, lefts, own, sib, w2, pair, ob, up, eb, dn, step_rows=8, group=4):
+    rows, cols, cz = pair.shape
+    cores, seqs, hid, _ = lefts[0].shape
+    total = len(lefts) * cores * seqs
+    ob = ob.reshape(1, -1)
+    eb = eb.reshape(1, -1)
+    tile = pl.BlockSpec((step_rows, cols, cz), lambda i, _: (i, 0, 0))
+    return pl.pallas_call(
+        functools.partial(packed_pair_kernel, step_rows, group, len(lefts)),
+        out_shape=jax.ShapeDtypeStruct(pair.shape, F32),
+        grid_spec=pltpu.PrefetchScalarGridSpec(
+            num_scalar_prefetch=1,
+            grid=(rows // step_rows,),
+            in_specs=[whole(a) for a in (*lefts, own, sib, w2)] + [tile] + [whole(a) for a in (ob, up, eb, dn)],
+            out_specs=tile,
+            scratch_shapes=[
+                pltpu.VMEM((cols, hid * total), BF16),
+                pltpu.VMEM((cols, hid * total), BF16),
+                pltpu.VMEM((3 * hid, w2.shape[1]), BF16),
+                pltpu.VMEM((3 * cz, up.shape[1]), BF16),
+                pltpu.VMEM((up.shape[1], 2 * cz), BF16),
+                pltpu.VMEM((rows * total, hid), F32),
+                pltpu.VMEM((total, hid, cols), F32),
+            ],
+        ),
+        compiler_params=PARAMS,
+        name="packed_pair_update",
+    )(slots, *lefts, own, sib, w2, pair, ob, up, eb, dn)
 
 
 def after(x, *deps):
@@ -757,25 +789,26 @@
     qkv = exchange(after(qkv, bias), parts)
     marked = after(n[None], near, second[0]) + 1
     q, k, v = stage(marked, after(qkv, near, second[0]), parts)
-    bias = after(bias, second[1], third[0])
+    bias = after(bias, third[0])
     att = None
     for i, tile in enumerate(((bias,), (near,), second, third)):
         att = head_attention(at, i, q, k, v, tile, att, hw)
     pieces = exchange([att[p, r] for p in range(parts) for r in range(CORES)], parts)
-    alignment_state_next, left, right = head_merge(
+    alignment_state_next, left_a, left_b, right = head_merge(
         ids, pieces, gate, homolog_embedding, mixing_projector, mixing_offset,
         first_factor_projector.T, second_factor_projector.T,
     )
     turn = lambda z0, c0, n0: (n0, c0, z0)
-    left = send(left, parts, turn)
+    left_b, left_a = send(left_b, parts, turn), send(left_a, parts, turn)
     sibling = lambda z0, c0, n0: (z0, c0 ^ 1, n0)
-    left = jnp.stack([left[0], send(left[1], parts, sibling)])
+    left_b = send(left_b, parts, sibling)
+    left = jnp.stack([left_a, left_b])
     rights = [right] + [send(right, parts, lambda z0, c0, n0, d=d: (z0 ^ d, c0, n0)) for d in range(1, PLANES)]
     lefts = [left] + [send(left, parts, lambda z0, c0, n0, d=d: (z0, c0, n0 ^ d)) for d in range(1, parts)]
     own = jnp.stack(rights)
-    left_rows, right_cols = pack(slots, lefts, own, send(own, parts, sibling))
-    pair_state_next = pair_update(
-        left_rows, right_cols, outer_product_weight.reshape(hid, hid * cz), pair_state,
+    pair_state_next = packed_pair_update(
+        slots, lefts, own, send(own, parts, sibling),
+        outer_product_weight.reshape(hid, hid * cz), pair_state,
         outer_product_bias, up_weight, expand_bias, down_weight,
     )
     return (alignment_state_next, pair_state_next)

time: 312 us -> 317 us (1.016)
  starting transfers between devices: 64.5 us -> 74.4 us
    ppermute x35 -> x36, starting transfers between devices: 64.5 us -> 74.4 us  [send(): return lax.ppermute(x, AXES, pairs)]
    ppermute x35 -> x36, waiting for transfers between devices: 80.2 us -> 77.3 us  [send(): return lax.ppermute(x, AXES, pairs)]
    pallas_call x2 -> x1, Pallas kernels: 86.9 us -> 85 us  [packed_pair_update(): pl.pallas_call(functools.partial(packed_pair_kernel, step_rows, group, le...]
  transfers between devices with their start and end apart: 35 -> 36, of which waited for: 16 -> 16; matrix products, arithmetic and copies ran while one was open for 2% -> 2% of each run, Pallas kernels for 12% -> 12%
where the time goes in v7:
time: 317 us; the launch traced here: 316 us
  Pallas kernels  150 us (47%)
  waiting for transfers between devices  77.3 us (24%)
  starting transfers between devices  74.4 us (23%)
  local copies, waits for them, and re-layouts  6.71 us (2%)
  between operations  4.13 us (1%)
  other arithmetic  3.73 us (1%)
    pallas_call x1, Pallas kernels, packed_pair_update(): pl.pallas_call(functools.partial(packed_pair_kernel, step_rows, group, le...  85 us
    ppermute x36, waiting for transfers between devices, send(): return lax.ppermute(x, AXES, pairs)  77.3 us
    ppermute x36, starting transfers between devices, send(): return lax.ppermute(x, AXES, pairs)  74.4 us
    pallas_call x4, Pallas kernels, head_attention(): pl.pallas_call(functools.partial(head_attention_kernel, hw, turn, len(til...  32 us
    pallas_call x1, Pallas kernels, head_bias(): pl.pallas_call(functools.partial(head_bias_kernel, group), out_shape=(jax...  13.6 us
    pallas_call x1, Pallas kernels, head_project(): pl.pallas_call(functools.partial(head_project_kernel, heads, 1.0 / math.s...  7.14 us
  transfers between devices with their start and end apart: 36, of which 16 were waited for; matrix products, arithmetic and copies ran while one was open for 2% of the time, Pallas kernels for 12%

profile of v7, /device:TPU:0, one launch (start us, length us, event | category | flops | bytes accessed | tf_op | source)
XLA Modules:
  0.0 316.1 jit_solution(17965494760116877015)
XLA Ops:
  1.3 13.6 %head_bias.1 = (f32[128,256]{1,0:T(8,128)}, f32[128,256]{1,0:T(8,128)}, f32[128,256]{1,0:T(8,128)}, f32[128,256]{1,0:T(8,128)}, f32[128,256]{1,0:T(8,128)}, /*in...) custom-call(s32[2]{0:T(128)} %pad_add_fusion.ids_ref, f32[128,256,128]{2,1,0:T(8,128)} %refs_7_.1, ...), custom_call_target="tpu_custom_call" | custom-call | tf_op jit(solution)/shard_map/head_bias/pallas_call | solution.py:453
  15.5 2.6 collective-permute-start.1
  23.7 2.7 collective-permute-start.5
  29.3 7.1 %head_project.1 = (f32[3,4,32,256]{3,2,1,0:T(8,128)}, f32[3,4,32,256]{3,2,1,0:T(8,128)}, f32[3,4,32,256]{3,2,1,0:T(8,128)}, f32[3,4,32,256]{3,2,1,0:T(8,128)}, f...) custom-call(s32[2]{0:T(128)} %pad_add_fusion.ids_ref, ...), custom_call_target="tpu_custom_call" | custom-call | tf_op jit(solution)/shard_map/head_project/pallas_call | solution.py:500
  40.2 22.0 %collective-permute-done.7.refs_0_ = f32[2,4,128,256]{3,2,1,0:T(8,128)S(1)} collective-permute-done((f32[2,4,128,256]{3,2,1,0:T(8,128)S(1)}, f32[2,4,128,256]{3,2,1,0:T(8,128)S(1)}, u32[]{:S(2)}, u32[]{:S(2)}) %collective-permute-start.7) | collective-permute-done | bytes 1048608 | tf_op jit(solution)/shard_map/ppermute | solution.py:403
  69.3 8.4 %collective-permute-done.10.refs_2_ = f32[3,4,32,256]{3,2,1,0:T(8,128)S(1)} collective-permute-done((f32[3,4,32,256]{3,2,1,0:T(8,128)S(1)}, f32[3,4,32,256]{3,2,1,0:T(8,128)S(1)}, u32[]{:S(2)}, u32[]{:S(2)}) %collective-permute-start.10) | collective-permute-done | bytes 393248 | tf_op jit(solution)/shard_map/ppermute | solution.py:403
  78.2 7.0 %collective-permute-done.11.refs_3_ = f32[3,4,32,256]{3,2,1,0:T(8,128)} collective-permute-done((f32[3,4,32,256]{3,2,1,0:T(8,128)S(1)}, f32[3,4,32,256]{3,2,1,0:T(8,128)}, u32[]{:S(2)}, u32[]{:S(2)}) %collective-permute-start.11) | collective-permute-done | bytes 393248 | tf_op jit(solution)/shard_map/ppermute | solution.py:403
  85.3 2.6 collective-permute-start.14
  89.0 9.3 %collective-permute-done.14.refs_6_ = f32[3,4,32,256]{3,2,1,0:T(8,128)} collective-permute-done((f32[3,4,32,256]{3,2,1,0:T(8,128)S(1)}, f32[3,4,32,256]{3,2,1,0:T(8,128)}, u32[]{:S(2)}, u32[]{:S(2)}) %collective-permute-start.14) | collective-permute-done | bytes 393248 | tf_op jit(solution)/shard_map/ppermute | solution.py:403
  98.2 7.7 %collective-permute-done.15.refs_7_ = f32[3,4,32,256]{3,2,1,0:T(8,128)} collective-permute-done((f32[3,4,32,256]{3,2,1,0:T(8,128)S(1)}, f32[3,4,32,256]{3,2,1,0:T(8,128)}, u32[]{:S(2)}, u32[]{:S(2)}) %collective-permute-start.15) | collective-permute-done | bytes 393248 | tf_op jit(solution)/shard_map/ppermute | solution.py:403
  106.6 6.0 %stage.1 = (bf16[2,4,4,256,128]{4,3,2,1,0:T(8,128)(2,1)}, bf16[2,4,128,1024]{3,2,1,0:T(8,128)(2,1)}, bf16[2,4,1024,128]{3,2,1,0:T(8,128)(2,1)}) custom-call(s32[1]{0:T(128)S(6)} %add.13.n_ref, f32[3,4,32,256]{3,2,1,0:T(8,128)} %get-tuple-element.90.refs_0_, f32[3,4,32,256]{3,2,1,0:T(8,128)} %copy-done.7, f32[3,4,32,256]{3,2,1,0:T(8,128)} %copy-done.8, ...), custom_call_target="tpu_custom_call" | custom-call | tf_op jit(solution)/shard_map/stage/pallas_call | solution.py:547
  112.6 7.7 %head_attention.4.refs_1_ = f32[4,2,4,32,256]{4,3,2,1,0:T(8,128)} custom-call(s32[12]{0:T(128)} %reshape.32.at_ref, bf16[2,4,4,256,128]{4,3,2,1,0:T(8,128)(2,1)} %get-tuple-element.98.q_ref, bf16[2,4,128,1024]{3,2,1,0:T(8,128)(2,1)} %get-tuple-element.99.k_ref, bf16[2,4,1024,128]{3,2,1,0:T(8,128)(2,1)} %get-tuple-element.100.v_ref, f32[2,4,128,256]{3,2,1,0:T(8,128)} %copy-done), custom_call_target="tpu_custom_call" | custom-call | tf_op jit(solution)/shard_map/head_attention/pallas_call | solution.py:597
  120.3 7.8 %head_attention.5.refs_2_ = f32[4,2,4,32,256]{4,3,2,1,0:T(8,128)} custom-call(s32[12]{0:T(128)} %reshape.32.at_ref, bf16[2,4,4,256,128]{4,3,2,1,0:T(8,128)(2,1)} %get-tuple-element.98.q_ref, bf16[2,4,128,1024]{3,2,1,0:T(8,128)(2,1)} %get-tuple-element.99.k_ref, bf16[2,4,1024,128]{3,2,1,0:T(8,128)(2,1)} %get-tuple-element.100.v_ref, ...), custom_call_target="tpu_custom_call", output_to_operand_aliasing={{}: (5, {})} | custom-call | tf_op jit(solution)/shard_map/head_attention/pallas_call | solution.py:597
  128.1 8.2 %head_attention.6.refs_2_ = f32[4,2,4,32,256]{4,3,2,1,0:T(8,128)} custom-call(s32[12]{0:T(128)} %reshape.32.at_ref, bf16[2,4,4,256,128]{4,3,2,1,0:T(8,128)(2,1)} %get-tuple-element.98.q_ref, bf16[2,4,128,1024]{3,2,1,0:T(8,128)(2,1)} %get-tuple-element.99.k_ref, bf16[2,4,1024,128]{3,2,1,0:T(8,128)(2,1)} %get-tuple-element.100.v_ref, ...), custom_call_target="tpu_custom_call", output_to_operand_aliasing={{}: (6, {})} | custom-call | tf_op jit(solution)/shard_map/head_attention/pallas_call | solution.py:597
  136.3 8.2 %head_attention.7 = f32[4,2,4,32,256]{4,3,2,1,0:T(8,128)} custom-call(s32[12]{0:T(128)} %reshape.32.at_ref, bf16[2,4,4,256,128]{4,3,2,1,0:T(8,128)(2,1)} %get-tuple-element.98.q_ref, bf16[2,4,128,1024]{3,2,1,0:T(8,128)(2,1)} %get-tuple-element.99.k_ref, bf16[2,4,1024,128]{3,2,1,0:T(8,128)(2,1)} %get-tuple-element.100.v_ref, ...), custom_call_target="tpu_custom_call", output_to_operand_aliasing={{}: (6, {})} | custom-call | tf_op jit(solution)/shard_map/head_attention/pallas_call | solution.py:597
  146.6 2.4 collective-permute-start.25
  156.5 2.4 collective-permute-done.23.refs_5_
  158.9 2.8 collective-permute-done.22.refs_4_
  162.7 6.1 %head_merge.1 = (f32[4,256,256]{2,1,0:T(8,128)}, f32[4,32,128]{2,1,0:T(8,128)}, f32[4,32,128]{2,1,0:T(8,128)}, f32[4,32,256]{2,1,0:T(8,128)}) custom-call(s32[2]{0:T(128)} %pad_add_fusion.ids_ref, f32[4,32,256]{2,1,0:T(8,128)} %get-tuple-element.113.refs_0_, f32[4,32,256]{2,1,0:T(8,128)} %copy-done.19, f32[4,32,256]{2,1,0:T(8,128)} %copy-done.18, ...), custom_call_target="tpu_custom_call" | custom-call | tf_op jit(solution)/shard_map/head_merge/pallas_call | solution.py:657
  168.7 3.7 %collective-permute-start.34 = (f32[4,32,256]{2,1,0:T(8,128)}, f32[4,32,256]{2,1,0:T(8,128)S(1)}, u32[]{:S(2)}, u32[]{:S(2)}) collective-permute-start(f32[4,32,256]{2,1,0:T(8,128)} %get-tuple-element.105), channel_id=1, source_target_pairs={{0,24},{1,25},{2,26},{3,27},{4,28},{5,29},{6,30},{7,31},{8,16},{9,... | collective-permute-start | bytes 393224 | tf_op jit(solution)/shard_map/ppermute | solution.py:403
  172.4 24.8 %collective-permute-start.33 = (f32[4,32,256]{2,1,0:T(8,128)}, f32[4,32,256]{2,1,0:T(8,128)S(1)}, u32[]{:S(2)}, u32[]{:S(2)}) collective-permute-start(f32[4,32,256]{2,1,0:T(8,128)} %get-tuple-element.105), channel_id=1, source_target_pairs={{0,16},{1,17},{2,18},{3,19},{4,20},{5,21},{6,22},{7,23},{8,24},{9,... | collective-permute-start | bytes 393224 | tf_op jit(solution)/shard_map/ppermute | solution.py:403
  197.4 9.2 %collective-permute-done.33 = f32[4,32,256]{2,1,0:T(8,128)S(1)} collective-permute-done((f32[4,32,256]{2,1,0:T(8,128)}, f32[4,32,256]{2,1,0:T(8,128)S(1)}, u32[]{:S(2)}, u32[]{:S(2)}) %collective-permute-start.33) | collective-permute-done | bytes 131104 | tf_op jit(solution)/shard_map/ppermute | solution.py:403
  212.0 12.5 %collective-permute-start.31 = (f32[2,4,32,128]{3,2,1,0:T(8,128)S(1)}, f32[2,4,32,128]{3,2,1,0:T(8,128)S(1)}, u32[]{:S(2)}, u32[]{:S(2)}) collective-permute-start(f32[2,4,32,128]{3,2,1,0:T(8,128)S(1)} %pad_maximum_fusion.2.refs_0_), channel_id=1, source_target_pairs={{0,3},{1,2},{2,1},{3,0},{4,7},{5,6},{6,5},{7,4},{8,11},{9,10},{10,... | collective-permute-start | bytes 393224 | tf_op jit(solution)/shard_map/ppermute | solution.py:403
  231.1 85.0 %packed_pair_update.1 = f32[128,256,128]{2,1,0:T(8,128)} custom-call(s32[4]{0:T(128)} %xor_xor_fusion.slots_ref, f32[2,4,32,128]{3,2,1,0:T(8,128)} %copy-done.5, f32[2,4,32,128]{3,2,1,0:T(8,128)} %copy-done.11, f32[2,4,32,128]{3,2,1,0:T(8,128)} %copy-done.10, f32[2,4,32,128]{3,2,1,0:T(8,128)} %copy-done.9, f32[4,4,32,256]{3,2,1,0:T(8,128)} %copy-done.1, ...), custom_call_target="tpu_custom_call" | custom-call | tf_op jit(solution)/shard_map/packed_pair_update/pallas_call | solution.py:721
  (133 shorter events, 42.2 us)
Async XLA Ops:
  15.5 10.9 %collective-permute-start.1 = (f32[128,256]{1,0:T(8,128)}, f32[128,256]{1,0:T(8,128)S(1)}, u32[]{:S(2)}, u32[]{:S(2)}) collective-permute-start(f32[128,256]{1,0:T(8,128)} %get-tuple-element.57), channel_id=1, source_target_pairs={{0,1},{1,0},{2,3},{3,2},{4,5},{5,4},{6,7},{7,6},{8,9},{9,8},{10,11... | collective-permute-start | bytes 393224 | tf_op jit(solution)/shard_map/ppermute | solution.py:403
  18.0 18.4 %collective-permute-start.2 = (f32[128,256]{1,0:T(8,128)}, f32[128,256]{1,0:T(8,128)S(1)}, u32[]{:S(2)}, u32[]{:S(2)}) collective-permute-start(f32[128,256]{1,0:T(8,128)} %get-tuple-element.58), channel_id=1, source_target_pairs={{0,5},{1,4},{2,7},{3,6},{4,1},{5,0},{6,3},{7,2},{8,13},{9,12},{10,... | collective-permute-start | bytes 393224 | tf_op jit(solution)/shard_map/ppermute | solution.py:403
  18.1 18.4 %collective-permute-start.3 = (f32[128,256]{1,0:T(8,128)}, f32[128,256]{1,0:T(8,128)S(1)}, u32[]{:S(2)}, u32[]{:S(2)}) collective-permute-start(f32[128,256]{1,0:T(8,128)} %get-tuple-element.59), channel_id=1, source_target_pairs={{0,2},{1,3},{2,0},{3,1},{4,6},{5,7},{6,4},{7,5},{8,10},{9,11},{10,... | collective-permute-start | bytes 393224 | tf_op jit(solution)/shard_map/ppermute | solution.py:403
  19.8 16.6 %collective-permute-start.4 = (f32[128,256]{1,0:T(8,128)}, f32[128,256]{1,0:T(8,128)S(1)}, u32[]{:S(2)}, u32[]{:S(2)}) collective-permute-start(f32[128,256]{1,0:T(8,128)} %get-tuple-element.60), channel_id=1, source_target_pairs={{0,6},{1,7},{2,4},{3,5},{4,2},{5,3},{6,0},{7,1},{8,14},{9,15},{10,... | collective-permute-start | bytes 393224 | tf_op jit(solution)/shard_map/ppermute | solution.py:403
  23.7 12.8 %collective-permute-start.5 = (f32[128,256]{1,0:T(8,128)}, f32[128,256]{1,0:T(8,128)S(1)}, u32[]{:S(2)}, u32[]{:S(2)}) collective-permute-start(f32[128,256]{1,0:T(8,128)} %get-tuple-element.61), channel_id=1, source_target_pairs={{0,3},{1,2},{2,1},{3,0},{4,7},{5,6},{6,5},{7,4},{8,11},{9,10},{10,... | collective-permute-start | bytes 393224 | tf_op jit(solution)/shard_map/ppermute | solution.py:403
  26.4 10.1 %collective-permute-start.6 = (f32[128,256]{1,0:T(8,128)}, f32[128,256]{1,0:T(8,128)S(1)}, u32[]{:S(2)}, u32[]{:S(2)}) collective-permute-start(f32[128,256]{1,0:T(8,128)} %get-tuple-element.62), channel_id=1, source_target_pairs={{0,7},{1,6},{2,5},{3,4},{4,3},{5,2},{6,1},{7,0},{8,15},{9,14},{10,... | collective-permute-start | bytes 393224 | tf_op jit(solution)/shard_map/ppermute | solution.py:403
  36.8 25.4 %collective-permute-start.7 = (f32[2,4,128,256]{3,2,1,0:T(8,128)S(1)}, f32[2,4,128,256]{3,2,1,0:T(8,128)S(1)}, u32[]{:S(2)}, u32[]{:S(2)}) collective-permute-start(f32[2,4,128,256]{3,2,1,0:T(8,128)S(1)} %pad_maximum_fusion.refs_0_), channel_id=1, source_target_pairs={{0,8},{1,9},{2,10},{3,11},{4,12},{5,13},{6,14},{7,15},{8,0},{9,1},... | collective-permute-start | bytes 3145736 | tf_op jit(solution)/shard_map/ppermute | solution.py:403
  38.5 24.5 %collective-permute-start.8 = (f32[2,4,128,256]{3,2,1,0:T(8,128)S(1)}, f32[2,4,128,256]{3,2,1,0:T(8,128)}, u32[]{:S(2)}, u32[]{:S(2)}) collective-permute-start(f32[2,4,128,256]{3,2,1,0:T(8,128)S(1)} %pad_maximum_fusion.refs_0_), channel_id=1, source_target_pairs={{8,16},{9,17},{10,18},{11,19},{12,20},{13,21},{14,22},{15,23},{16,... | collective-permute-start | bytes 3145736 | tf_op jit(solution)/shard_map/ppermute | solution.py:403
  63.0 65.1 %collective-permute-start.18 = (f32[2,4,128,256]{3,2,1,0:T(8,128)}, f32[2,4,128,256]{3,2,1,0:T(8,128)}, u32[]{:S(2)}, u32[]{:S(2)}) collective-permute-start(f32[2,4,128,256]{3,2,1,0:T(8,128)} %collective-permute-done.8.refs_0_), channel_id=1, source_target_pairs={{8,0},{9,1},{10,2},{11,3},{12,4},{13,5},{14,6},{15,7},{16,24},{17,... | collective-permute-start | bytes 3145736 | tf_op jit(solution)/shard_map/ppermute | solution.py:403
  64.3 72.0 %collective-permute-start.17 = (f32[2,4,128,256]{3,2,1,0:T(8,128)S(1)}, f32[2,4,128,256]{3,2,1,0:T(8,128)}, u32[]{:S(2)}, u32[]{:S(2)}) collective-permute-start(f32[2,4,128,256]{3,2,1,0:T(8,128)S(1)} %collective-permute-done.16.refs_0_), channel_id=1, source_target_pairs={{8,0},{9,1},{10,2},{11,3},{12,4},{13,5},{14,6},{15,7},{16,24},{17,... | collective-permute-start | bytes 3145736 | tf_op jit(solution)/shard_map/ppermute | solution.py:403
  65.7 12.1 %collective-permute-start.10 = (f32[3,4,32,256]{3,2,1,0:T(8,128)S(1)}, f32[3,4,32,256]{3,2,1,0:T(8,128)S(1)}, u32[]{:S(2)}, u32[]{:S(2)}) collective-permute-start(f32[3,4,32,256]{3,2,1,0:T(8,128)S(1)} %copy-done.28), channel_id=1, source_target_pairs={{0,1},{1,0},{2,3},{3,2},{4,5},{5,4},{6,7},{7,6},{8,9},{9,8},{10,11... | collective-permute-start | bytes 1179656 | tf_op jit(solution)/shard_map/ppermute | solution.py:403
  67.4 17.9 %collective-permute-start.11 = (f32[3,4,32,256]{3,2,1,0:T(8,128)S(1)}, f32[3,4,32,256]{3,2,1,0:T(8,128)}, u32[]{:S(2)}, u32[]{:S(2)}) collective-permute-start(f32[3,4,32,256]{3,2,1,0:T(8,128)S(1)} %copy-done.27), channel_id=1, source_target_pairs={{0,5},{1,4},{2,7},{3,6},{4,1},{5,0},{6,3},{7,2},{8,13},{9,12},{10,... | collective-permute-start | bytes 1179656 | tf_op jit(solution)/shard_map/ppermute | solution.py:403
  67.6 20.3 %collective-permute-start.12 = (f32[3,4,32,256]{3,2,1,0:T(8,128)S(1)}, f32[3,4,32,256]{3,2,1,0:T(8,128)}, u32[]{:S(2)}, u32[]{:S(2)}) collective-permute-start(f32[3,4,32,256]{3,2,1,0:T(8,128)S(1)} %copy-done.26), channel_id=1, source_target_pairs={{0,2},{1,3},{2,0},{3,1},{4,6},{5,7},{6,4},{7,5},{8,10},{9,11},{10,... | collective-permute-start | bytes 1179656 | tf_op jit(solution)/shard_map/ppermute | solution.py:403
  77.7 11.3 %collective-permute-start.13 = (f32[3,4,32,256]{3,2,1,0:T(8,128)S(1)}, f32[3,4,32,256]{3,2,1,0:T(8,128)}, u32[]{:S(2)}, u32[]{:S(2)}) collective-permute-start(f32[3,4,32,256]{3,2,1,0:T(8,128)S(1)} %copy-done.25), channel_id=1, source_target_pairs={{0,6},{1,7},{2,4},{3,5},{4,2},{5,3},{6,0},{7,1},{8,14},{9,15},{10,... | collective-permute-start | bytes 1179656 | tf_op jit(solution)/shard_map/ppermute | solution.py:403
  85.3 13.0 %collective-permute-start.14 = (f32[3,4,32,256]{3,2,1,0:T(8,128)S(1)}, f32[3,4,32,256]{3,2,1,0:T(8,128)}, u32[]{:S(2)}, u32[]{:S(2)}) collective-permute-start(f32[3,4,32,256]{3,2,1,0:T(8,128)S(1)} %copy-done.24), channel_id=1, source_target_pairs={{0,3},{1,2},{2,1},{3,0},{4,7},{5,6},{6,5},{7,4},{8,11},{9,10},{10,... | collective-permute-start | bytes 1179656 | tf_op jit(solution)/shard_map/ppermute | solution.py:403
  87.9 18.1 %collective-permute-start.15 = (f32[3,4,32,256]{3,2,1,0:T(8,128)S(1)}, f32[3,4,32,256]{3,2,1,0:T(8,128)}, u32[]{:S(2)}, u32[]{:S(2)}) collective-permute-start(f32[3,4,32,256]{3,2,1,0:T(8,128)S(1)} %copy-done.23), channel_id=1, source_target_pairs={{0,7},{1,6},{2,5},{3,4},{4,3},{5,2},{6,1},{7,0},{8,15},{9,14},{10,... | collective-permute-start | bytes 1179656 | tf_op jit(solution)/shard_map/ppermute | solution.py:403
  149.3 9.6 %collective-permute-start.23 = (f32[4,32,256]{2,1,0:T(8,128)S(1)}, f32[4,32,256]{2,1,0:T(8,128)S(1)}, u32[]{:S(2)}, u32[]{:S(2)}) collective-permute-start(f32[4,32,256]{2,1,0:T(8,128)S(1)} %get-tuple-element.108), channel_id=1, source_target_pairs={{0,6},{1,7},{2,4},{3,5},{4,2},{5,3},{6,0},{7,1},{8,14},{9,15},{10,... | collective-permute-start | bytes 393224 | tf_op jit(solution)/shard_map/ppermute | solution.py:403
  150.6 11.1 %collective-permute-start.22 = (f32[4,32,256]{2,1,0:T(8,128)S(1)}, f32[4,32,256]{2,1,0:T(8,128)S(1)}, u32[]{:S(2)}, u32[]{:S(2)}) collective-permute-start(f32[4,32,256]{2,1,0:T(8,128)S(1)} %get-tuple-element.109), channel_id=1, source_target_pairs={{0,2},{1,3},{2,0},{3,1},{4,6},{5,7},{6,4},{7,5},{8,10},{9,11},{10,... | collective-permute-start | bytes 393224 | tf_op jit(solution)/shard_map/ppermute | solution.py:403
  151.0 10.7 %collective-permute-start.21 = (f32[4,32,256]{2,1,0:T(8,128)S(1)}, f32[4,32,256]{2,1,0:T(8,128)S(1)}, u32[]{:S(2)}, u32[]{:S(2)}) collective-permute-start(f32[4,32,256]{2,1,0:T(8,128)S(1)} %get-tuple-element.110), channel_id=1, source_target_pairs={{0,5},{1,4},{2,7},{3,6},{4,1},{5,0},{6,3},{7,2},{8,13},{9,12},{10,... | collective-permute-start | bytes 393224 | tf_op jit(solution)/shard_map/ppermute | solution.py:403
  168.7 28.6 %collective-permute-start.34 = (f32[4,32,256]{2,1,0:T(8,128)}, f32[4,32,256]{2,1,0:T(8,128)S(1)}, u32[]{:S(2)}, u32[]{:S(2)}) collective-permute-start(f32[4,32,256]{2,1,0:T(8,128)} %get-tuple-element.105), channel_id=1, source_target_pairs={{0,24},{1,25},{2,26},{3,27},{4,28},{5,29},{6,30},{7,31},{8,16},{9,... | collective-permute-start | bytes 393224 | tf_op jit(solution)/shard_map/ppermute | solution.py:403
  172.4 34.1 %collective-permute-start.33 = (f32[4,32,256]{2,1,0:T(8,128)}, f32[4,32,256]{2,1,0:T(8,128)S(1)}, u32[]{:S(2)}, u32[]{:S(2)}) collective-permute-start(f32[4,32,256]{2,1,0:T(8,128)} %get-tuple-element.105), channel_id=1, source_target_pairs={{0,16},{1,17},{2,18},{3,19},{4,20},{5,21},{6,22},{7,23},{8,24},{9,... | collective-permute-start | bytes 393224 | tf_op jit(solution)/shard_map/ppermute | solution.py:403
  197.2 9.3 %collective-permute-start.32 = (f32[4,32,256]{2,1,0:T(8,128)}, f32[4,32,256]{2,1,0:T(8,128)S(1)}, u32[]{:S(2)}, u32[]{:S(2)}) collective-permute-start(f32[4,32,256]{2,1,0:T(8,128)} %get-tuple-element.105), channel_id=1, source_target_pairs={{0,8},{1,9},{2,10},{3,11},{4,12},{5,13},{6,14},{7,15},{8,0},{9,1},... | collective-permute-start | bytes 393224 | tf_op jit(solution)/shard_map/ppermute | solution.py:403
  207.5 22.7 %collective-permute-start.35 = (f32[4,4,32,256]{3,2,1,0:T(8,128)S(1)}, f32[4,4,32,256]{3,2,1,0:T(8,128)S(1)}, u32[]{:S(2)}, u32[]{:S(2)}) collective-permute-start(f32[4,4,32,256]{3,2,1,0:T(8,128)S(1)} %pad_maximum_fusion.1.refs_4_), channel_id=1, source_target_pairs={{0,4},{1,5},{2,6},{3,7},{4,0},{5,1},{6,2},{7,3},{8,12},{9,13},{10,... | collective-permute-start | bytes 1572872 | tf_op jit(solution)/shard_map/ppermute | solution.py:403
  212.0 15.9 %collective-permute-start.31 = (f32[2,4,32,128]{3,2,1,0:T(8,128)S(1)}, f32[2,4,32,128]{3,2,1,0:T(8,128)S(1)}, u32[]{:S(2)}, u32[]{:S(2)}) collective-permute-start(f32[2,4,32,128]{3,2,1,0:T(8,128)S(1)} %pad_maximum_fusion.2.refs_0_), channel_id=1, source_target_pairs={{0,3},{1,2},{2,1},{3,0},{4,7},{5,6},{6,5},{7,4},{8,11},{9,10},{10,... | collective-permute-start | bytes 393224 | tf_op jit(solution)/shard_map/ppermute | solution.py:403
  (42 other events, 792.9 us)

commit v8 on v7

--- a/solution.py
+++ b/solution.py
@@ -566,11 +566,9 @@
     )(n, *pieces)
 
 
-def head_attention_kernel(hw, turn, tiles, at_ref, q_ref, k_ref, v_ref, *refs):
-    bias_refs, out_ref = refs[:tiles], refs[-1]
+def attend_tile(hw, core, q_ref, k_ref, v_ref, bias_refs, store):
     parts = bias_refs[0].shape[1]
     cores, seqs = q_ref.shape[:2]
-    core = at_ref[3 * turn + 2]
     bias = jnp.concatenate(
         [
             jnp.concatenate([sum(b[h ^ core, n] for b in bias_refs) for n in range(parts)], axis=1)
@@ -588,7 +586,60 @@
         top = jnp.max(scores, axis=1, keepdims=True)
         ph, plo = split(jnp.exp(scores - top))
         t = (mm(ph, v_ref[g, s]) + mm(plo, v_ref[g, s])).T
-        out_ref[0, g, s] = (t[0:hw] + t[hw:2 * hw]) / t[2 * hw:2 * hw + 1]
+        store(g, s, (t[0:hw] + t[hw:2 * hw]) / t[2 * hw:2 * hw + 1])
+
+
+def head_attention_kernel(hw, turn, tiles, at_ref, q_ref, k_ref, v_ref, *refs):
+    bias_refs, out_ref = refs[:tiles], refs[-1]
+
+    def store(g, s, value):
+        out_ref[0, g, s] = value
+
+    attend_tile(hw, at_ref[3 * turn + 2], q_ref, k_ref, v_ref, bias_refs, store)
+
+
+def last_attention_kernel(hw, turn, tiles, at_ref, q_ref, k_ref, v_ref, *refs):
+    bias_refs, prev_ref, out_refs, tile = refs[:tiles], refs[tiles], refs[tiles + 1:-1], refs[-1]
+    cores = q_ref.shape[0]
+
+    def store(g, s, value):
+        tile[g, s] = value
+
+    attend_tile(hw, at_ref[3 * turn + 2], q_ref, k_ref, v_ref, bias_refs, store)
+    for k, out_ref in enumerate(out_refs):
+        p, g = divmod(k, cores)
+        mine = at_ref[3 * turn + 1] == p
+
+        @pl.when(mine)
+        def _():
+            out_ref[...] = tile[g]
+
+        @pl.when(jnp.logical_not(mine))
+        def _():
+            out_ref[...] = prev_ref[p, g]
+
+
+def last_attention(at, turn, q, k, v, tiles, prev, hw, step=2):
+    cores, seqs, parts, span, _ = q.shape
+    return pl.pallas_call(
+        functools.partial(last_attention_kernel, hw, turn, len(tiles)),
+        out_shape=(jax.ShapeDtypeStruct((seqs, hw, span), F32),) * (parts * cores),
+        grid_spec=pltpu.PrefetchScalarGridSpec(
+            num_scalar_prefetch=1,
+            grid=(seqs // step,),
+            in_specs=[
+                pl.BlockSpec((cores, step, 1, span, 4 * hw), lambda s, at: (0, s, at[3 * turn], 0, 0)),
+                pl.BlockSpec((cores, step, 4 * hw, parts * span), lambda s, at: (0, s, 0, 0)),
+                pl.BlockSpec((cores, step, parts * span, 4 * hw), lambda s, at: (0, s, 0, 0)),
+            ]
+            + [whole(b) for b in tiles]
+            + [pl.BlockSpec((parts, cores, step, hw, span), lambda s, at: (0, 0, s, 0, 0))],
+            out_specs=(pl.BlockSpec((step, hw, span), lambda s, at: (s, 0, 0)),) * (parts * cores),
+            scratch_shapes=[pltpu.VMEM((cores, step, hw, span), F32)],
+        ),
+        compiler_params=PARAMS,
+        name="last_attention",
+    )(at, q, k, v, *tiles, prev)
 
 
 def head_attention(at, turn, q, k, v, tiles, prev, hw, step=2):
@@ -686,18 +737,19 @@
 
 
 def packed_pair_kernel(step_rows, group, lefts, slots_ref, *refs):
-    left_refs, (own_ref, sib_ref, w_ref, pair_ref, ob_ref, up_ref, eb_ref, dn_ref) = refs[:lefts], refs[lefts:lefts + 8]
-    out_ref, r_hi, r_lo, w_st, up_st, dn_st, left, right = refs[lefts + 8:]
+    left_refs, refs = refs[:lefts], refs[lefts:]
     cores, seqs, hid, rows = left_refs[0].shape
+    right_refs, refs = refs[:lefts * cores], refs[lefts * cores:]
+    w_ref, pair_ref, ob_ref, up_ref, eb_ref, dn_ref = refs[:6]
+    out_ref, r_hi, r_lo, w_st, up_st, dn_st, left, right = refs[6:]
     total = lefts * cores * seqs
 
     @pl.when(pl.program_id(0) == 0)
     def _():
         pair_weights(w_ref, up_ref, dn_ref, w_st, up_st, dn_st)
-        for i in range(own_ref.shape[0]):
-            at = slots_ref[i] * cores
-            for t, ref in enumerate((own_ref, sib_ref)):
-                right[pl.ds((at + t) * seqs, seqs)] = ref[i]
+        for i, ref in enumerate(right_refs):
+            core, plane = divmod(i, lefts)
+            right[pl.ds((slots_ref[plane] * cores + core) * seqs, seqs)] = ref[...]
         r_hi[...], r_lo[...] = split(jnp.concatenate([right[:, d, :] for d in range(hid)], axis=0).T)
         for p, ref in enumerate(left_refs):
             for t in range(cores):
@@ -711,7 +763,7 @@
     )
 
 
-def packed_pair_update(slots, lefts, own, sib, w2, pair, ob, up, eb, dn, step_rows=8, group=4):
+def packed_pair_update(slots, lefts, rights, w2, pair, ob, up, eb, dn, step_rows=8, group=4):
     rows, cols, cz = pair.shape
     cores, seqs, hid, _ = lefts[0].shape
     total = len(lefts) * cores * seqs
@@ -724,7 +776,7 @@
         grid_spec=pltpu.PrefetchScalarGridSpec(
             num_scalar_prefetch=1,
             grid=(rows // step_rows,),
-            in_specs=[whole(a) for a in (*lefts, own, sib, w2)] + [tile] + [whole(a) for a in (ob, up, eb, dn)],
+            in_specs=[whole(a) for a in (*lefts, *rights, w2)] + [tile] + [whole(a) for a in (ob, up, eb, dn)],
             out_specs=tile,
             scratch_shapes=[
                 pltpu.VMEM((cols, hid * total), BF16),
@@ -738,7 +790,7 @@
         ),
         compiler_params=PARAMS,
         name="packed_pair_update",
-    )(slots, *lefts, own, sib, w2, pair, ob, up, eb, dn)
+    )(slots, *lefts, *rights, w2, pair, ob, up, eb, dn)
 
 
 def after(x, *deps):
@@ -788,27 +840,25 @@
     near, second, third = line_gather(bias, parts)
     qkv = exchange(after(qkv, bias), parts)
     marked = after(n[None], near, second[0]) + 1
-    q, k, v = stage(marked, after(qkv, near, second[0]), parts)
+    w2 = outer_product_weight.reshape(hid, hid * cz)
+    q, k, v = stage(marked, after(qkv, near, second[0], w2), parts)
     bias = after(bias, third[0])
     att = None
-    for i, tile in enumerate(((bias,), (near,), second, third)):
+    for i, tile in enumerate(((bias,), (near,), second)):
         att = head_attention(at, i, q, k, v, tile, att, hw)
-    pieces = exchange([att[p, r] for p in range(parts) for r in range(CORES)], parts)
+    pieces = exchange(last_attention(at, PLANES - 1, q, k, v, third, att, hw), parts)
     alignment_state_next, left_a, left_b, right = head_merge(
         ids, pieces, gate, homolog_embedding, mixing_projector, mixing_offset,
         first_factor_projector.T, second_factor_projector.T,
     )
-    turn = lambda z0, c0, n0: (n0, c0, z0)
-    left_b, left_a = send(left_b, parts, turn), send(left_a, parts, turn)
-    sibling = lambda z0, c0, n0: (z0, c0 ^ 1, n0)
-    left_b = send(left_b, parts, sibling)
+    left_b = send(left_b, parts, lambda z0, c0, n0: (n0, c0 ^ 1, z0))
+    left_a = send(left_a, parts, lambda z0, c0, n0: (n0, c0, z0))
     left = jnp.stack([left_a, left_b])
     rights = [right] + [send(right, parts, lambda z0, c0, n0, d=d: (z0 ^ d, c0, n0)) for d in range(1, PLANES)]
     lefts = [left] + [send(left, parts, lambda z0, c0, n0, d=d: (z0, c0, n0 ^ d)) for d in range(1, parts)]
-    own = jnp.stack(rights)
+    rights += [send(a, parts, lambda z0, c0, n0: (z0, c0 ^ 1, n0)) for a in rights]
     pair_state_next = packed_pair_update(
-        slots, lefts, own, send(own, parts, sibling),
-        outer_product_weight.reshape(hid, hid * cz), pair_state,
+        slots, lefts, rights, w2, pair_state,
         outer_product_bias, up_weight, expand_bias, down_weight,
     )
     return (alignment_state_next, pair_state_next)

time: 317 us -> 306 us (0.965)
  waiting for transfers between devices: 77.3 us -> 66.5 us
    ppermute x36 -> x38, waiting for transfers between devices: 77.3 us -> 66.5 us  [send(): return lax.ppermute(x, AXES, pairs)]
    pallas_call x0 -> x1, Pallas kernels: none -> 8.75 us  [last_attention(): pl.pallas_call(functools.partial(last_attention_kernel, hw, turn, len(til...]
    pallas_call x4 -> x3, Pallas kernels: 32 us -> 23.8 us  [head_attention(): pl.pallas_call(functools.partial(head_attention_kernel, hw, turn, len(til...]
    ppermute x36 -> x38, starting transfers between devices: 74.4 us -> 75.6 us  [send(): return lax.ppermute(x, AXES, pairs)]
  transfers between devices with their start and end apart: 36 -> 38, of which waited for: 16 -> 10; matrix products, arithmetic and copies ran while one was open for 2% -> 2% of each run, Pallas kernels for 12% -> 12%
where the time goes in v8:
time: 306 us; the launch traced here: 305 us
  Pallas kernels  150 us (49%)
  starting transfers between devices  75.6 us (25%)
  waiting for transfers between devices  66.5 us (22%)
  local copies, waits for them, and re-layouts  5.63 us (2%)
  between operations  4.28 us (1%)
    pallas_call x1, Pallas kernels, packed_pair_update(): pl.pallas_call(functools.partial(packed_pair_kernel, step_rows, group, le...  85.2 us
    ppermute x38, starting transfers between devices, send(): return lax.ppermute(x, AXES, pairs)  75.6 us
    ppermute x38, waiting for transfers between devices, send(): return lax.ppermute(x, AXES, pairs)  66.5 us
    pallas_call x3, Pallas kernels, head_attention(): pl.pallas_call(functools.partial(head_attention_kernel, hw, turn, len(til...  23.8 us
    pallas_call x1, Pallas kernels, head_bias(): pl.pallas_call(functools.partial(head_bias_kernel, group), out_shape=(jax...  13.6 us
    pallas_call x1, Pallas kernels, last_attention(): pl.pallas_call(functools.partial(last_attention_kernel, hw, turn, len(til...  8.75 us
    pallas_call x1, Pallas kernels, head_project(): pl.pallas_call(functools.partial(head_project_kernel, heads, 1.0 / math.s...  7.17 us
  transfers between devices with their start and end apart: 38, of which 10 were waited for; matrix products, arithmetic and copies ran while one was open for 2% of the time, Pallas kernels for 12%

profile of v8, /device:TPU:0, one launch (start us, length us, event | category | flops | bytes accessed | tf_op | source)
XLA Modules:
  0.0 304.9 jit_solution(13410408698949257125)
XLA Ops:
  1.2 13.6 %head_bias.1 = (f32[128,256]{1,0:T(8,128)}, f32[128,256]{1,0:T(8,128)}, f32[128,256]{1,0:T(8,128)}, f32[128,256]{1,0:T(8,128)}, f32[128,256]{1,0:T(8,128)}, /*in...) custom-call(s32[2]{0:T(128)} %pad_add_fusion.ids_ref, f32[128,256,128]{2,1,0:T(8,128)} %refs_13_.1, ...), custom_call_target="tpu_custom_call" | custom-call | tf_op jit(solution)/shard_map/head_bias/pallas_call | solution.py:453
  15.4 2.6 collective-permute-start.1
  23.7 2.7 collective-permute-start.5
  29.2 7.2 %head_project.1 = (f32[3,4,32,256]{3,2,1,0:T(8,128)}, f32[3,4,32,256]{3,2,1,0:T(8,128)}, f32[3,4,32,256]{3,2,1,0:T(8,128)}, f32[3,4,32,256]{3,2,1,0:T(8,128)}, f...) custom-call(s32[2]{0:T(128)} %pad_add_fusion.ids_ref, ...), custom_call_target="tpu_custom_call" | custom-call | tf_op jit(solution)/shard_map/head_project/pallas_call | solution.py:500
  40.1 22.0 %collective-permute-done.7.refs_0_ = f32[2,4,128,256]{3,2,1,0:T(8,128)S(1)} collective-permute-done((f32[2,4,128,256]{3,2,1,0:T(8,128)S(1)}, f32[2,4,128,256]{3,2,1,0:T(8,128)S(1)}, u32[]{:S(2)}, u32[]{:S(2)}) %collective-permute-start.7) | collective-permute-done | bytes 1048608 | tf_op jit(solution)/shard_map/ppermute | solution.py:403
  69.5 8.5 %collective-permute-done.10.refs_2_ = f32[3,4,32,256]{3,2,1,0:T(8,128)} collective-permute-done((f32[3,4,32,256]{3,2,1,0:T(8,128)S(1)}, f32[3,4,32,256]{3,2,1,0:T(8,128)}, u32[]{:S(2)}, u32[]{:S(2)}) %collective-permute-start.10) | collective-permute-done | bytes 393248 | tf_op jit(solution)/shard_map/ppermute | solution.py:403
  78.4 7.0 %collective-permute-done.11.refs_3_ = f32[3,4,32,256]{3,2,1,0:T(8,128)} collective-permute-done((f32[3,4,32,256]{3,2,1,0:T(8,128)S(1)}, f32[3,4,32,256]{3,2,1,0:T(8,128)}, u32[]{:S(2)}, u32[]{:S(2)}) %collective-permute-start.11) | collective-permute-done | bytes 393248 | tf_op jit(solution)/shard_map/ppermute | solution.py:403
  85.4 2.6 collective-permute-start.14
  88.3 1.9 reshape.34.refs_12_
  90.3 8.4 %collective-permute-done.14.refs_6_ = f32[3,4,32,256]{3,2,1,0:T(8,128)} collective-permute-done((f32[3,4,32,256]{3,2,1,0:T(8,128)}, f32[3,4,32,256]{3,2,1,0:T(8,128)}, u32[]{:S(2)}, u32[]{:S(2)}) %collective-permute-start.14) | collective-permute-done | bytes 393248 | tf_op jit(solution)/shard_map/ppermute | solution.py:403
  98.6 7.7 %collective-permute-done.15.refs_7_ = f32[3,4,32,256]{3,2,1,0:T(8,128)} collective-permute-done((f32[3,4,32,256]{3,2,1,0:T(8,128)}, f32[3,4,32,256]{3,2,1,0:T(8,128)}, u32[]{:S(2)}, u32[]{:S(2)}) %collective-permute-start.15) | collective-permute-done | bytes 393248 | tf_op jit(solution)/shard_map/ppermute | solution.py:403
  107.0 5.8 %stage.1 = (bf16[2,4,4,256,128]{4,3,2,1,0:T(8,128)(2,1)}, bf16[2,4,128,1024]{3,2,1,0:T(8,128)(2,1)}, bf16[2,4,1024,128]{3,2,1,0:T(8,128)(2,1)}) custom-call(s32[1]{0:T(128)S(6)} %add.13.n_ref, f32[3,4,32,256]{3,2,1,0:T(8,128)} %get-tuple-element.98.refs_0_, f32[3,4,32,256]{3,2,1,0:T(8,128)} %copy-done.4, f32[3,4,32,256]{3,2,1,0:T(8,128)} %collective-permute-done.10.refs_2_, ...), custom_call_target="tpu_custom_call" | custom-call | tf_op jit(solution)/shard_map/stage/pallas_call | solution.py:547
  112.8 7.8 %head_attention.3.refs_1_ = f32[4,2,4,32,256]{4,3,2,1,0:T(8,128)} custom-call(s32[12]{0:T(128)} %reshape.32.at_ref, bf16[2,4,4,256,128]{4,3,2,1,0:T(8,128)(2,1)} %get-tuple-element.106.q_ref, bf16[2,4,128,1024]{3,2,1,0:T(8,128)(2,1)} %get-tuple-element.107.k_ref, bf16[2,4,1024,128]{3,2,1,0:T(8,128)(2,1)} %get-tuple-element.108.v_ref, f32[2,4,128,256]{3,2,1,0:T(8,128)} %copy-done), custom_call_target="tpu_custom_call" | custom-call | tf_op jit(solution)/shard_map/head_attention/pallas_call | solution.py:648
  120.6 7.8 %head_attention.4.refs_2_ = f32[4,2,4,32,256]{4,3,2,1,0:T(8,128)} custom-call(s32[12]{0:T(128)} %reshape.32.at_ref, bf16[2,4,4,256,128]{4,3,2,1,0:T(8,128)(2,1)} %get-tuple-element.106.q_ref, bf16[2,4,128,1024]{3,2,1,0:T(8,128)(2,1)} %get-tuple-element.107.k_ref, bf16[2,4,1024,128]{3,2,1,0:T(8,128)(2,1)} %get-tuple-element.108.v_ref, ...), custom_call_target="tpu_custom_call", output_to_operand_aliasing={{}: (5, {})} | custom-call | tf_op jit(solution)/shard_map/head_attention/pallas_call | solution.py:648
  128.4 8.2 %head_attention.5.refs_2_ = f32[4,2,4,32,256]{4,3,2,1,0:T(8,128)} custom-call(s32[12]{0:T(128)} %reshape.32.at_ref, bf16[2,4,4,256,128]{4,3,2,1,0:T(8,128)(2,1)} %get-tuple-element.106.q_ref, bf16[2,4,128,1024]{3,2,1,0:T(8,128)(2,1)} %get-tuple-element.107.k_ref, bf16[2,4,1024,128]{3,2,1,0:T(8,128)(2,1)} %get-tuple-element.108.v_ref, ...), custom_call_target="tpu_custom_call", output_to_operand_aliasing={{}: (6, {})} | custom-call | tf_op jit(solution)/shard_map/head_attention/pallas_call | solution.py:648
  136.6 8.8 %last_attention.1 = (f32[4,32,256]{2,1,0:T(8,128)}, f32[4,32,256]{2,1,0:T(8,128)}, f32[4,32,256]{2,1,0:T(8,128)}, f32[4,32,256]{2,1,0:T(8,128)}, f32[4,32,256]{2...) custom-call(s32[12]{0:T(128)} %reshape.32.at_ref, ...), custom_call_target="tpu_custom_call" | custom-call | tf_op jit(solution)/shard_map/last_attention/pallas_call | solution.py:624
  149.1 2.6 collective-permute-start.24
  154.3 7.0 %collective-permute-done.23.refs_5_ = f32[4,32,256]{2,1,0:T(8,128)S(1)} collective-permute-done((f32[4,32,256]{2,1,0:T(8,128)}, f32[4,32,256]{2,1,0:T(8,128)S(1)}, u32[]{:S(2)}, u32[]{:S(2)}) %collective-permute-start.23) | collective-permute-done | bytes 131104 | tf_op jit(solution)/shard_map/ppermute | solution.py:403
  162.0 5.9 %head_merge.1 = (f32[4,256,256]{2,1,0:T(8,128)}, f32[4,32,128]{2,1,0:T(8,128)}, f32[4,32,128]{2,1,0:T(8,128)}, f32[4,32,256]{2,1,0:T(8,128)}) custom-call(s32[2]{0:T(128)} %pad_add_fusion.ids_ref, f32[4,32,256]{2,1,0:T(8,128)} %get-tuple-element.110.refs_0_, f32[4,32,256]{2,1,0:T(8,128)} %copy-done.16, f32[4,32,256]{2,1,0:T(8,128)} %copy-done.17, ...), custom_call_target="tpu_custom_call" | custom-call | tf_op jit(solution)/shard_map/head_merge/pallas_call | solution.py:708
  170.0 9.6 %collective-permute-start.33 = (f32[4,32,256]{2,1,0:T(8,128)}, f32[4,32,256]{2,1,0:T(8,128)S(1)}, u32[]{:S(2)}, u32[]{:S(2)}) collective-permute-start(f32[4,32,256]{2,1,0:T(8,128)} %get-tuple-element.121.refs_4_), channel_id=1, source_target_pairs={{0,24},{1,25},{2,26},{3,27},{4,28},{5,29},{6,30},{7,31},{8,16},{9,... | collective-permute-start | bytes 393224 | tf_op jit(solution)/shard_map/ppermute | solution.py:403
  179.6 22.4 %collective-permute-start.32 = (f32[4,32,256]{2,1,0:T(8,128)}, f32[4,32,256]{2,1,0:T(8,128)S(1)}, u32[]{:S(2)}, u32[]{:S(2)}) collective-permute-start(f32[4,32,256]{2,1,0:T(8,128)} %get-tuple-element.121.refs_4_), channel_id=1, source_target_pairs={{0,16},{1,17},{2,18},{3,19},{4,20},{5,21},{6,22},{7,23},{8,24},{9,... | collective-permute-start | bytes 393224 | tf_op jit(solution)/shard_map/ppermute | solution.py:403
  205.4 7.3 %collective-permute-start.29 = (f32[2,4,32,128]{3,2,1,0:T(8,128)S(1)}, f32[2,4,32,128]{3,2,1,0:T(8,128)S(1)}, u32[]{:S(2)}, u32[]{:S(2)}) collective-permute-start(f32[2,4,32,128]{3,2,1,0:T(8,128)S(1)} %pad_maximum_fusion.1.refs_0_), channel_id=1, source_target_pairs={{0,2},{1,3},{2,0},{3,1},{4,6},{5,7},{6,4},{7,5},{8,10},{9,11},{10,... | collective-permute-start | bytes 393224 | tf_op jit(solution)/shard_map/ppermute | solution.py:403
  214.8 2.3 collective-permute-done.29.refs_2_
  219.7 85.2 %packed_pair_update.1 = f32[128,256,128]{2,1,0:T(8,128)} custom-call(s32[4]{0:T(128)} %xor_xor_fusion.slots_ref, f32[2,4,32,128]{3,2,1,0:T(8,128)} %copy-done.3, f32[2,4,32,128]{3,2,1,0:T(8,128)} %copy-done.11, f32[2,4,32,128]{3,2,1,0:T(8,128)} %copy-done.10, f32[2,4,32,128]{3,2,1,0:T(8,128)} %copy-done.9, f32[4,32,256]{2,1,0:T(8,128)} %get-tuple-element.121.refs_4_, ...), custom_call_target="tpu_custom_call" | custom-call | tf_op jit(solution)/shard_map/packed_pair_update/pallas_call | solution.py:773
  (135 shorter events, 35.7 us)
Async XLA Ops:
  15.4 11.0 %collective-permute-start.1 = (f32[128,256]{1,0:T(8,128)}, f32[128,256]{1,0:T(8,128)S(1)}, u32[]{:S(2)}, u32[]{:S(2)}) collective-permute-start(f32[128,256]{1,0:T(8,128)} %get-tuple-element.65), channel_id=1, source_target_pairs={{0,1},{1,0},{2,3},{3,2},{4,5},{5,4},{6,7},{7,6},{8,9},{9,8},{10,11... | collective-permute-start | bytes 393224 | tf_op jit(solution)/shard_map/ppermute | solution.py:403
  17.9 18.5 %collective-permute-start.2 = (f32[128,256]{1,0:T(8,128)}, f32[128,256]{1,0:T(8,128)S(1)}, u32[]{:S(2)}, u32[]{:S(2)}) collective-permute-start(f32[128,256]{1,0:T(8,128)} %get-tuple-element.66), channel_id=1, source_target_pairs={{0,5},{1,4},{2,7},{3,6},{4,1},{5,0},{6,3},{7,2},{8,13},{9,12},{10,... | collective-permute-start | bytes 393224 | tf_op jit(solution)/shard_map/ppermute | solution.py:403
  18.0 18.5 %collective-permute-start.3 = (f32[128,256]{1,0:T(8,128)}, f32[128,256]{1,0:T(8,128)S(1)}, u32[]{:S(2)}, u32[]{:S(2)}) collective-permute-start(f32[128,256]{1,0:T(8,128)} %get-tuple-element.67), channel_id=1, source_target_pairs={{0,2},{1,3},{2,0},{3,1},{4,6},{5,7},{6,4},{7,5},{8,10},{9,11},{10,... | collective-permute-start | bytes 393224 | tf_op jit(solution)/shard_map/ppermute | solution.py:403
  19.7 16.7 %collective-permute-start.4 = (f32[128,256]{1,0:T(8,128)}, f32[128,256]{1,0:T(8,128)S(1)}, u32[]{:S(2)}, u32[]{:S(2)}) collective-permute-start(f32[128,256]{1,0:T(8,128)} %get-tuple-element.68), channel_id=1, source_target_pairs={{0,6},{1,7},{2,4},{3,5},{4,2},{5,3},{6,0},{7,1},{8,14},{9,15},{10,... | collective-permute-start | bytes 393224 | tf_op jit(solution)/shard_map/ppermute | solution.py:403
  23.7 12.7 %collective-permute-start.5 = (f32[128,256]{1,0:T(8,128)}, f32[128,256]{1,0:T(8,128)S(1)}, u32[]{:S(2)}, u32[]{:S(2)}) collective-permute-start(f32[128,256]{1,0:T(8,128)} %get-tuple-element.69), channel_id=1, source_target_pairs={{0,3},{1,2},{2,1},{3,0},{4,7},{5,6},{6,5},{7,4},{8,11},{9,10},{10,... | collective-permute-start | bytes 393224 | tf_op jit(solution)/shard_map/ppermute | solution.py:403
  36.8 25.4 %collective-permute-start.7 = (f32[2,4,128,256]{3,2,1,0:T(8,128)S(1)}, f32[2,4,128,256]{3,2,1,0:T(8,128)S(1)}, u32[]{:S(2)}, u32[]{:S(2)}) collective-permute-start(f32[2,4,128,256]{3,2,1,0:T(8,128)S(1)} %pad_maximum_fusion.refs_0_), channel_id=1, source_target_pairs={{0,8},{1,9},{2,10},{3,11},{4,12},{5,13},{6,14},{7,15},{8,0},{9,1},... | collective-permute-start | bytes 3145736 | tf_op jit(solution)/shard_map/ppermute | solution.py:403
  38.5 24.5 %collective-permute-start.8 = (f32[2,4,128,256]{3,2,1,0:T(8,128)S(1)}, f32[2,4,128,256]{3,2,1,0:T(8,128)}, u32[]{:S(2)}, u32[]{:S(2)}) collective-permute-start(f32[2,4,128,256]{3,2,1,0:T(8,128)S(1)} %pad_maximum_fusion.refs_0_), channel_id=1, source_target_pairs={{8,16},{9,17},{10,18},{11,19},{12,20},{13,21},{14,22},{15,23},{16,... | collective-permute-start | bytes 3145736 | tf_op jit(solution)/shard_map/ppermute | solution.py:403
  63.0 65.3 %collective-permute-start.18 = (f32[2,4,128,256]{3,2,1,0:T(8,128)}, f32[2,4,128,256]{3,2,1,0:T(8,128)}, u32[]{:S(2)}, u32[]{:S(2)}) collective-permute-start(f32[2,4,128,256]{3,2,1,0:T(8,128)} %collective-permute-done.8.refs_0_), channel_id=1, source_target_pairs={{8,0},{9,1},{10,2},{11,3},{12,4},{13,5},{14,6},{15,7},{16,24},{17,... | collective-permute-start | bytes 3145736 | tf_op jit(solution)/shard_map/ppermute | solution.py:403
  64.3 72.3 %collective-permute-start.17 = (f32[2,4,128,256]{3,2,1,0:T(8,128)S(1)}, f32[2,4,128,256]{3,2,1,0:T(8,128)}, u32[]{:S(2)}, u32[]{:S(2)}) collective-permute-start(f32[2,4,128,256]{3,2,1,0:T(8,128)S(1)} %collective-permute-done.16.refs_0_), channel_id=1, source_target_pairs={{8,0},{9,1},{10,2},{11,3},{12,4},{13,5},{14,6},{15,7},{16,24},{17,... | collective-permute-start | bytes 3145736 | tf_op jit(solution)/shard_map/ppermute | solution.py:403
  65.8 12.2 %collective-permute-start.10 = (f32[3,4,32,256]{3,2,1,0:T(8,128)S(1)}, f32[3,4,32,256]{3,2,1,0:T(8,128)}, u32[]{:S(2)}, u32[]{:S(2)}) collective-permute-start(f32[3,4,32,256]{3,2,1,0:T(8,128)S(1)} %copy-done.28), channel_id=1, source_target_pairs={{0,1},{1,0},{2,3},{3,2},{4,5},{5,4},{6,7},{7,6},{8,9},{9,8},{10,11... | collective-permute-start | bytes 1179656 | tf_op jit(solution)/shard_map/ppermute | solution.py:403
  67.6 17.9 %collective-permute-start.11 = (f32[3,4,32,256]{3,2,1,0:T(8,128)S(1)}, f32[3,4,32,256]{3,2,1,0:T(8,128)}, u32[]{:S(2)}, u32[]{:S(2)}) collective-permute-start(f32[3,4,32,256]{3,2,1,0:T(8,128)S(1)} %copy-done.27), channel_id=1, source_target_pairs={{0,5},{1,4},{2,7},{3,6},{4,1},{5,0},{6,3},{7,2},{8,13},{9,12},{10,... | collective-permute-start | bytes 1179656 | tf_op jit(solution)/shard_map/ppermute | solution.py:403
  67.7 20.3 %collective-permute-start.12 = (f32[3,4,32,256]{3,2,1,0:T(8,128)S(1)}, f32[3,4,32,256]{3,2,1,0:T(8,128)}, u32[]{:S(2)}, u32[]{:S(2)}) collective-permute-start(f32[3,4,32,256]{3,2,1,0:T(8,128)S(1)} %copy-done.26), channel_id=1, source_target_pairs={{0,2},{1,3},{2,0},{3,1},{4,6},{5,7},{6,4},{7,5},{8,10},{9,11},{10,... | collective-permute-start | bytes 1179656 | tf_op jit(solution)/shard_map/ppermute | solution.py:403
  78.0 12.3 %collective-permute-start.13 = (f32[3,4,32,256]{3,2,1,0:T(8,128)}, f32[3,4,32,256]{3,2,1,0:T(8,128)}, u32[]{:S(2)}, u32[]{:S(2)}) collective-permute-start(f32[3,4,32,256]{3,2,1,0:T(8,128)} %get-tuple-element.95), channel_id=1, source_target_pairs={{0,6},{1,7},{2,4},{3,5},{4,2},{5,3},{6,0},{7,1},{8,14},{9,15},{10,... | collective-permute-start | bytes 1179656 | tf_op jit(solution)/shard_map/ppermute | solution.py:403
  85.4 13.2 %collective-permute-start.14 = (f32[3,4,32,256]{3,2,1,0:T(8,128)}, f32[3,4,32,256]{3,2,1,0:T(8,128)}, u32[]{:S(2)}, u32[]{:S(2)}) collective-permute-start(f32[3,4,32,256]{3,2,1,0:T(8,128)} %get-tuple-element.96), channel_id=1, source_target_pairs={{0,3},{1,2},{2,1},{3,0},{4,7},{5,6},{6,5},{7,4},{8,11},{9,10},{10,... | collective-permute-start | bytes 1179656 | tf_op jit(solution)/shard_map/ppermute | solution.py:403
  88.1 18.3 %collective-permute-start.15 = (f32[3,4,32,256]{3,2,1,0:T(8,128)}, f32[3,4,32,256]{3,2,1,0:T(8,128)}, u32[]{:S(2)}, u32[]{:S(2)}) collective-permute-start(f32[3,4,32,256]{3,2,1,0:T(8,128)} %get-tuple-element.97), channel_id=1, source_target_pairs={{0,7},{1,6},{2,5},{3,4},{4,3},{5,2},{6,1},{7,0},{8,15},{9,14},{10,... | collective-permute-start | bytes 1179656 | tf_op jit(solution)/shard_map/ppermute | solution.py:403
  148.9 12.4 %collective-permute-start.23 = (f32[4,32,256]{2,1,0:T(8,128)}, f32[4,32,256]{2,1,0:T(8,128)S(1)}, u32[]{:S(2)}, u32[]{:S(2)}) collective-permute-start(f32[4,32,256]{2,1,0:T(8,128)} %get-tuple-element.115), channel_id=1, source_target_pairs={{0,6},{1,7},{2,4},{3,5},{4,2},{5,3},{6,0},{7,1},{8,14},{9,15},{10,... | collective-permute-start | bytes 393224 | tf_op jit(solution)/shard_map/ppermute | solution.py:403
  149.1 12.2 %collective-permute-start.24 = (f32[4,32,256]{2,1,0:T(8,128)}, f32[4,32,256]{2,1,0:T(8,128)S(1)}, u32[]{:S(2)}, u32[]{:S(2)}) collective-permute-start(f32[4,32,256]{2,1,0:T(8,128)} %get-tuple-element.116), channel_id=1, source_target_pairs={{0,3},{1,2},{2,1},{3,0},{4,7},{5,6},{6,5},{7,4},{8,11},{9,10},{10,... | collective-permute-start | bytes 393224 | tf_op jit(solution)/shard_map/ppermute | solution.py:403
  167.9 34.0 %collective-permute-start.26 = (f32[4,32,128]{2,1,0:T(8,128)}, f32[4,32,128]{2,1,0:T(8,128)S(1)}, u32[]{:S(2)}, u32[]{:S(2)}) collective-permute-start(f32[4,32,128]{2,1,0:T(8,128)} %get-tuple-element.119), channel_id=1, source_target_pairs={{0,0},{1,8},{2,16},{3,24},{4,4},{5,12},{6,20},{7,28},{8,1},{9,9},{... | collective-permute-start | bytes 196616 | tf_op jit(solution)/shard_map/ppermute | solution.py:403
  169.4 34.4 %collective-permute-start.27 = (f32[4,32,128]{2,1,0:T(8,128)}, f32[4,32,128]{2,1,0:T(8,128)S(1)}, u32[]{:S(2)}, u32[]{:S(2)}) collective-permute-start(f32[4,32,128]{2,1,0:T(8,128)} %get-tuple-element.120), channel_id=1, source_target_pairs={{0,4},{1,12},{2,20},{3,28},{4,0},{5,8},{6,16},{7,24},{8,5},{9,13},... | collective-permute-start | bytes 196616 | tf_op jit(solution)/shard_map/ppermute | solution.py:403
  169.8 35.6 %collective-permute-start.34 = (f32[4,32,256]{2,1,0:T(8,128)}, f32[4,32,256]{2,1,0:T(8,128)S(1)}, u32[]{:S(2)}, u32[]{:S(2)}) collective-permute-start(f32[4,32,256]{2,1,0:T(8,128)} %get-tuple-element.121.refs_4_), channel_id=1, source_target_pairs={{0,4},{1,5},{2,6},{3,7},{4,0},{5,1},{6,2},{7,3},{8,12},{9,13},{10,... | collective-permute-start | bytes 393224 | tf_op jit(solution)/shard_map/ppermute | solution.py:403
  170.0 42.7 %collective-permute-start.33 = (f32[4,32,256]{2,1,0:T(8,128)}, f32[4,32,256]{2,1,0:T(8,128)S(1)}, u32[]{:S(2)}, u32[]{:S(2)}) collective-permute-start(f32[4,32,256]{2,1,0:T(8,128)} %get-tuple-element.121.refs_4_), channel_id=1, source_target_pairs={{0,24},{1,25},{2,26},{3,27},{4,28},{5,29},{6,30},{7,31},{8,16},{9,... | collective-permute-start | bytes 393224 | tf_op jit(solution)/shard_map/ppermute | solution.py:403
  179.6 34.5 %collective-permute-start.32 = (f32[4,32,256]{2,1,0:T(8,128)}, f32[4,32,256]{2,1,0:T(8,128)S(1)}, u32[]{:S(2)}, u32[]{:S(2)}) collective-permute-start(f32[4,32,256]{2,1,0:T(8,128)} %get-tuple-element.121.refs_4_), channel_id=1, source_target_pairs={{0,16},{1,17},{2,18},{3,19},{4,20},{5,21},{6,22},{7,23},{8,24},{9,... | collective-permute-start | bytes 393224 | tf_op jit(solution)/shard_map/ppermute | solution.py:403
  202.0 12.2 %collective-permute-start.31 = (f32[4,32,256]{2,1,0:T(8,128)}, f32[4,32,256]{2,1,0:T(8,128)S(1)}, u32[]{:S(2)}, u32[]{:S(2)}) collective-permute-start(f32[4,32,256]{2,1,0:T(8,128)} %get-tuple-element.121.refs_4_), channel_id=1, source_target_pairs={{0,8},{1,9},{2,10},{3,11},{4,12},{5,13},{6,14},{7,15},{8,0},{9,1},... | collective-permute-start | bytes 393224 | tf_op jit(solution)/shard_map/ppermute | solution.py:403
  205.4 11.7 %collective-permute-start.29 = (f32[2,4,32,128]{3,2,1,0:T(8,128)S(1)}, f32[2,4,32,128]{3,2,1,0:T(8,128)S(1)}, u32[]{:S(2)}, u32[]{:S(2)}) collective-permute-start(f32[2,4,32,128]{3,2,1,0:T(8,128)S(1)} %pad_maximum_fusion.1.refs_0_), channel_id=1, source_target_pairs={{0,2},{1,3},{2,0},{3,1},{4,6},{5,7},{6,4},{7,5},{8,10},{9,11},{10,... | collective-permute-start | bytes 393224 | tf_op jit(solution)/shard_map/ppermute | solution.py:403
  (44 other events, 600.7 us)

commit v9 on v7

--- a/solution.py
+++ b/solution.py
@@ -686,18 +686,19 @@
 
 
 def packed_pair_kernel(step_rows, group, lefts, slots_ref, *refs):
-    left_refs, (own_ref, sib_ref, w_ref, pair_ref, ob_ref, up_ref, eb_ref, dn_ref) = refs[:lefts], refs[lefts:lefts + 8]
-    out_ref, r_hi, r_lo, w_st, up_st, dn_st, left, right = refs[lefts + 8:]
+    left_refs, refs = refs[:lefts], refs[lefts:]
     cores, seqs, hid, rows = left_refs[0].shape
+    right_refs, refs = refs[:lefts * cores], refs[lefts * cores:]
+    w_ref, pair_ref, ob_ref, up_ref, eb_ref, dn_ref = refs[:6]
+    out_ref, r_hi, r_lo, w_st, up_st, dn_st, left, right = refs[6:]
     total = lefts * cores * seqs
 
     @pl.when(pl.program_id(0) == 0)
     def _():
         pair_weights(w_ref, up_ref, dn_ref, w_st, up_st, dn_st)
-        for i in range(own_ref.shape[0]):
-            at = slots_ref[i] * cores
-            for t, ref in enumerate((own_ref, sib_ref)):
-                right[pl.ds((at + t) * seqs, seqs)] = ref[i]
+        for i, ref in enumerate(right_refs):
+            core, plane = divmod(i, lefts)
+            right[pl.ds((slots_ref[plane] * cores + core) * seqs, seqs)] = ref[...]
         r_hi[...], r_lo[...] = split(jnp.concatenate([right[:, d, :] for d in range(hid)], axis=0).T)
         for p, ref in enumerate(left_refs):
             for t in range(cores):
@@ -711,7 +712,7 @@
     )
 
 
-def packed_pair_update(slots, lefts, own, sib, w2, pair, ob, up, eb, dn, step_rows=8, group=4):
+def packed_pair_update(slots, lefts, rights, w2, pair, ob, up, eb, dn, step_rows=8, group=4):
     rows, cols, cz = pair.shape
     cores, seqs, hid, _ = lefts[0].shape
     total = len(lefts) * cores * seqs
@@ -724,7 +725,7 @@
         grid_spec=pltpu.PrefetchScalarGridSpec(
             num_scalar_prefetch=1,
             grid=(rows // step_rows,),
-            in_specs=[whole(a) for a in (*lefts, own, sib, w2)] + [tile] + [whole(a) for a in (ob, up, eb, dn)],
+            in_specs=[whole(a) for a in (*lefts, *rights, w2)] + [tile] + [whole(a) for a in (ob, up, eb, dn)],
             out_specs=tile,
             scratch_shapes=[
                 pltpu.VMEM((cols, hid * total), BF16),
@@ -738,7 +739,7 @@
         ),
         compiler_params=PARAMS,
         name="packed_pair_update",
-    )(slots, *lefts, own, sib, w2, pair, ob, up, eb, dn)
+    )(slots, *lefts, *rights, w2, pair, ob, up, eb, dn)
 
 
 def after(x, *deps):
@@ -798,17 +799,15 @@
         ids, pieces, gate, homolog_embedding, mixing_projector, mixing_offset,
         first_factor_projector.T, second_factor_projector.T,
     )
-    turn = lambda z0, c0, n0: (n0, c0, z0)
-    left_b, left_a = send(left_b, parts, turn), send(left_a, parts, turn)
-    sibling = lambda z0, c0, n0: (z0, c0 ^ 1, n0)
-    left_b = send(left_b, parts, sibling)
+    left_b = send(left_b, parts, lambda z0, c0, n0: (n0, c0 ^ 1, z0))
+    left_a = send(left_a, parts, lambda z0, c0, n0: (n0, c0, z0))
     left = jnp.stack([left_a, left_b])
     rights = [right] + [send(right, parts, lambda z0, c0, n0, d=d: (z0 ^ d, c0, n0)) for d in range(1, PLANES)]
     lefts = [left] + [send(left, parts, lambda z0, c0, n0, d=d: (z0, c0, n0 ^ d)) for d in range(1, parts)]
-    own = jnp.stack(rights)
+    rights += [send(a, parts, lambda z0, c0, n0: (z0, c0 ^ 1, n0)) for a in rights]
+    w2 = outer_product_weight.reshape(hid, hid * cz)
     pair_state_next = packed_pair_update(
-        slots, lefts, own, send(own, parts, sibling),
-        outer_product_weight.reshape(hid, hid * cz), pair_state,
+        slots, lefts, rights, w2, pair_state,
         outer_product_bias, up_weight, expand_bias, down_weight,
     )
     return (alignment_state_next, pair_state_next)

time: 317 us -> 306 us (0.965)
  waiting for transfers between devices: 77.3 us -> 66 us
    ppermute x36 -> x38, waiting for transfers between devices: 77.3 us -> 66 us  [send(): return lax.ppermute(x, AXES, pairs)]
    ppermute x36 -> x38, starting transfers between devices: 74.4 us -> 75.9 us  [send(): return lax.ppermute(x, AXES, pairs)]
  transfers between devices with their start and end apart: 36 -> 38, of which waited for: 16 -> 13; matrix products, arithmetic and copies ran while one was open for 2% -> 2% of each run, Pallas kernels for 12% -> 12%
where the time goes in v9:
time: 306 us; the launch traced here: 305 us
  Pallas kernels  150 us (49%)
  starting transfers between devices  75.9 us (25%)
  waiting for transfers between devices  66 us (22%)
  local copies, waits for them, and re-layouts  6.68 us (2%)
  between operations  4.26 us (1%)
    pallas_call x1, Pallas kernels, packed_pair_update(): pl.pallas_call(functools.partial(packed_pair_kernel, step_rows, group, le...  85.2 us
    ppermute x38, starting transfers between devices, send(): return lax.ppermute(x, AXES, pairs)  75.9 us
    ppermute x38, waiting for transfers between devices, send(): return lax.ppermute(x, AXES, pairs)  66 us
    pallas_call x4, Pallas kernels, head_attention(): pl.pallas_call(functools.partial(head_attention_kernel, hw, turn, len(til...  31.9 us
    pallas_call x1, Pallas kernels, head_bias(): pl.pallas_call(functools.partial(head_bias_kernel, group), out_shape=(jax...  13.6 us
    pallas_call x1, Pallas kernels, head_project(): pl.pallas_call(functools.partial(head_project_kernel, heads, 1.0 / math.s...  7.15 us
  transfers between devices with their start and end apart: 38, of which 13 were waited for; matrix products, arithmetic and copies ran while one was open for 2% of the time, Pallas kernels for 12%

profile of v9, /device:TPU:0, one launch (start us, length us, event | category | flops | bytes accessed | tf_op | source)
XLA Modules:
  0.0 305.2 jit_solution(8833532156993506233)
XLA Ops:
  1.2 13.6 %head_bias.1 = (f32[128,256]{1,0:T(8,128)}, f32[128,256]{1,0:T(8,128)}, f32[128,256]{1,0:T(8,128)}, f32[128,256]{1,0:T(8,128)}, f32[128,256]{1,0:T(8,128)}, /*in...) custom-call(s32[2]{0:T(128)} %pad_add_fusion.ids_ref, f32[128,256,128]{2,1,0:T(8,128)} %refs_13_.1, ...), custom_call_target="tpu_custom_call" | custom-call | tf_op jit(solution)/shard_map/head_bias/pallas_call | solution.py:453
  15.4 2.6 collective-permute-start.1
  23.7 2.7 collective-permute-start.5
  29.3 7.1 %head_project.1 = (f32[3,4,32,256]{3,2,1,0:T(8,128)}, f32[3,4,32,256]{3,2,1,0:T(8,128)}, f32[3,4,32,256]{3,2,1,0:T(8,128)}, f32[3,4,32,256]{3,2,1,0:T(8,128)}, f...) custom-call(s32[2]{0:T(128)} %pad_add_fusion.ids_ref, ...), custom_call_target="tpu_custom_call" | custom-call | tf_op jit(solution)/shard_map/head_project/pallas_call | solution.py:500
  40.2 22.0 %collective-permute-done.7.refs_0_ = f32[2,4,128,256]{3,2,1,0:T(8,128)S(1)} collective-permute-done((f32[2,4,128,256]{3,2,1,0:T(8,128)S(1)}, f32[2,4,128,256]{3,2,1,0:T(8,128)S(1)}, u32[]{:S(2)}, u32[]{:S(2)}) %collective-permute-start.7) | collective-permute-done | bytes 1048608 | tf_op jit(solution)/shard_map/ppermute | solution.py:403
  69.5 8.4 %collective-permute-done.10.refs_2_ = f32[3,4,32,256]{3,2,1,0:T(8,128)S(1)} collective-permute-done((f32[3,4,32,256]{3,2,1,0:T(8,128)S(1)}, f32[3,4,32,256]{3,2,1,0:T(8,128)S(1)}, u32[]{:S(2)}, u32[]{:S(2)}) %collective-permute-start.10) | collective-permute-done | bytes 393248 | tf_op jit(solution)/shard_map/ppermute | solution.py:403
  78.5 7.0 %collective-permute-done.11.refs_3_ = f32[3,4,32,256]{3,2,1,0:T(8,128)} collective-permute-done((f32[3,4,32,256]{3,2,1,0:T(8,128)S(1)}, f32[3,4,32,256]{3,2,1,0:T(8,128)}, u32[]{:S(2)}, u32[]{:S(2)}) %collective-permute-start.11) | collective-permute-done | bytes 393248 | tf_op jit(solution)/shard_map/ppermute | solution.py:403
  85.5 2.6 collective-permute-start.14
  89.2 9.3 %collective-permute-done.14.refs_6_ = f32[3,4,32,256]{3,2,1,0:T(8,128)} collective-permute-done((f32[3,4,32,256]{3,2,1,0:T(8,128)S(1)}, f32[3,4,32,256]{3,2,1,0:T(8,128)}, u32[]{:S(2)}, u32[]{:S(2)}) %collective-permute-start.14) | collective-permute-done | bytes 393248 | tf_op jit(solution)/shard_map/ppermute | solution.py:403
  98.5 7.7 %collective-permute-done.15.refs_7_ = f32[3,4,32,256]{3,2,1,0:T(8,128)} collective-permute-done((f32[3,4,32,256]{3,2,1,0:T(8,128)S(1)}, f32[3,4,32,256]{3,2,1,0:T(8,128)}, u32[]{:S(2)}, u32[]{:S(2)}) %collective-permute-start.15) | collective-permute-done | bytes 393248 | tf_op jit(solution)/shard_map/ppermute | solution.py:403
  106.8 5.8 %stage.1 = (bf16[2,4,4,256,128]{4,3,2,1,0:T(8,128)(2,1)}, bf16[2,4,128,1024]{3,2,1,0:T(8,128)(2,1)}, bf16[2,4,1024,128]{3,2,1,0:T(8,128)(2,1)}) custom-call(s32[1]{0:T(128)S(6)} %add.13.n_ref, f32[3,4,32,256]{3,2,1,0:T(8,128)} %get-tuple-element.90.refs_0_, f32[3,4,32,256]{3,2,1,0:T(8,128)} %copy-done.5, f32[3,4,32,256]{3,2,1,0:T(8,128)} %copy-done.6, ...), custom_call_target="tpu_custom_call" | custom-call | tf_op jit(solution)/shard_map/stage/pallas_call | solution.py:547
  112.6 7.7 %head_attention.4.refs_1_ = f32[4,2,4,32,256]{4,3,2,1,0:T(8,128)} custom-call(s32[12]{0:T(128)} %reshape.32.at_ref, bf16[2,4,4,256,128]{4,3,2,1,0:T(8,128)(2,1)} %get-tuple-element.98.q_ref, bf16[2,4,128,1024]{3,2,1,0:T(8,128)(2,1)} %get-tuple-element.99.k_ref, bf16[2,4,1024,128]{3,2,1,0:T(8,128)(2,1)} %get-tuple-element.100.v_ref, f32[2,4,128,256]{3,2,1,0:T(8,128)} %copy-done), custom_call_target="tpu_custom_call" | custom-call | tf_op jit(solution)/shard_map/head_attention/pallas_call | solution.py:597
  120.4 7.7 %head_attention.5.refs_2_ = f32[4,2,4,32,256]{4,3,2,1,0:T(8,128)} custom-call(s32[12]{0:T(128)} %reshape.32.at_ref, bf16[2,4,4,256,128]{4,3,2,1,0:T(8,128)(2,1)} %get-tuple-element.98.q_ref, bf16[2,4,128,1024]{3,2,1,0:T(8,128)(2,1)} %get-tuple-element.99.k_ref, bf16[2,4,1024,128]{3,2,1,0:T(8,128)(2,1)} %get-tuple-element.100.v_ref, ...), custom_call_target="tpu_custom_call", output_to_operand_aliasing={{}: (5, {})} | custom-call | tf_op jit(solution)/shard_map/head_attention/pallas_call | solution.py:597
  128.1 8.2 %head_attention.6.refs_2_ = f32[4,2,4,32,256]{4,3,2,1,0:T(8,128)} custom-call(s32[12]{0:T(128)} %reshape.32.at_ref, bf16[2,4,4,256,128]{4,3,2,1,0:T(8,128)(2,1)} %get-tuple-element.98.q_ref, bf16[2,4,128,1024]{3,2,1,0:T(8,128)(2,1)} %get-tuple-element.99.k_ref, bf16[2,4,1024,128]{3,2,1,0:T(8,128)(2,1)} %get-tuple-element.100.v_ref, ...), custom_call_target="tpu_custom_call", output_to_operand_aliasing={{}: (6, {})} | custom-call | tf_op jit(solution)/shard_map/head_attention/pallas_call | solution.py:597
  136.3 8.2 %head_attention.7 = f32[4,2,4,32,256]{4,3,2,1,0:T(8,128)} custom-call(s32[12]{0:T(128)} %reshape.32.at_ref, bf16[2,4,4,256,128]{4,3,2,1,0:T(8,128)(2,1)} %get-tuple-element.98.q_ref, bf16[2,4,128,1024]{3,2,1,0:T(8,128)(2,1)} %get-tuple-element.99.k_ref, bf16[2,4,1024,128]{3,2,1,0:T(8,128)(2,1)} %get-tuple-element.100.v_ref, ...), custom_call_target="tpu_custom_call", output_to_operand_aliasing={{}: (6, {})} | custom-call | tf_op jit(solution)/shard_map/head_attention/pallas_call | solution.py:597
  144.6 2.0 slice_bitcast_fusion
  146.6 2.4 collective-permute-start.25
  156.5 2.4 collective-permute-done.23.refs_5_
  158.9 2.8 collective-permute-done.22.refs_4_
  162.7 5.9 %head_merge.1 = (f32[4,256,256]{2,1,0:T(8,128)}, f32[4,32,128]{2,1,0:T(8,128)}, f32[4,32,128]{2,1,0:T(8,128)}, f32[4,32,256]{2,1,0:T(8,128)}) custom-call(s32[2]{0:T(128)} %pad_add_fusion.ids_ref, f32[4,32,256]{2,1,0:T(8,128)} %get-tuple-element.113.refs_0_, f32[4,32,256]{2,1,0:T(8,128)} %copy-done.24, f32[4,32,256]{2,1,0:T(8,128)} %copy-done.23, ...), custom_call_target="tpu_custom_call" | custom-call | tf_op jit(solution)/shard_map/head_merge/pallas_call | solution.py:657
  170.6 9.5 %collective-permute-start.33 = (f32[4,32,256]{2,1,0:T(8,128)}, f32[4,32,256]{2,1,0:T(8,128)S(1)}, u32[]{:S(2)}, u32[]{:S(2)}) collective-permute-start(f32[4,32,256]{2,1,0:T(8,128)} %get-tuple-element.105.refs_4_), channel_id=1, source_target_pairs={{0,24},{1,25},{2,26},{3,27},{4,28},{5,29},{6,30},{7,31},{8,16},{9,... | collective-permute-start | bytes 393224 | tf_op jit(solution)/shard_map/ppermute | solution.py:403
  180.2 22.4 %collective-permute-start.32 = (f32[4,32,256]{2,1,0:T(8,128)}, f32[4,32,256]{2,1,0:T(8,128)S(1)}, u32[]{:S(2)}, u32[]{:S(2)}) collective-permute-start(f32[4,32,256]{2,1,0:T(8,128)} %get-tuple-element.105.refs_4_), channel_id=1, source_target_pairs={{0,16},{1,17},{2,18},{3,19},{4,20},{5,21},{6,22},{7,23},{8,24},{9,... | collective-permute-start | bytes 393224 | tf_op jit(solution)/shard_map/ppermute | solution.py:403
  205.6 7.7 %collective-permute-start.29 = (f32[2,4,32,128]{3,2,1,0:T(8,128)S(1)}, f32[2,4,32,128]{3,2,1,0:T(8,128)S(1)}, u32[]{:S(2)}, u32[]{:S(2)}) collective-permute-start(f32[2,4,32,128]{3,2,1,0:T(8,128)S(1)} %pad_maximum_fusion.1.refs_0_), channel_id=1, source_target_pairs={{0,2},{1,3},{2,0},{3,1},{4,6},{5,7},{6,4},{7,5},{8,10},{9,11},{10,... | collective-permute-start | bytes 393224 | tf_op jit(solution)/shard_map/ppermute | solution.py:403
  220.0 85.2 %packed_pair_update.1 = f32[128,256,128]{2,1,0:T(8,128)} custom-call(s32[4]{0:T(128)} %xor_xor_fusion.slots_ref, f32[2,4,32,128]{3,2,1,0:T(8,128)} %copy-done.3, f32[2,4,32,128]{3,2,1,0:T(8,128)} %copy-done.13, f32[2,4,32,128]{3,2,1,0:T(8,128)} %copy-done.12, f32[2,4,32,128]{3,2,1,0:T(8,128)} %copy-done.11, f32[4,32,256]{2,1,0:T(8,128)} %get-tuple-element.105.refs_4_, ...), custom_call_target="tpu_custom_call" | custom-call | tf_op jit(solution)/shard_map/packed_pair_update/pallas_call | solution.py:722
  (146 shorter events, 39.8 us)
Async XLA Ops:
  15.4 11.0 %collective-permute-start.1 = (f32[128,256]{1,0:T(8,128)}, f32[128,256]{1,0:T(8,128)S(1)}, u32[]{:S(2)}, u32[]{:S(2)}) collective-permute-start(f32[128,256]{1,0:T(8,128)} %get-tuple-element.57), channel_id=1, source_target_pairs={{0,1},{1,0},{2,3},{3,2},{4,5},{5,4},{6,7},{7,6},{8,9},{9,8},{10,11... | collective-permute-start | bytes 393224 | tf_op jit(solution)/shard_map/ppermute | solution.py:403
  18.0 18.5 %collective-permute-start.2 = (f32[128,256]{1,0:T(8,128)}, f32[128,256]{1,0:T(8,128)S(1)}, u32[]{:S(2)}, u32[]{:S(2)}) collective-permute-start(f32[128,256]{1,0:T(8,128)} %get-tuple-element.58), channel_id=1, source_target_pairs={{0,5},{1,4},{2,7},{3,6},{4,1},{5,0},{6,3},{7,2},{8,13},{9,12},{10,... | collective-permute-start | bytes 393224 | tf_op jit(solution)/shard_map/ppermute | solution.py:403
  18.0 18.5 %collective-permute-start.3 = (f32[128,256]{1,0:T(8,128)}, f32[128,256]{1,0:T(8,128)S(1)}, u32[]{:S(2)}, u32[]{:S(2)}) collective-permute-start(f32[128,256]{1,0:T(8,128)} %get-tuple-element.59), channel_id=1, source_target_pairs={{0,2},{1,3},{2,0},{3,1},{4,6},{5,7},{6,4},{7,5},{8,10},{9,11},{10,... | collective-permute-start | bytes 393224 | tf_op jit(solution)/shard_map/ppermute | solution.py:403
  19.8 16.7 %collective-permute-start.4 = (f32[128,256]{1,0:T(8,128)}, f32[128,256]{1,0:T(8,128)S(1)}, u32[]{:S(2)}, u32[]{:S(2)}) collective-permute-start(f32[128,256]{1,0:T(8,128)} %get-tuple-element.60), channel_id=1, source_target_pairs={{0,6},{1,7},{2,4},{3,5},{4,2},{5,3},{6,0},{7,1},{8,14},{9,15},{10,... | collective-permute-start | bytes 393224 | tf_op jit(solution)/shard_map/ppermute | solution.py:403
  23.7 12.8 %collective-permute-start.5 = (f32[128,256]{1,0:T(8,128)}, f32[128,256]{1,0:T(8,128)S(1)}, u32[]{:S(2)}, u32[]{:S(2)}) collective-permute-start(f32[128,256]{1,0:T(8,128)} %get-tuple-element.61), channel_id=1, source_target_pairs={{0,3},{1,2},{2,1},{3,0},{4,7},{5,6},{6,5},{7,4},{8,11},{9,10},{10,... | collective-permute-start | bytes 393224 | tf_op jit(solution)/shard_map/ppermute | solution.py:403
  36.8 25.4 %collective-permute-start.7 = (f32[2,4,128,256]{3,2,1,0:T(8,128)S(1)}, f32[2,4,128,256]{3,2,1,0:T(8,128)S(1)}, u32[]{:S(2)}, u32[]{:S(2)}) collective-permute-start(f32[2,4,128,256]{3,2,1,0:T(8,128)S(1)} %pad_maximum_fusion.refs_0_), channel_id=1, source_target_pairs={{0,8},{1,9},{2,10},{3,11},{4,12},{5,13},{6,14},{7,15},{8,0},{9,1},... | collective-permute-start | bytes 3145736 | tf_op jit(solution)/shard_map/ppermute | solution.py:403
  38.5 24.5 %collective-permute-start.8 = (f32[2,4,128,256]{3,2,1,0:T(8,128)S(1)}, f32[2,4,128,256]{3,2,1,0:T(8,128)}, u32[]{:S(2)}, u32[]{:S(2)}) collective-permute-start(f32[2,4,128,256]{3,2,1,0:T(8,128)S(1)} %pad_maximum_fusion.refs_0_), channel_id=1, source_target_pairs={{8,16},{9,17},{10,18},{11,19},{12,20},{13,21},{14,22},{15,23},{16,... | collective-permute-start | bytes 3145736 | tf_op jit(solution)/shard_map/ppermute | solution.py:403
  63.1 65.1 %collective-permute-start.18 = (f32[2,4,128,256]{3,2,1,0:T(8,128)}, f32[2,4,128,256]{3,2,1,0:T(8,128)}, u32[]{:S(2)}, u32[]{:S(2)}) collective-permute-start(f32[2,4,128,256]{3,2,1,0:T(8,128)} %collective-permute-done.8.refs_0_), channel_id=1, source_target_pairs={{8,0},{9,1},{10,2},{11,3},{12,4},{13,5},{14,6},{15,7},{16,24},{17,... | collective-permute-start | bytes 3145736 | tf_op jit(solution)/shard_map/ppermute | solution.py:403
  64.4 72.0 %collective-permute-start.17 = (f32[2,4,128,256]{3,2,1,0:T(8,128)S(1)}, f32[2,4,128,256]{3,2,1,0:T(8,128)}, u32[]{:S(2)}, u32[]{:S(2)}) collective-permute-start(f32[2,4,128,256]{3,2,1,0:T(8,128)S(1)} %collective-permute-done.16.refs_0_), channel_id=1, source_target_pairs={{8,0},{9,1},{10,2},{11,3},{12,4},{13,5},{14,6},{15,7},{16,24},{17,... | collective-permute-start | bytes 3145736 | tf_op jit(solution)/shard_map/ppermute | solution.py:403
  65.9 12.1 %collective-permute-start.10 = (f32[3,4,32,256]{3,2,1,0:T(8,128)S(1)}, f32[3,4,32,256]{3,2,1,0:T(8,128)S(1)}, u32[]{:S(2)}, u32[]{:S(2)}) collective-permute-start(f32[3,4,32,256]{3,2,1,0:T(8,128)S(1)} %copy-done.33), channel_id=1, source_target_pairs={{0,1},{1,0},{2,3},{3,2},{4,5},{5,4},{6,7},{7,6},{8,9},{9,8},{10,11... | collective-permute-start | bytes 1179656 | tf_op jit(solution)/shard_map/ppermute | solution.py:403
  67.6 17.9 %collective-permute-start.11 = (f32[3,4,32,256]{3,2,1,0:T(8,128)S(1)}, f32[3,4,32,256]{3,2,1,0:T(8,128)}, u32[]{:S(2)}, u32[]{:S(2)}) collective-permute-start(f32[3,4,32,256]{3,2,1,0:T(8,128)S(1)} %copy-done.32), channel_id=1, source_target_pairs={{0,5},{1,4},{2,7},{3,6},{4,1},{5,0},{6,3},{7,2},{8,13},{9,12},{10,... | collective-permute-start | bytes 1179656 | tf_op jit(solution)/shard_map/ppermute | solution.py:403
  67.8 20.3 %collective-permute-start.12 = (f32[3,4,32,256]{3,2,1,0:T(8,128)S(1)}, f32[3,4,32,256]{3,2,1,0:T(8,128)}, u32[]{:S(2)}, u32[]{:S(2)}) collective-permute-start(f32[3,4,32,256]{3,2,1,0:T(8,128)S(1)} %copy-done.31), channel_id=1, source_target_pairs={{0,2},{1,3},{2,0},{3,1},{4,6},{5,7},{6,4},{7,5},{8,10},{9,11},{10,... | collective-permute-start | bytes 1179656 | tf_op jit(solution)/shard_map/ppermute | solution.py:403
  77.9 11.3 %collective-permute-start.13 = (f32[3,4,32,256]{3,2,1,0:T(8,128)S(1)}, f32[3,4,32,256]{3,2,1,0:T(8,128)}, u32[]{:S(2)}, u32[]{:S(2)}) collective-permute-start(f32[3,4,32,256]{3,2,1,0:T(8,128)S(1)} %copy-done.30), channel_id=1, source_target_pairs={{0,6},{1,7},{2,4},{3,5},{4,2},{5,3},{6,0},{7,1},{8,14},{9,15},{10,... | collective-permute-start | bytes 1179656 | tf_op jit(solution)/shard_map/ppermute | solution.py:403
  85.5 13.0 %collective-permute-start.14 = (f32[3,4,32,256]{3,2,1,0:T(8,128)S(1)}, f32[3,4,32,256]{3,2,1,0:T(8,128)}, u32[]{:S(2)}, u32[]{:S(2)}) collective-permute-start(f32[3,4,32,256]{3,2,1,0:T(8,128)S(1)} %copy-done.29), channel_id=1, source_target_pairs={{0,3},{1,2},{2,1},{3,0},{4,7},{5,6},{6,5},{7,4},{8,11},{9,10},{10,... | collective-permute-start | bytes 1179656 | tf_op jit(solution)/shard_map/ppermute | solution.py:403
  88.1 18.1 %collective-permute-start.15 = (f32[3,4,32,256]{3,2,1,0:T(8,128)S(1)}, f32[3,4,32,256]{3,2,1,0:T(8,128)}, u32[]{:S(2)}, u32[]{:S(2)}) collective-permute-start(f32[3,4,32,256]{3,2,1,0:T(8,128)S(1)} %copy-done.28), channel_id=1, source_target_pairs={{0,7},{1,6},{2,5},{3,4},{4,3},{5,2},{6,1},{7,0},{8,15},{9,14},{10,... | collective-permute-start | bytes 1179656 | tf_op jit(solution)/shard_map/ppermute | solution.py:403
  150.7 11.1 %collective-permute-start.22 = (f32[4,32,256]{2,1,0:T(8,128)S(1)}, f32[4,32,256]{2,1,0:T(8,128)S(1)}, u32[]{:S(2)}, u32[]{:S(2)}) collective-permute-start(f32[4,32,256]{2,1,0:T(8,128)S(1)} %get-tuple-element.109), channel_id=1, source_target_pairs={{0,2},{1,3},{2,0},{3,1},{4,6},{5,7},{6,4},{7,5},{8,10},{9,11},{10,... | collective-permute-start | bytes 393224 | tf_op jit(solution)/shard_map/ppermute | solution.py:403
  168.6 34.0 %collective-permute-start.26 = (f32[4,32,128]{2,1,0:T(8,128)}, f32[4,32,128]{2,1,0:T(8,128)S(1)}, u32[]{:S(2)}, u32[]{:S(2)}) collective-permute-start(f32[4,32,128]{2,1,0:T(8,128)} %get-tuple-element.103), channel_id=1, source_target_pairs={{0,0},{1,8},{2,16},{3,24},{4,4},{5,12},{6,20},{7,28},{8,1},{9,9},{... | collective-permute-start | bytes 196616 | tf_op jit(solution)/shard_map/ppermute | solution.py:403
  170.1 33.9 %collective-permute-start.27 = (f32[4,32,128]{2,1,0:T(8,128)}, f32[4,32,128]{2,1,0:T(8,128)S(1)}, u32[]{:S(2)}, u32[]{:S(2)}) collective-permute-start(f32[4,32,128]{2,1,0:T(8,128)} %get-tuple-element.104), channel_id=1, source_target_pairs={{0,4},{1,12},{2,20},{3,28},{4,0},{5,8},{6,16},{7,24},{8,5},{9,13},... | collective-permute-start | bytes 196616 | tf_op jit(solution)/shard_map/ppermute | solution.py:403
  170.1 35.5 %collective-permute-start.34 = (f32[4,32,256]{2,1,0:T(8,128)}, f32[4,32,256]{2,1,0:T(8,128)S(1)}, u32[]{:S(2)}, u32[]{:S(2)}) collective-permute-start(f32[4,32,256]{2,1,0:T(8,128)} %get-tuple-element.105.refs_4_), channel_id=1, source_target_pairs={{0,4},{1,5},{2,6},{3,7},{4,0},{5,1},{6,2},{7,3},{8,12},{9,13},{10,... | collective-permute-start | bytes 393224 | tf_op jit(solution)/shard_map/ppermute | solution.py:403
  170.6 42.6 %collective-permute-start.33 = (f32[4,32,256]{2,1,0:T(8,128)}, f32[4,32,256]{2,1,0:T(8,128)S(1)}, u32[]{:S(2)}, u32[]{:S(2)}) collective-permute-start(f32[4,32,256]{2,1,0:T(8,128)} %get-tuple-element.105.refs_4_), channel_id=1, source_target_pairs={{0,24},{1,25},{2,26},{3,27},{4,28},{5,29},{6,30},{7,31},{8,16},{9,... | collective-permute-start | bytes 393224 | tf_op jit(solution)/shard_map/ppermute | solution.py:403
  180.2 34.6 %collective-permute-start.32 = (f32[4,32,256]{2,1,0:T(8,128)}, f32[4,32,256]{2,1,0:T(8,128)S(1)}, u32[]{:S(2)}, u32[]{:S(2)}) collective-permute-start(f32[4,32,256]{2,1,0:T(8,128)} %get-tuple-element.105.refs_4_), channel_id=1, source_target_pairs={{0,16},{1,17},{2,18},{3,19},{4,20},{5,21},{6,22},{7,23},{8,24},{9,... | collective-permute-start | bytes 393224 | tf_op jit(solution)/shard_map/ppermute | solution.py:403
  202.6 12.2 %collective-permute-start.31 = (f32[4,32,256]{2,1,0:T(8,128)}, f32[4,32,256]{2,1,0:T(8,128)S(1)}, u32[]{:S(2)}, u32[]{:S(2)}) collective-permute-start(f32[4,32,256]{2,1,0:T(8,128)} %get-tuple-element.105.refs_4_), channel_id=1, source_target_pairs={{0,8},{1,9},{2,10},{3,11},{4,12},{5,13},{6,14},{7,15},{8,0},{9,1},... | collective-permute-start | bytes 393224 | tf_op jit(solution)/shard_map/ppermute | solution.py:403
  204.0 11.2 %collective-permute-start.30 = (f32[2,4,32,128]{3,2,1,0:T(8,128)S(1)}, f32[2,4,32,128]{3,2,1,0:T(8,128)S(1)}, u32[]{:S(2)}, u32[]{:S(2)}) collective-permute-start(f32[2,4,32,128]{3,2,1,0:T(8,128)S(1)} %pad_maximum_fusion.1.refs_0_), channel_id=1, source_target_pairs={{0,3},{1,2},{2,1},{3,0},{4,7},{5,6},{6,5},{7,4},{8,11},{9,10},{10,... | collective-permute-start | bytes 393224 | tf_op jit(solution)/shard_map/ppermute | solution.py:403
  205.6 11.7 %collective-permute-start.29 = (f32[2,4,32,128]{3,2,1,0:T(8,128)S(1)}, f32[2,4,32,128]{3,2,1,0:T(8,128)S(1)}, u32[]{:S(2)}, u32[]{:S(2)}) collective-permute-start(f32[2,4,32,128]{3,2,1,0:T(8,128)S(1)} %pad_maximum_fusion.1.refs_0_), channel_id=1, source_target_pairs={{0,2},{1,3},{2,0},{3,1},{4,6},{5,7},{6,4},{7,5},{8,10},{9,11},{10,... | collective-permute-start | bytes 393224 | tf_op jit(solution)/shard_map/ppermute | solution.py:403
  (49 other events, 840.0 us)
